TPU v7x, 32 devices: a whole 2x2x4 slice. The times are simulated.
32 devices in a mesh: view: 8 (over y, x, core), row: 4 (over z).
Axes of the slice: x: 2, y: 2, z: 4, core: 2. Of those that a mesh axis runs over, the one named last changes fastest.
Arguments:
- queries: bfloat16 [8, 16, 64, 2048], P('view', 'row'), may hold values from -60 to 60
- target_keys: bfloat16 [8, 16, 64, 2048], P('view', 'row'), may hold values from -6 to 6
- target_values: bfloat16 [8, 16, 64, 2048], P('view', 'row'), may hold values from -6 to 6
- cond_keys: bfloat16 [512, 2048], P(('view', 'row')), may hold values from -21 to 21
- cond_values: bfloat16 [512, 2048], P(('view', 'row')), may hold values from -6 to 6
Outputs:
- attended: bfloat16 [8, 16, 64, 2048], P('view', 'row')
All inputs are finite; a program needn't handle non-finite values.
Results may differ from a plain program's by a relative error of at most 0.0089.
Values may be sent and summed in bfloat16 or wider, within the bound.
No kernel may reach another device: no remote copies, remote signals or barrier semaphores. Data moves between devices by JAX's collectives and lax.ppermute only.
A program may use at most 64 MiB of HBM per device.

v0:
```python
import functools

import jax
import jax.numpy as jnp
import numpy as np
from jax import lax
from jax.experimental import pallas as pl
from jax.experimental.pallas import tpu as pltpu
from jax.sharding import PartitionSpec as P


HD = 128
RADIUS = 8
BASE = 10000.0
NEG = -1e30
EXP_SCALE = HD ** (-0.5) * float(np.log2(np.e))


def group_layout(head_dim):
    view_width = head_dim // 4
    row_width = 3 * head_dim // 8
    return (
        (0, view_width),
        (view_width, row_width),
        (view_width + row_width, head_dim - view_width - row_width),
    )


def axis_table(group_index, count):
    offset, width = group_layout(HD)[group_index]
    half = width // 2
    frequency = BASE ** (-np.arange(half, dtype=np.float64) / half)
    angles = np.arange(count, dtype=np.float64)[:, None] * frequency
    cosine = np.zeros((count, HD), np.float32)
    sine = np.zeros((count, HD), np.float32)
    for start in (offset, offset + half):
        cosine[:, start : start + half] = np.cos(angles)
        sine[:, start : start + half] = np.sin(angles)
    return np.stack([cosine, sine])


def partner_matrix():
    m = np.zeros((HD, HD), np.float32)
    for offset, width in group_layout(HD):
        half = width // 2
        for i in range(half):
            m[offset + half + i, offset + i] = -1.0
            m[offset + i, offset + half + i] = 1.0
    return m


def window_bias(rows, cols, row_shift):
    row = np.arange(rows * cols) // cols
    col = np.arange(rows * cols) % cols
    row_ok = np.abs(row[None, :] + row_shift - row[:, None]) <= RADIUS
    col_ok = np.abs(col[None, :] - col[:, None]) <= RADIUS
    return np.where(row_ok & col_ok, 0.0, NEG).astype(np.float32).T


def rotated(x, partners, cosine, sine):
    swapped = jnp.dot(x, partners, preferred_element_type=jnp.float32)
    return (x.astype(jnp.float32) * cosine + swapped * sine).astype(jnp.bfloat16)


def cond_kernel(keys_ref, values_ref, table_ref, partners_ref, out_ref):
    for start in range(0, keys_ref.shape[1], HD):
        span = pl.ds(start, HD)
        out_ref[0, :, span] = rotated(
            keys_ref[:, span], partners_ref[...], table_ref[0], table_ref[1]
        )
    out_ref[1] = values_ref[...]


def rotate_kernel(q_ref, k_ref, table_ref, partners_ref, qo_ref, ko_ref):
    for start in range(0, q_ref.shape[1], HD):
        span = pl.ds(start, HD)
        for source, target in ((k_ref, ko_ref), (q_ref, qo_ref)):
            target[:, span] = rotated(
                source[:, span], partners_ref[...], table_ref[0], table_ref[1]
            )


def attend_kernel(stages, first, last, group, *refs):
    refs = list(refs)
    valid_ref, q_ref = refs.pop(0), refs.pop(0)
    if not first:
        acc_in, ml_in = refs.pop(0), refs.pop(0)
    pulled = [[(refs.pop(0), refs.pop(0)) for _ in blocks] for _, blocks in stages]
    biases = [[refs.pop(0) if bias is not None else None for bias in blocks] for _, blocks in stages]
    if last:
        out_ref, acc_ref, ml_ref = refs
    else:
        acc_ref, ml_ref = refs
        ml_ref = ml_ref.at[0]
    if not first:
        acc_ref[...] = acc_in[...]
        ml_ref[...] = ml_in[0]

    def stage(sources, masks, have):
        for head in range(group):
            span = pl.ds(head * HD, HD)
            m_row, l_row = pl.ds(head, 1), pl.ds(group + head, 1)
            q = q_ref[:, span]
            scores = []
            for (k_ref, _), bias_ref in zip(sources, masks):
                s = lax.dot_general(
                    k_ref[:, span], q, (((1,), (1,)), ((), ())),
                    preferred_element_type=jnp.float32,
                )
                scores.append(s if bias_ref is None else s + bias_ref[...])
            top = functools.reduce(
                jnp.maximum, [jnp.max(s, axis=0, keepdims=True) for s in scores]
            )
            if have:
                m_old = ml_ref[m_row, :]
                top = jnp.maximum(top, m_old)
                alpha = jnp.exp2((m_old - top) * EXP_SCALE)
                total = ml_ref[l_row, :] * alpha
                summed = acc_ref[span, :] * alpha
            else:
                total = summed = 0.0
            for s, (_, v_ref) in zip(scores, sources):
                p = jnp.exp2((s - top) * EXP_SCALE)
                total = total + jnp.sum(p, axis=0, keepdims=True)
                summed = summed + lax.dot_general(
                    v_ref[:, span], p.astype(jnp.bfloat16), (((0,), (0,)), ((), ())),
                    preferred_element_type=jnp.float32,
                )
            ml_ref[m_row, :] = top
            ml_ref[l_row, :] = total
            acc_ref[span, :] = summed

    have = not first
    for (flag, _), sources, masks in zip(stages, pulled, biases):
        step = functools.partial(stage, sources, masks, have)
        if flag is None:
            step()
        else:
            pl.when(valid_ref[flag] != 0)(step)
        have = True
    if last:
        for head in range(group):
            span = pl.ds(head * HD, HD)
            scaled = acc_ref[span, :] * (1.0 / ml_ref[pl.ds(group + head, 1), :])
            out_ref[:, span] = scaled.astype(out_ref.dtype).T


def attend(valid, q, state, sources, stages, last, group):
    tokens, width = q.shape
    steps = width // HD // group
    lane_block = pl.BlockSpec((tokens, group * HD), lambda g, _: (0, g))
    acc_block = pl.BlockSpec((group * HD, tokens), lambda g, _: (g, 0))
    ml_block = pl.BlockSpec((1, 2 * group, tokens), lambda g, _: (g, 0, 0))
    operands = [q]
    specs = [lane_block]
    if state is not None:
        operands += list(state)
        specs += [acc_block, ml_block]
    keys_seen = 0
    for source in sources:
        for index, array in enumerate(source):
            if array.ndim == 3:
                specs.append(
                    pl.BlockSpec(
                        (None, array.shape[1], group * HD), lambda g, _, i=index: (i, 0, g)
                    )
                )
            else:
                specs.append(pl.BlockSpec((array.shape[0], group * HD), lambda g, _: (0, g)))
            operands.append(array)
        keys_seen += source[0].shape[-2]
    for _, blocks in stages:
        for bias in blocks:
            if bias is not None:
                operands.append(jnp.asarray(bias))
                specs.append(pl.BlockSpec(bias.shape, lambda g, _: (0, 0)))
    if last:
        out_shape = jax.ShapeDtypeStruct((tokens, width), jnp.bfloat16)
        out_specs = lane_block
        scratch = [
            pltpu.VMEM((group * HD, tokens), jnp.float32),
            pltpu.VMEM((2 * group, tokens), jnp.float32),
        ]
    else:
        out_shape = (
            jax.ShapeDtypeStruct((width, tokens), jnp.float32),
            jax.ShapeDtypeStruct((steps, 2 * group, tokens), jnp.float32),
        )
        out_specs = (acc_block, ml_block)
        scratch = []
    return pl.pallas_call(
        functools.partial(attend_kernel, stages, state is None, last, group),
        out_shape=out_shape,
        grid_spec=pltpu.PrefetchScalarGridSpec(
            num_scalar_prefetch=1,
            grid=(steps,),
            in_specs=specs,
            out_specs=out_specs,
            scratch_shapes=scratch,
        ),
        cost_estimate=pl.CostEstimate(
            flops=4 * tokens * keys_seen * width,
            bytes_accessed=(4 * keys_seen + 8 * tokens) * width,
            transcendentals=tokens * keys_seen * width // HD,
        ),
    )(valid, *operands)


def passed_along(x, axis, by):
    length = lax.axis_size(axis)
    pairs = [(i, i + by) for i in range(length) if 0 <= i + by < length]
    return lax.ppermute(x, axis, pairs)


def gathered(piece, axes):
    held = (piece,)
    for axis in axes:
        distance = lax.axis_size(axis) // 2
        while distance:
            whole = jnp.concatenate(held, axis=1) if len(held) > 1 else held[0]
            pairs = [(i, i ^ distance) for i in range(lax.axis_size(axis))]
            held = (whole, lax.ppermute(whole, axis, pairs))
            distance //= 2
    return held


def local(queries, target_keys, target_values, cond_keys, cond_values):
    view_dev, rows_dev, cols, width = queries.shape
    heads = width // HD
    row_count = lax.axis_size("row")
    view_count = lax.axis_size("view")
    tokens = rows_dev * cols
    row_index = lax.axis_index("row")
    view_index = lax.axis_index("view")
    ctok_dev = cond_keys.shape[0]
    ctok = ctok_dev * view_count * row_count
    group = 4 if heads % 4 == 0 else 1

    partners = jnp.asarray(partner_matrix(), jnp.bfloat16)
    view_table = axis_table(0, view_count * view_dev + 1)
    row_table = axis_table(1, max(row_count * rows_dev, -(-ctok // cols)))
    col_table = axis_table(2, cols)

    cond_ids = np.arange(ctok)
    cond_table = view_table[:, :1] + row_table[:, cond_ids // cols] + col_table[:, cond_ids % cols]
    cond_base = (view_index * row_count + row_index) * ctok_dev
    cond_slice = lax.dynamic_slice_in_dim(jnp.asarray(cond_table), cond_base, ctok_dev, axis=1)
    piece = pl.pallas_call(
        cond_kernel, out_shape=jax.ShapeDtypeStruct((2, ctok_dev, width), jnp.bfloat16)
    )(cond_keys, cond_values, cond_slice, partners)
    cond_held = gathered(piece, ("row", "view"))

    view_dev_ids = view_index * view_dev + 1
    tables = lax.dynamic_slice_in_dim(jnp.asarray(view_table), view_dev_ids, view_dev, axis=1)
    rows_here = lax.dynamic_slice_in_dim(
        jnp.asarray(row_table), row_index * rows_dev, rows_dev, axis=1
    )
    place = (rows_here[:, :, None] + jnp.asarray(col_table)[:, None]).reshape(2, tokens, HD)

    reach = -(-RADIUS // rows_dev)
    near = [d for d in range(1, reach)]
    flags = []
    for d in range(1, reach + 1):
        flags += [row_index - d >= 0, row_index + d < row_count]
    valid = jnp.stack(flags).astype(jnp.int32)

    outputs = []
    for v in range(view_dev):
        values = target_values[v].reshape(tokens, width)
        table = tables[:, v : v + 1] + place
        lane_block = pl.BlockSpec((tokens, 4 * HD), lambda g: (0, g))
        rotate = pl.pallas_call(
            rotate_kernel,
            out_shape=(jax.ShapeDtypeStruct((tokens, width), jnp.bfloat16),) * 2,
            grid=(heads // 4,),
            in_specs=[
                lane_block,
                lane_block,
                pl.BlockSpec((2, tokens, HD), lambda g: (0, 0, 0)),
                pl.BlockSpec((HD, HD), lambda g: (0, 0)),
            ],
            out_specs=(lane_block, lane_block),
            cost_estimate=pl.CostEstimate(
                flops=4 * tokens * width * HD,
                bytes_accessed=8 * tokens * width,
                transcendentals=0,
            ),
            name="rotate",
        )
        q_rot, k_rot = rotate(
            queries[v].reshape(tokens, width),
            target_keys[v].reshape(tokens, width),
            table,
            partners,
        )
        from_above, from_below = [values], [values]
        above, below = [], []
        for _ in range(reach):
            from_above.append(passed_along(from_above[-1], "row", 1))
            from_below.append(passed_along(from_below[-1], "row", -1))
        keys_above, keys_below = k_rot, k_rot
        for d in range(1, reach + 1):
            keys_above = passed_along(keys_above, "row", 1)
            keys_below = passed_along(keys_below, "row", -1)
            above.append((keys_above, from_above[d]))
            below.append((keys_below, from_below[d]))

        def stage_of(d, sign):
            bias = window_bias(rows_dev, cols, sign * d * rows_dev)
            return (2 * (d - 1) + (sign > 0), (bias,))

        state = attend(
            valid, q_rot, None, [(k_rot, values)],
            [(None, (window_bias(rows_dev, cols, 0),))], False, group,
        )
        if near:
            state = attend(
                valid, q_rot, state, [s for d in near for s in (above[d - 1], below[d - 1])],
                [s for d in near for s in (stage_of(d, -1), stage_of(d, 1))], False, group,
            )
        state = attend(
            valid, q_rot, state, [(c, c) for c in cond_held],
            [(None, (None,) * len(cond_held))], False, group,
        )
        out = attend(
            valid, q_rot, state, [above[reach - 1], below[reach - 1]],
            [stage_of(reach, -1), stage_of(reach, 1)], True, group,
        )
        outputs.append(out.reshape(rows_dev, cols, width))
    return jnp.stack(outputs) if view_dev > 1 else outputs[0][None]


def solution(mesh):
    return jax.shard_map(
        local,
        mesh=mesh,
        in_specs=(
            P("view", "row", None, None),
            P("view", "row", None, None),
            P("view", "row", None, None),
            P(("view", "row"), None),
            P(("view", "row"), None),
        ),
        out_specs=P("view", "row", None, None),
        check_vma=False,
    )
```

profile of v0, /device:TPU:0, one launch (start us, length us, event | category | flops | bytes accessed | tf_op | source)
XLA Modules:
  0.0 174.0 jit_solution(6982359987379120192)
XLA Ops:
  0.0 1.3 constant_dynamic-slice_fusion.table_ref
  1.3 1.8 %shard_map.147 = bf16[2,16,2048]{2,1,0:T(8,128)(2,1)} custom-call(bf16[16,2048]{1,0:T(8,128)(2,1)} %keys_ref.1, bf16[16,2048]{1,0:T(8,128)(2,1)} %values_ref.1, f32[2,16,128]{2,1,0:T(8,128)} %constant_dynamic-slice_fusion.table_ref, bf16[128,128]{1,0:T(8,128)(2,1)} %constant.44.clone.partners_ref), custom_call_target="tpu_custom_call" | custom-call | tf_op jit(solution)/shard_map/pallas_call | solution.py:248
  3.1 4.1 %collective-permute-start.4 = (bf16[2,16,2048]{2,1,0:T(8,128)(2,1)}, bf16[2,16,2048]{2,1,0:T(8,128)(2,1)S(1)}, u32[]{:S(2)}, u32[]{:S(2)}) collective-permute-start(bf16[2,16,2048]{2,1,0:T(8,128)(2,1)} %shard_map.147), channel_id=1, source_target_pairs={{0,2},{1,3},{2,0},{3,1},{4,6},{5,7},{6,4},{7,5},{8,10},{9,11},{10,... | collective-permute-start | bytes 393224 | tf_op jit(solution)/shard_map/ppermute | solution.py:222
  7.2 6.5 %collective-permute-done.4 = bf16[2,16,2048]{2,1,0:T(8,128)(2,1)S(1)} collective-permute-done((bf16[2,16,2048]{2,1,0:T(8,128)(2,1)}, bf16[2,16,2048]{2,1,0:T(8,128)(2,1)S(1)}, u32[]{:S(2)}, u32[]{:S(2)}) %collective-permute-start.4) | collective-permute-done | bytes 131104 | tf_op jit(solution)/shard_map/ppermute | solution.py:222
  13.7 0.9 pad_maximum_fusion.2
  14.6 0.9 collective-permute-start.5
  15.5 6.6 %collective-permute-done.5 = bf16[2,32,2048]{2,1,0:T(8,128)(2,1)S(1)} collective-permute-done((bf16[2,32,2048]{2,1,0:T(8,128)(2,1)S(1)}, bf16[2,32,2048]{2,1,0:T(8,128)(2,1)S(1)}, u32[]{:S(2)}, u32[]{:S(2)}) %collective-permute-start.5) | collective-permute-done | bytes 262176 | tf_op jit(solution)/shard_map/ppermute | solution.py:222
  22.2 0.9 pad_maximum_fusion.1
  23.1 1.4 collective-permute-start.6
  24.5 0.9 constant_dynamic-update-slice_fusion.4
  25.5 9.9 %collective-permute-done.6 = bf16[2,64,2048]{2,1,0:T(8,128)(2,1)S(1)} collective-permute-done((bf16[2,64,2048]{2,1,0:T(8,128)(2,1)S(1)}, bf16[2,64,2048]{2,1,0:T(8,128)(2,1)S(1)}, u32[]{:S(2)}, u32[]{:S(2)}) %collective-permute-start.6) | collective-permute-done | bytes 524320 | tf_op jit(solution)/shard_map/ppermute | solution.py:222
  35.4 1.9 %pad_maximum_fusion = bf16[2,128,2048]{2,1,0:T(8,128)(2,1)} fusion(bf16[2,64,2048]{2,1,0:T(8,128)(2,1)S(1)} %collective-permute-done.6, bf16[2,32,2048]{2,1,0:T(8,128)(2,1)S(1)} %collective-permute-done.5, bf16[2,16,2048]{2,1,0:T(8,128)(2,1)S(1)} %collective-permute-done.4, bf16[2,16,2048]{2,1,0:T(8,128)(2,1)} %shard_map.147), kind=kLoop, calls=%fused_computation | loop fusion | flops 4194304 | bytes 2097152 | tf_op jit(solution)/shard_map/concatenate | solution.py:220
  37.4 1.4 collective-permute-start.7
  38.7 0.7 dynamic-slice_bitcast_fusion
  39.4 0.7 constant_dynamic-slice_fusion.1
  40.1 0.9 broadcast_add_fusion
  41.0 19.2 %collective-permute-done.7 = bf16[2,128,2048]{2,1,0:T(8,128)(2,1)} collective-permute-done((bf16[2,128,2048]{2,1,0:T(8,128)(2,1)}, bf16[2,128,2048]{2,1,0:T(8,128)(2,1)}, u32[]{:S(2)}, u32[]{:S(2)}) %collective-permute-start.7) | collective-permute-done | bytes 1048608 | tf_op jit(solution)/shard_map/ppermute | solution.py:222
  60.3 1.3 constant_dynamic-update-slice_fusion.refs_4_.refs_5_
  61.6 0.0 copy-start
  61.6 0.1 collective-permute-start.8
  61.7 0.8 bitcast_add_fusion.table_ref
  62.5 4.5 %rotate.1 = (bf16[256,2048]{1,0:T(8,128)(2,1)}, bf16[256,2048]{1,0:T(8,128)(2,1)}) custom-call(bf16[256,2048]{1,0:T(8,128)(2,1)} %bitcast.12, bf16[256,2048]{1,0:T(8,128)(2,1)} %bitcast.13, f32[2,256,128]{2,1,0:T(8,128)} %bitcast_add_fusion.table_ref, bf16[128,128]{1,0:T(8,128)(2,1)} %constant.44.clone.partners_ref), custom_call_target="tpu_custom_call" | custom-call | flops 268435456 | bytes 4194304 | tf_op jit(solution)/shard_map/rotate/pallas_call | solution.py:290
  67.0 1.3 collective-permute-start.2
  68.3 6.7 %collective-permute-start = (bf16[256,2048]{1,0:T(8,128)(2,1)}, bf16[256,2048]{1,0:T(8,128)(2,1)}, u32[]{:S(2)}, u32[]{:S(2)}) collective-permute-start(bf16[256,2048]{1,0:T(8,128)(2,1)} %get-tuple-element.14.refs_2_), channel_id=1, source_target_pairs={{0,1},{1,2},{2,3},{4,5},{5,6},{6,7},{8,9},{9,10},{10,11},{12,13},{... | collective-permute-start | bytes 3145736 | tf_op jit(solution)/shard_map/ppermute | solution.py:212
  74.9 4.5 %collective-permute-start.1 = (bf16[256,2048]{1,0:T(8,128)(2,1)}, bf16[256,2048]{1,0:T(8,128)(2,1)}, u32[]{:S(2)}, u32[]{:S(2)}) collective-permute-start(bf16[256,2048]{1,0:T(8,128)(2,1)} %bitcast.8.refs_3_), channel_id=1, source_target_pairs={{0,1},{1,2},{2,3},{4,5},{5,6},{6,7},{8,9},{9,10},{10,11},{12,13},{... | collective-permute-start | bytes 3145736 | tf_op jit(solution)/shard_map/ppermute | solution.py:212
  79.4 1.3 collective-permute-start.3
  80.7 15.5 %collective-permute-done.2.refs_6_ = bf16[256,2048]{1,0:T(8,128)(2,1)} collective-permute-done((bf16[256,2048]{1,0:T(8,128)(2,1)}, bf16[256,2048]{1,0:T(8,128)(2,1)}, u32[]{:S(2)}, u32[]{:S(2)}) %collective-permute-start.2) | collective-permute-done | bytes 1048608 | tf_op jit(solution)/shard_map/ppermute | solution.py:212
  96.3 1.3 collective-permute-start.11
  97.6 0.2 collective-permute-done.refs_4_
  97.8 6.0 %collective-permute-start.9 = (bf16[256,2048]{1,0:T(8,128)(2,1)}, bf16[256,2048]{1,0:T(8,128)(2,1)}, u32[]{:S(2)}, u32[]{:S(2)}) collective-permute-start(bf16[256,2048]{1,0:T(8,128)(2,1)} %collective-permute-done.refs_4_), channel_id=1, source_target_pairs={{0,1},{1,2},{2,3},{4,5},{5,6},{6,7},{8,9},{9,10},{10,11},{12,13},{... | collective-permute-start | bytes 3145736 | tf_op jit(solution)/shard_map/ppermute | solution.py:212
  103.8 16.4 %collective-permute-done.1.refs_5_ = bf16[256,2048]{1,0:T(8,128)(2,1)} collective-permute-done((bf16[256,2048]{1,0:T(8,128)(2,1)}, bf16[256,2048]{1,0:T(8,128)(2,1)}, u32[]{:S(2)}, u32[]{:S(2)}) %collective-permute-start.1) | collective-permute-done | bytes 1048608 | tf_op jit(solution)/shard_map/ppermute | solution.py:212
  120.2 5.5 %collective-permute-start.10 = (bf16[256,2048]{1,0:T(8,128)(2,1)}, bf16[256,2048]{1,0:T(8,128)(2,1)}, u32[]{:S(2)}, u32[]{:S(2)}) collective-permute-start(bf16[256,2048]{1,0:T(8,128)(2,1)} %collective-permute-done.1.refs_5_), channel_id=1, source_target_pairs={{0,1},{1,2},{2,3},{4,5},{5,6},{6,7},{8,9},{9,10},{10,11},{12,13},{... | collective-permute-start | bytes 3145736 | tf_op jit(solution)/shard_map/ppermute | solution.py:212
  125.8 0.0 collective-permute-done.3.refs_7_
  125.8 1.3 collective-permute-start.12
  127.1 0.7 add_convert_fusion.refs_0_
  127.7 8.1 %shard_map.145 = (f32[2048,256]{1,0:T(8,128)}, f32[4,8,256]{2,1,0:T(8,128)}) custom-call(s32[4]{0:T(128)} %add_convert_fusion.refs_0_, bf16[256,2048]{1,0:T(8,128)(2,1)} %get-tuple-element.13.refs_1_, bf16[256,2048]{1,0:T(8,128)(2,1)} %get-tuple-element.14.refs_2_, bf16[256,2048]{1,0:T(8,128)(2,1)} %bitcast.8.refs_3_, ...), custom_call_target="tpu_custom_call" | custom-call | flops 536870912 | bytes 6291456 | tf_op jit(solution)/shard_map/pallas_call | solution.py:191
  135.9 0.0 copy-done
  135.9 9.3 %shard_map.146 = (f32[2048,256]{1,0:T(8,128)}, f32[4,8,256]{2,1,0:T(8,128)}) custom-call(s32[4]{0:T(128)} %add_convert_fusion.refs_0_, bf16[256,2048]{1,0:T(8,128)(2,1)} %get-tuple-element.13.refs_1_, f32[2048,256]{1,0:T(8,128)} %get-tuple-element.15.refs_2_, f32[4,8,256]{2,1,0:T(8,128)} %get-tuple-element.16.refs_3_, ...), custom_call_target="tpu_custom_call" | custom-call | flops 1073741824 | bytes 8388608 | tf_op jit(solution)/shard_map/pallas_call | solution.py:191
  145.2 0.0 collective-permute-done.8.refs_6_.refs_7_
  145.2 9.6 %shard_map.148 = (f32[2048,256]{1,0:T(8,128)}, f32[4,8,256]{2,1,0:T(8,128)}) custom-call(s32[4]{0:T(128)} %add_convert_fusion.refs_0_, bf16[256,2048]{1,0:T(8,128)(2,1)} %get-tuple-element.13.refs_1_, f32[2048,256]{1,0:T(8,128)} %get-tuple-element.17.refs_2_, f32[4,8,256]{2,1,0:T(8,128)} %get-tuple-element.18.refs_3_, bf16[2,256,2048]{2,1,0:T(8,128)(2,1)} %copy-done, ...), custom_call_target="tpu_custom_call" | custom-call | flops 1073741824 | bytes 8388608 | tf_op jit(solution)/shard_map/pallas_call | solution.py:191
  154.7 0.0 collective-permute-done.11.refs_6_
  154.7 0.0 copy-start.1
  154.8 0.0 collective-permute-done.9.refs_4_
  154.8 9.8 %collective-permute-done.10.refs_5_ = bf16[256,2048]{1,0:T(8,128)(2,1)} collective-permute-done((bf16[256,2048]{1,0:T(8,128)(2,1)}, bf16[256,2048]{1,0:T(8,128)(2,1)}, u32[]{:S(2)}, u32[]{:S(2)}) %collective-permute-start.10) | collective-permute-done | bytes 1048608 | tf_op jit(solution)/shard_map/ppermute | solution.py:212
  164.6 0.0 collective-permute-done.12.refs_7_
  164.6 0.0 copy-done.1
  164.6 9.4 %shard_map.149 = bf16[256,2048]{1,0:T(8,128)(2,1)} custom-call(s32[4]{0:T(128)} %add_convert_fusion.refs_0_, bf16[256,2048]{1,0:T(8,128)(2,1)} %get-tuple-element.13.refs_1_, f32[2048,256]{1,0:T(8,128)} %get-tuple-element.19.refs_2_, f32[4,8,256]{2,1,0:T(8,128)} %get-tuple-element.20.refs_3_, bf16[256,2048]{1,0:T(8,128)(2,1)} %collective-permute-done.9.refs_4_, ...), custom_call_target="tpu_custom_call" | custom-call | flops 1073741824 | bytes 8388608 | tf_op jit(solution)/shard_map/pallas_call | solution.py:191
  (3 shorter events, 0.1 us)
Async XLA Ops:
  3.1 10.6 %collective-permute-start.4 = (bf16[2,16,2048]{2,1,0:T(8,128)(2,1)}, bf16[2,16,2048]{2,1,0:T(8,128)(2,1)S(1)}, u32[]{:S(2)}, u32[]{:S(2)}) collective-permute-start(bf16[2,16,2048]{2,1,0:T(8,128)(2,1)} %shard_map.147), channel_id=1, source_target_pairs={{0,2},{1,3},{2,0},{3,1},{4,6},{5,7},{6,4},{7,5},{8,10},{9,11},{10,... | collective-permute-start | bytes 393224 | tf_op jit(solution)/shard_map/ppermute | solution.py:222
  14.6 7.5 %collective-permute-start.5 = (bf16[2,32,2048]{2,1,0:T(8,128)(2,1)S(1)}, bf16[2,32,2048]{2,1,0:T(8,128)(2,1)S(1)}, u32[]{:S(2)}, u32[]{:S(2)}) collective-permute-start(bf16[2,32,2048]{2,1,0:T(8,128)(2,1)S(1)} %pad_maximum_fusion.2), channel_id=1, source_target_pairs={{0,1},{1,0},{2,3},{3,2},{4,5},{5,4},{6,7},{7,6},{8,9},{9,8},{10,11... | collective-permute-start | bytes 786440 | tf_op jit(solution)/shard_map/ppermute | solution.py:222
  23.1 12.3 %collective-permute-start.6 = (bf16[2,64,2048]{2,1,0:T(8,128)(2,1)S(1)}, bf16[2,64,2048]{2,1,0:T(8,128)(2,1)S(1)}, u32[]{:S(2)}, u32[]{:S(2)}) collective-permute-start(bf16[2,64,2048]{2,1,0:T(8,128)(2,1)S(1)} %pad_maximum_fusion.1), channel_id=1, source_target_pairs={{0,16},{4,20},{8,24},{12,28},{16,0},{20,4},{24,8},{28,12},{1,17},{... | collective-permute-start | bytes 1572872 | tf_op jit(solution)/shard_map/ppermute | solution.py:222
  37.4 22.9 %collective-permute-start.7 = (bf16[2,128,2048]{2,1,0:T(8,128)(2,1)}, bf16[2,128,2048]{2,1,0:T(8,128)(2,1)}, u32[]{:S(2)}, u32[]{:S(2)}) collective-permute-start(bf16[2,128,2048]{2,1,0:T(8,128)(2,1)} %pad_maximum_fusion), channel_id=1, source_target_pairs={{0,8},{4,12},{8,0},{12,4},{16,24},{20,28},{24,16},{28,20},{1,9},{5... | collective-permute-start | bytes 3145736 | tf_op jit(solution)/shard_map/ppermute | solution.py:222
  61.6 74.3 %copy-start = (bf16[2,256,2048]{2,1,0:T(8,128)(2,1)}, bf16[2,256,2048]{2,1,0:T(8,128)(2,1)S(1)}, u32[]{:S(2)}) copy-start(bf16[2,256,2048]{2,1,0:T(8,128)(2,1)S(1)} %constant_dynamic-update-slice_fusion.refs_4_.refs_5_) | copy-start | bytes 6291460
  61.6 83.6 %collective-permute-start.8 = (bf16[2,256,2048]{2,1,0:T(8,128)(2,1)S(1)}, bf16[2,256,2048]{2,1,0:T(8,128)(2,1)}, u32[]{:S(2)}, u32[]{:S(2)}) collective-permute-start(bf16[2,256,2048]{2,1,0:T(8,128)(2,1)S(1)} %constant_dynamic-update-slice_fusion.refs_4_.refs_5_), channel_id=1, source_target_pairs={{0,4},{4,0},{8,12},{12,8},{16,20},{20,16},{24,28},{28,24},{1,5},{5... | collective-permute-start | bytes 6291464 | tf_op jit(solution)/shard_map/ppermute | solution.py:222
  67.0 29.3 %collective-permute-start.2 = (bf16[256,2048]{1,0:T(8,128)(2,1)}, bf16[256,2048]{1,0:T(8,128)(2,1)}, u32[]{:S(2)}, u32[]{:S(2)}) collective-permute-start(bf16[256,2048]{1,0:T(8,128)(2,1)} %get-tuple-element.14.refs_2_), channel_id=1, source_target_pairs={{1,0},{2,1},{3,2},{5,4},{6,5},{7,6},{9,8},{10,9},{11,10},{13,12},{... | collective-permute-start | bytes 3145736 | tf_op jit(solution)/shard_map/ppermute | solution.py:212
  68.3 29.5 %collective-permute-start = (bf16[256,2048]{1,0:T(8,128)(2,1)}, bf16[256,2048]{1,0:T(8,128)(2,1)}, u32[]{:S(2)}, u32[]{:S(2)}) collective-permute-start(bf16[256,2048]{1,0:T(8,128)(2,1)} %get-tuple-element.14.refs_2_), channel_id=1, source_target_pairs={{0,1},{1,2},{2,3},{4,5},{5,6},{6,7},{8,9},{9,10},{10,11},{12,13},{... | collective-permute-start | bytes 3145736 | tf_op jit(solution)/shard_map/ppermute | solution.py:212
  74.9 45.3 %collective-permute-start.1 = (bf16[256,2048]{1,0:T(8,128)(2,1)}, bf16[256,2048]{1,0:T(8,128)(2,1)}, u32[]{:S(2)}, u32[]{:S(2)}) collective-permute-start(bf16[256,2048]{1,0:T(8,128)(2,1)} %bitcast.8.refs_3_), channel_id=1, source_target_pairs={{0,1},{1,2},{2,3},{4,5},{5,6},{6,7},{8,9},{9,10},{10,11},{12,13},{... | collective-permute-start | bytes 3145736 | tf_op jit(solution)/shard_map/ppermute | solution.py:212
  79.4 46.3 %collective-permute-start.3 = (bf16[256,2048]{1,0:T(8,128)(2,1)}, bf16[256,2048]{1,0:T(8,128)(2,1)}, u32[]{:S(2)}, u32[]{:S(2)}) collective-permute-start(bf16[256,2048]{1,0:T(8,128)(2,1)} %bitcast.8.refs_3_), channel_id=1, source_target_pairs={{1,0},{2,1},{3,2},{5,4},{6,5},{7,6},{9,8},{10,9},{11,10},{13,12},{... | collective-permute-start | bytes 3145736 | tf_op jit(solution)/shard_map/ppermute | solution.py:212
  96.3 58.5 %collective-permute-start.11 = (bf16[256,2048]{1,0:T(8,128)(2,1)}, bf16[256,2048]{1,0:T(8,128)(2,1)S(1)}, u32[]{:S(2)}, u32[]{:S(2)}) collective-permute-start(bf16[256,2048]{1,0:T(8,128)(2,1)} %collective-permute-done.2.refs_6_), channel_id=1, source_target_pairs={{1,0},{2,1},{3,2},{5,4},{6,5},{7,6},{9,8},{10,9},{11,10},{13,12},{... | collective-permute-start | bytes 3145736 | tf_op jit(solution)/shard_map/ppermute | solution.py:212
  97.8 57.0 %collective-permute-start.9 = (bf16[256,2048]{1,0:T(8,128)(2,1)}, bf16[256,2048]{1,0:T(8,128)(2,1)}, u32[]{:S(2)}, u32[]{:S(2)}) collective-permute-start(bf16[256,2048]{1,0:T(8,128)(2,1)} %collective-permute-done.refs_4_), channel_id=1, source_target_pairs={{0,1},{1,2},{2,3},{4,5},{5,6},{6,7},{8,9},{9,10},{10,11},{12,13},{... | collective-permute-start | bytes 3145736 | tf_op jit(solution)/shard_map/ppermute | solution.py:212
  120.2 44.4 %collective-permute-start.10 = (bf16[256,2048]{1,0:T(8,128)(2,1)}, bf16[256,2048]{1,0:T(8,128)(2,1)}, u32[]{:S(2)}, u32[]{:S(2)}) collective-permute-start(bf16[256,2048]{1,0:T(8,128)(2,1)} %collective-permute-done.1.refs_5_), channel_id=1, source_target_pairs={{0,1},{1,2},{2,3},{4,5},{5,6},{6,7},{8,9},{9,10},{10,11},{12,13},{... | collective-permute-start | bytes 3145736 | tf_op jit(solution)/shard_map/ppermute | solution.py:212
  125.8 38.8 %collective-permute-start.12 = (bf16[256,2048]{1,0:T(8,128)(2,1)}, bf16[256,2048]{1,0:T(8,128)(2,1)}, u32[]{:S(2)}, u32[]{:S(2)}) collective-permute-start(bf16[256,2048]{1,0:T(8,128)(2,1)} %collective-permute-done.3.refs_7_), channel_id=1, source_target_pairs={{1,0},{2,1},{3,2},{5,4},{6,5},{7,6},{9,8},{10,9},{11,10},{13,12},{... | collective-permute-start | bytes 3145736 | tf_op jit(solution)/shard_map/ppermute | solution.py:212
  154.7 9.8 %copy-start.1 = (bf16[256,2048]{1,0:T(8,128)(2,1)}, bf16[256,2048]{1,0:T(8,128)(2,1)S(1)}, u32[]{:S(2)}) copy-start(bf16[256,2048]{1,0:T(8,128)(2,1)S(1)} %collective-permute-done.11.refs_6_) | copy-start | bytes 3145732
where the time goes:
time: 177 us; the launch traced here: 174 us
  waiting for transfers between devices  84.3 us (48%)
  Pallas kernels  42.7 us (24%)
  starting transfers between devices  35.7 us (20%)
  other arithmetic  6.17 us (3%)
  local copies, waits for them, and re-layouts  4.99 us (3%)
    ppermute x5, waiting for transfers between devices, gathered(): held = (whole, lax.ppermute(whole, axis, pairs))  42.3 us
    ppermute x8, waiting for transfers between devices, passed_along(): return lax.ppermute(x, axis, pairs)  42 us
    pallas_call x4, Pallas kernels, attend(): pl.pallas_call(functools.partial(attend_kernel, stages, state is None, la...  36.4 us
    ppermute x8, starting transfers between devices, passed_along(): return lax.ppermute(x, axis, pairs)  27.9 us
    ppermute x5, starting transfers between devices, gathered(): held = (whole, lax.ppermute(whole, axis, pairs))  7.82 us
    pallas_call x1, Pallas kernels, local(): rotate(queries[v].reshape(tokens, width), target_keys[v].reshape(tokens,...  4.46 us
    concatenate x3, other arithmetic, gathered(): whole = jnp.concatenate(held, axis=1) if len(held) > 1 else held[0]  3.81 us
  transfers between devices with their start and end apart: 13, of which 8 were waited for; matrix products, arithmetic and copies ran while one was open for 3% of the time, Pallas kernels for 18%

commit v1 on v0

v1 whole, which is shorter than its diff:
```python
import functools
from typing import NamedTuple

import jax
import jax.numpy as jnp
import numpy as np
from jax import lax
from jax.experimental import pallas as pl
from jax.experimental.pallas import tpu as pltpu
from jax.sharding import PartitionSpec as P


HD = 128
RADIUS = 8
BASE = 10000.0
NEG = -1e30
KERNEL_VMEM = 16 * 2**20
EXP_SCALE = HD ** (-0.5) * float(np.log2(np.e))


def group_layout(head_dim):
    view_width = head_dim // 4
    row_width = 3 * head_dim // 8
    return (
        (0, view_width),
        (view_width, row_width),
        (view_width + row_width, head_dim - view_width - row_width),
    )


def axis_table(group_index, count):
    offset, width = group_layout(HD)[group_index]
    half = width // 2
    frequency = BASE ** (-np.arange(half, dtype=np.float64) / half)
    angles = np.arange(count, dtype=np.float64)[:, None] * frequency
    cosine = np.zeros((count, HD), np.float32)
    sine = np.zeros((count, HD), np.float32)
    for start in (offset, offset + half):
        cosine[:, start : start + half] = np.cos(angles)
        sine[:, start : start + half] = np.sin(angles)
    return np.stack([cosine, sine])


def partner_matrix():
    m = np.zeros((HD, HD), np.float32)
    for offset, width in group_layout(HD):
        half = width // 2
        for i in range(half):
            m[offset + half + i, offset + i] = -1.0
            m[offset + i, offset + half + i] = 1.0
    return m


def rotated(x, partners, cosine, sine):
    swapped = jnp.dot(x, partners, preferred_element_type=jnp.float32)
    return (x.astype(jnp.float32) * cosine + swapped * sine).astype(jnp.bfloat16)


def cond_kernel(parts, *refs):
    partners_ref, out_ref = refs[3 * parts :]
    for part in range(parts):
        keys_ref, values_ref, table_ref = refs[3 * part : 3 * part + 3]
        count = keys_ref.shape[0]
        here = pl.ds(part * count, count)
        for start in range(0, keys_ref.shape[1], HD):
            span = pl.ds(start, HD)
            out_ref[0, here, span] = rotated(
                keys_ref[:, span], partners_ref[...], table_ref[0], table_ref[1]
            )
        out_ref[1, here] = values_ref[...]


def rotate_kernel(chunks, group, q_ref, k_ref, table_ref, partners_ref, qo_ref, *ko_refs):
    unit = pl.program_id(0)

    def turn(source, start):
        return rotated(
            source[:, pl.ds(start, HD)], partners_ref[...], table_ref[0], table_ref[1]
        )

    for head in range(group):
        qo_ref[:, pl.ds(pl.multiple_of((unit * group + head) * HD, HD), HD)] = turn(
            q_ref, head * HD
        )
    for (first, count), ko_ref in zip(chunks, ko_refs):

        @pl.when((unit * group >= first) & (unit * group < first + count))
        def _(first=first, ko_ref=ko_ref):
            for head in range(group):
                start = pl.multiple_of((unit * group - first + head) * HD, HD)
                ko_ref[:, pl.ds(start, HD)] = turn(k_ref, head * HD)


def mask_tiles(rows, cols, row_shift, lanes):
    tokens = rows * cols
    row = np.arange(tokens) // cols
    col = np.arange(tokens) % cols
    inside = (np.abs(row[:, None] + row_shift - row[None, :]) <= RADIUS) & (
        np.abs(col[:, None] - col[None, :]) <= RADIUS
    )
    tiles, plan = [], []
    for start in range(0, tokens, lanes):
        parts = [inside[r * cols : (r + 1) * cols, start : start + lanes] for r in range(rows)]
        used = [r for r in range(rows) if parts[r].any()]
        names = []
        for r in range(used[0], used[-1] + 1):
            found = [i for i, tile in enumerate(tiles) if (tile == parts[r]).all()]
            if not found:
                tiles.append(parts[r])
            names.append(found[0] if found else len(tiles) - 1)
        plan.append((used[0], used[-1] + 1, tuple(names)))
    return np.where(np.stack(tiles), 0.0, NEG).astype(np.float32), tuple(plan)


def attend_kernel(stages, first, last, group, lanes, *refs):
    refs = list(refs)
    valid_ref, q_ref = refs.pop(0), refs.pop(0)

    def pull(block):
        if block.stacked:
            pair = refs.pop(0)
            return pair.at[0], pair.at[1]
        return refs.pop(0), refs.pop(0)

    pulled = [[pull(b) for b in blocks] for _, blocks in stages]
    masks = [[refs.pop(0) if b.plan else None for b in blocks] for _, blocks in stages]
    if not first:
        acc_in, ml_in = refs.pop(0), refs.pop(0)
    if last is not None:
        if last:
            refs.pop(0)
        out_ref = refs.pop(0)
    acc_ref, ml_ref = refs
    tokens = q_ref.shape[0]
    unit = pl.program_id(0)

    def span_of(head, offset):
        return pl.ds(pl.multiple_of((unit * group + head + offset) * HD, HD), HD)

    def stage(blocks, sources, mask_refs, have):
        def scores(head, start):
            q = q_ref[pl.ds(start, lanes), span_of(head, blocks[0].head)]
            found = []
            for block, (k_ref, _) in zip(blocks, sources):
                low, high = block.rows(start // lanes, k_ref.shape[0])
                k = k_ref[low:high, span_of(head, block.head - block.keys_head)]
                found.append(
                    lax.dot_general(
                        k, q, (((1,), (1,)), ((), ())), preferred_element_type=jnp.float32
                    )
                )
            return found

        def update(head, start, found):
            at = unit * group + head
            here = pl.ds(start, lanes)
            if have:
                top = ml_ref[at, 0:1, here]
                total = ml_ref[at, 1:2, here]
                summed = acc_ref[at, :, here]
            started = have
            for s, block, (k_ref, v_ref), mask_ref in zip(found, blocks, sources, mask_refs):
                low, high = block.rows(start // lanes, k_ref.shape[0])
                if mask_ref is not None:
                    names = block.plan[start // lanes][2]
                    s = s + jnp.concatenate([mask_ref[n] for n in names], axis=0)
                peak = jnp.max(s, axis=0, keepdims=True)
                if started:
                    peak = jnp.maximum(peak, top)
                p = jnp.exp2((s - peak) * EXP_SCALE)
                part = jnp.sum(p, axis=0, keepdims=True)
                v = v_ref[low:high, span_of(head, block.head - block.values_head)]
                pv = lax.dot_general(
                    v, p.astype(jnp.bfloat16), (((0,), (0,)), ((), ())),
                    preferred_element_type=jnp.float32,
                )
                if started:
                    alpha = jnp.exp2((top - peak) * EXP_SCALE)
                    part = part + total * alpha
                    pv = pv + summed * alpha
                top, total, summed, started = peak, part, pv, True
            ml_ref[at, 0:1, here] = top
            ml_ref[at, 1:2, here] = total
            acc_ref[at, :, here] = summed

        work = [(head, start) for head in range(group) for start in range(0, tokens, lanes)]
        ahead = scores(*work[0])
        for index, item in enumerate(work):
            found = ahead
            if index + 1 < len(work):
                ahead = scores(*work[index + 1])
            update(*item, found)

    have = not first
    for (flag, blocks), sources, mask_refs in zip(stages, pulled, masks):
        step = functools.partial(stage, blocks, sources, mask_refs, have)
        if flag is None:
            step()
        else:
            pl.when(valid_ref[flag] != 0)(step)
        have = True
    if last is not None:
        for head in range(group):
            at = unit * group + head
            scaled = acc_ref[at] * (1.0 / ml_ref[at, 1:2, :])
            out_ref[:, pl.ds(head * HD, HD)] = scaled.astype(out_ref.dtype).T


class Block(NamedTuple):
    plan: tuple = ()
    head: int = 0
    keys_head: int = 0
    values_head: int = 0
    cols: int = 0
    stacked: bool = False

    def rows(self, tile, count):
        if not self.plan:
            return 0, count
        return self.plan[tile][0] * self.cols, self.plan[tile][1] * self.cols


def resident(x):
    return pltpu.with_memory_space_constraint(x, pltpu.VMEM)


def attend(valid, q, state, sources, stages, tiles, heads, group, out=None, last=False):
    tokens, width = q.shape
    lanes = 128 if tokens % 128 == 0 else tokens
    first_head = stages[0][1][0].head
    operands = [resident(a) for a in (q, *(a for source in sources for a in source))]
    operands += [resident(jnp.asarray(t)) for t in tiles]
    whole = pl.BlockSpec(memory_space=pltpu.VMEM)
    aliases = {}
    if state is not None:
        aliases = {len(operands) + 1 + i: i + last for i in range(2)}
        operands += [resident(a) for a in state]
    specs = [whole] * len(operands)
    out_shape = [
        pltpu.VMEM((heads, HD, tokens), jnp.float32),
        pltpu.VMEM((heads, 2, tokens), jnp.float32),
    ]
    out_specs = [whole] * 2
    if last:
        out_shape.insert(0, jax.ShapeDtypeStruct((tokens, width), jnp.bfloat16))
        out_specs.insert(
            0, pl.BlockSpec((tokens, group * HD), lambda g, _: (0, first_head // group + g))
        )
        if out is not None:
            aliases[len(operands) + 1] = 0
            operands.append(out)
            specs.append(pl.BlockSpec(memory_space=pl.ANY))
    keys_seen = sum(source[0].shape[-2] for source in sources)
    return pl.pallas_call(
        functools.partial(
            attend_kernel, stages, state is None, (out is not None) if last else None, group, lanes
        ),
        out_shape=out_shape,
        grid_spec=pltpu.PrefetchScalarGridSpec(
            num_scalar_prefetch=1, grid=(heads // group,), in_specs=specs, out_specs=out_specs
        ),
        input_output_aliases=aliases,
        compiler_params=pltpu.CompilerParams(vmem_limit_bytes=KERNEL_VMEM),
        cost_estimate=pl.CostEstimate(
            flops=4 * tokens * keys_seen * heads * HD,
            bytes_accessed=(4 * keys_seen + 8 * tokens) * heads * HD,
            transcendentals=tokens * keys_seen * heads,
        ),
    )(valid, *operands)


def passed_along(x, axis, by):
    length = lax.axis_size(axis)
    pairs = [(i, i + by) for i in range(length) if 0 <= i + by < length]
    return lax.ppermute(x, axis, pairs)


def gathered(piece, steps):
    held = (piece,)
    for axis, distance in steps:
        whole = jnp.concatenate(held, axis=1) if len(held) > 1 else held[0]
        held = (whole, swapped(whole, axis, distance))
    return held


def swapped(x, axis, distance):
    return lax.ppermute(x, axis, [(i, i ^ distance) for i in range(lax.axis_size(axis))])


def swap_steps(mesh_shape):
    steps = []
    for axis in ("row", "view"):
        distance = mesh_shape[axis] // 2
        while distance:
            steps.append((axis, distance))
            distance //= 2
    return steps


def local(queries, target_keys, target_values, cond_keys, cond_values):
    view_dev, rows_dev, cols, width = queries.shape
    heads = width // HD
    row_count = lax.axis_size("row")
    view_count = lax.axis_size("view")
    tokens = rows_dev * cols
    lanes = 128 if tokens % 128 == 0 else tokens
    row_index = lax.axis_index("row")
    view_index = lax.axis_index("view")
    ctok_dev = cond_keys.shape[0]
    ctok = ctok_dev * view_count * row_count
    group = 4 if heads % 4 == 0 else 1
    last_heads = group if heads > group else 0
    chunks = [(0, heads - last_heads)] + [(heads - last_heads, last_heads)] * (last_heads > 0)

    partners = jnp.asarray(partner_matrix(), jnp.bfloat16)
    view_table = axis_table(0, view_count * view_dev + 1)
    row_table = axis_table(1, max(row_count * rows_dev, -(-ctok // cols)))
    col_table = axis_table(2, cols)

    cond_ids = np.arange(ctok)
    cond_table = view_table[:, :1] + row_table[:, cond_ids // cols] + col_table[:, cond_ids % cols]
    steps = swap_steps({"row": row_count, "view": view_count})
    place = {"row": row_index, "view": view_index}

    def cond_part(keys, values, place):
        base = (place["view"] * row_count + place["row"]) * ctok_dev
        table = lax.dynamic_slice_in_dim(jnp.asarray(cond_table), base, ctok_dev, axis=1)
        return keys, values, table

    parts = [cond_part(cond_keys, cond_values, place)]
    if steps:
        axis, distance = steps[0]
        met_keys = swapped(cond_keys, axis, distance)
        met_values = swapped(cond_values, axis, distance)
        met_place = dict(place, **{axis: place[axis] ^ distance})
        parts.append(cond_part(met_keys, met_values, met_place))
    piece = pl.pallas_call(
        functools.partial(cond_kernel, len(parts)),
        out_shape=jax.ShapeDtypeStruct((2, len(parts) * ctok_dev, width), jnp.bfloat16),
        compiler_params=pltpu.CompilerParams(vmem_limit_bytes=KERNEL_VMEM),
        name="join",
    )(*(x for part in parts for x in part), partners)
    cond_held = gathered(piece, steps[1:])

    view_first = view_index * view_dev + 1
    tables = lax.dynamic_slice_in_dim(jnp.asarray(view_table), view_first, view_dev, axis=1)
    rows_here = lax.dynamic_slice_in_dim(
        jnp.asarray(row_table), row_index * rows_dev, rows_dev, axis=1
    )
    in_view = (rows_here[:, :, None] + jnp.asarray(col_table)[:, None]).reshape(2, tokens, HD)

    reach = -(-RADIUS // rows_dev)
    flags = []
    for d in range(1, reach + 1):
        flags += [row_index - d >= 0, row_index + d < row_count]
    valid = jnp.stack(flags).astype(jnp.int32)

    outputs = []
    for v in range(view_dev):
        values = target_values[v].reshape(tokens, width)
        whole = pl.BlockSpec(memory_space=pltpu.VMEM)
        lane_block = pl.BlockSpec((tokens, group * HD), lambda g: (0, g))
        rotate = pl.pallas_call(
            functools.partial(rotate_kernel, chunks, group),
            out_shape=[
                pltpu.VMEM((tokens, width), jnp.bfloat16),
                *(
                    jax.ShapeDtypeStruct((tokens, count * HD), jnp.bfloat16)
                    for _, count in chunks
                ),
            ],
            grid=(heads // group,),
            in_specs=[
                lane_block,
                lane_block,
                pl.BlockSpec((2, tokens, HD), lambda g: (0, 0, 0)),
                pl.BlockSpec((HD, HD), lambda g: (0, 0)),
            ],
            out_specs=[whole] * (1 + len(chunks)),
            compiler_params=pltpu.CompilerParams(vmem_limit_bytes=KERNEL_VMEM),
            cost_estimate=pl.CostEstimate(
                flops=4 * tokens * width * HD, bytes_accessed=8 * tokens * width, transcendentals=0
            ),
            name="rotate",
        )
        q_rot, *k_rot = rotate(
            queries[v].reshape(tokens, width),
            target_keys[v].reshape(tokens, width),
            tables[:, v : v + 1] + in_view,
            partners,
        )

        travels = {"values": values} | {f"keys{c}": k for c, k in enumerate(k_rot)}
        met = {}
        for what, block in travels.items():
            above = below = block
            for d in range(1, reach + 1):
                above = passed_along(above, "row", 1)
                below = passed_along(below, "row", -1)
                met[what, -d], met[what, d] = above, below
            met[what, 0] = block

        out = None
        for c, (first, count) in enumerate(chunks):

            def stage_of(d):
                tiles, plan = mask_tiles(rows_dev, cols, d * rows_dev, lanes)
                block = Block(plan, first, first, 0, cols)
                flag = 2 * (abs(d) - 1) + (d > 0) if d else None
                return (met[f"keys{c}", d], met["values", d]), (flag, (block,)), tiles

            def run(state, picked, **more):
                sources, stages, tiles = zip(*map(stage_of, picked))
                return attend(valid, q_rot, state, sources, stages, tiles, count, group, **more)

            state = run(None, [0])
            near = [d for far in range(1, reach) for d in (-far, far)]
            if near:
                state = run(state, near)
            block = Block((), first, 0, 0, cols, True)
            state = attend(
                valid, q_rot, state, [(x,) for x in cond_held],
                [(None, (block,) * len(cond_held))], [], count, group,
            )
            out, *_ = run(state, [-reach, reach], out=out, last=True)
        outputs.append(out.reshape(rows_dev, cols, width))
    return jnp.stack(outputs) if view_dev > 1 else outputs[0][None]


def solution(mesh):
    return jax.shard_map(
        local,
        mesh=mesh,
        in_specs=(
            P("view", "row", None, None),
            P("view", "row", None, None),
            P("view", "row", None, None),
            P(("view", "row"), None),
            P(("view", "row"), None),
        ),
        out_specs=P("view", "row", None, None),
        check_vma=False,
    )
```

time: 177 us -> 173 us (0.977)
  starting transfers between devices: 35.7 us -> 48.2 us
  waiting for transfers between devices: 84.3 us -> 72.7 us
  other arithmetic: 6.17 us -> 1.65 us
  Pallas kernels: 42.7 us -> 39.6 us
  local copies, waits for them, and re-layouts: 4.99 us -> 7.2 us
    ppermute x8 -> x12, starting transfers between devices: 27.9 us -> 38.8 us  [passed_along(): return lax.ppermute(x, axis, pairs)]
    ppermute x8 -> x12, waiting for transfers between devices: 42 us -> 35.7 us  [passed_along(): return lax.ppermute(x, axis, pairs)]
    ppermute x5 -> x6, waiting for transfers between devices: 42.3 us -> 36.9 us  [swapped(): lax.ppermute(x, axis, [(i, i ^ distance) for i in range(lax.axis_size(axi...]
    unnamed x8 -> x32, local copies, waits for them, and re-layouts: 0.99 us -> 5.08 us
    concatenate x3, other arithmetic: 3.81 us -> 1.53 us  [gathered(): whole = jnp.concatenate(held, axis=1) if len(held) > 1 else held[0]]
    pallas_call x1, Pallas kernels: 4.46 us -> 2.19 us  [local(): rotate(queries[v].reshape(tokens, width), target_keys[v].reshape(tokens,...]
    ppermute x5 -> x6, starting transfers between devices: 7.82 us -> 9.36 us  [swapped(): lax.ppermute(x, axis, [(i, i ^ distance) for i in range(lax.axis_size(axi...]
    pallas_call x5 -> x9, Pallas kernels: 38.2 us -> 37.4 us  [the longest x8 37.1 us: attend(): pl.pallas_call(functools.partial(attend_kernel, stages, state is None, ou...]
  transfers between devices with their start and end apart: 13 -> 18, of which waited for: 8 -> 9; matrix products, arithmetic and copies ran while one was open for 3% -> 2% of each run, Pallas kernels for 18% -> 21%
where the time goes in v1:
time: 173 us; the launch traced here: 170 us
  waiting for transfers between devices  72.7 us (42%)
  starting transfers between devices  48.2 us (28%)
  Pallas kernels  39.6 us (23%)
  local copies, waits for them, and re-layouts  7.2 us (4%)
    ppermute x12, starting transfers between devices, passed_along(): return lax.ppermute(x, axis, pairs)  38.8 us
    pallas_call x8, Pallas kernels, attend(): pl.pallas_call(functools.partial(attend_kernel, stages, state is None, ou...  37.1 us
    ppermute x6, waiting for transfers between devices, swapped(): lax.ppermute(x, axis, [(i, i ^ distance) for i in range(lax.axis_size(axi...  36.9 us
    ppermute x12, waiting for transfers between devices, passed_along(): return lax.ppermute(x, axis, pairs)  35.7 us
    ppermute x6, starting transfers between devices, swapped(): lax.ppermute(x, axis, [(i, i ^ distance) for i in range(lax.axis_size(axi...  9.36 us
    unnamed x32, local copies, waits for them, and re-layouts  5.08 us
  transfers between devices with their start and end apart: 18, of which 9 were waited for; matrix products, arithmetic and copies ran while one was open for 2% of the time, Pallas kernels for 21%

profile of v1, /device:TPU:0, one launch (start us, length us, event | category | flops | bytes accessed | tf_op | source)
XLA Modules:
  0.0 169.7 jit_solution(2076293042935907799)
XLA Ops:
  0.0 4.1 %collective-permute-start.8 = (bf16[16,2048]{1,0:T(8,128)(2,1)}, bf16[16,2048]{1,0:T(8,128)(2,1)S(1)}, u32[]{:S(2)}, u32[]{:S(2)}) collective-permute-start(bf16[16,2048]{1,0:T(8,128)(2,1)} %refs_0_.1), channel_id=1, source_target_pairs={{0,2},{1,3},{2,0},{3,1},{4,6},{5,7},{6,4},{7,5},{8,10},{9,11},{10,... | collective-permute-start | bytes 196616 | tf_op jit(solution)/shard_map/ppermute | solution.py:287
  4.1 0.1 collective-permute-start.9
  4.1 0.7 constant_dynamic-slice_fusion
  4.9 3.1 %collective-permute-done.8.refs_3_ = bf16[16,2048]{1,0:T(8,128)(2,1)S(1)} collective-permute-done((bf16[16,2048]{1,0:T(8,128)(2,1)}, bf16[16,2048]{1,0:T(8,128)(2,1)S(1)}, u32[]{:S(2)}, u32[]{:S(2)}) %collective-permute-start.8) | collective-permute-done | bytes 65568 | tf_op jit(solution)/shard_map/ppermute | solution.py:287
  8.0 2.8 %collective-permute-done.9.refs_4_ = bf16[16,2048]{1,0:T(8,128)(2,1)S(1)} collective-permute-done((bf16[16,2048]{1,0:T(8,128)(2,1)}, bf16[16,2048]{1,0:T(8,128)(2,1)S(1)}, u32[]{:S(2)}, u32[]{:S(2)}) %collective-permute-start.9) | collective-permute-done | bytes 65568 | tf_op jit(solution)/shard_map/ppermute | solution.py:287
  10.7 0.8 copy-done.11
  11.5 0.8 copy-done.13
  12.3 0.8 copy-done.14
  13.2 0.4 join.1
  13.6 0.7 collective-permute-start.10
  14.3 6.5 %collective-permute-done.10 = bf16[2,32,2048]{2,1,0:T(8,128)(2,1)S(1)} collective-permute-done((bf16[2,32,2048]{2,1,0:T(8,128)(2,1)S(1)}, bf16[2,32,2048]{2,1,0:T(8,128)(2,1)S(1)}, u32[]{:S(2)}, u32[]{:S(2)}) %collective-permute-start.10) | collective-permute-done | bytes 262176 | tf_op jit(solution)/shard_map/ppermute | solution.py:287
  20.8 2.7 %collective-permute-start.11 = (bf16[2,64,2048]{2,1,0:T(8,128)(2,1)S(1)}, bf16[2,64,2048]{2,1,0:T(8,128)(2,1)S(1)}, u32[]{:S(2)}, u32[]{:S(2)}) collective-permute-start(bf16[2,64,2048]{2,1,0:T(8,128)(2,1)S(1)} %pad_maximum_fusion.2), channel_id=1, source_target_pairs={{0,16},{4,20},{8,24},{12,28},{16,0},{20,4},{24,8},{28,12},{1,17},{... | collective-permute-start | bytes 1572872 | tf_op jit(solution)/shard_map/ppermute | solution.py:287
  23.5 11.0 %collective-permute-done.11 = bf16[2,64,2048]{2,1,0:T(8,128)(2,1)S(1)} collective-permute-done((bf16[2,64,2048]{2,1,0:T(8,128)(2,1)S(1)}, bf16[2,64,2048]{2,1,0:T(8,128)(2,1)S(1)}, u32[]{:S(2)}, u32[]{:S(2)}) %collective-permute-start.11) | collective-permute-done | bytes 524320 | tf_op jit(solution)/shard_map/ppermute | solution.py:287
  34.5 0.1 pad_maximum_fusion.1
  34.6 1.8 %collective-permute-start.12 = (bf16[2,128,2048]{2,1,0:T(8,128)(2,1)S(1)}, bf16[2,128,2048]{2,1,0:T(8,128)(2,1)}, u32[]{:S(2)}, u32[]{:S(2)}) collective-permute-start(bf16[2,128,2048]{2,1,0:T(8,128)(2,1)S(1)} %pad_maximum_fusion.1), channel_id=1, source_target_pairs={{0,8},{4,12},{8,0},{12,4},{16,24},{20,28},{24,16},{28,20},{1,9},{5... | collective-permute-start | bytes 3145736 | tf_op jit(solution)/shard_map/ppermute | solution.py:287
  36.4 1.3 collective-permute-start.6
  37.7 5.6 %collective-permute-start.2 = (bf16[256,2048]{1,0:T(8,128)(2,1)}, bf16[256,2048]{1,0:T(8,128)(2,1)}, u32[]{:S(2)}, u32[]{:S(2)}) collective-permute-start(bf16[256,2048]{1,0:T(8,128)(2,1)} %bitcast.8.refs_3_), channel_id=1, source_target_pairs={{0,1},{1,2},{2,3},{4,5},{5,6},{6,7},{8,9},{9,10},{10,11},{12,13},{... | collective-permute-start | bytes 3145736 | tf_op jit(solution)/shard_map/ppermute | solution.py:275
  43.2 0.7 dynamic-slice_bitcast_fusion
  43.9 0.7 constant_dynamic-slice_fusion.2
  44.7 0.0 copy-start.1
  44.7 0.0 copy-start.2
  44.7 0.0 copy-start.12
  44.7 13.5 %collective-permute-done.12 = bf16[2,128,2048]{2,1,0:T(8,128)(2,1)} collective-permute-done((bf16[2,128,2048]{2,1,0:T(8,128)(2,1)S(1)}, bf16[2,128,2048]{2,1,0:T(8,128)(2,1)}, u32[]{:S(2)}, u32[]{:S(2)}) %collective-permute-start.12) | collective-permute-done | bytes 1048608 | tf_op jit(solution)/shard_map/ppermute | solution.py:287
  58.2 1.4 pad_maximum_fusion.refs_2_
  59.6 0.0 copy-start
  59.7 0.1 collective-permute-start.13
  59.8 2.2 %rotate.1 = (bf16[256,2048]{1,0:T(8,128)(2,1)S(1)}, bf16[256,1536]{1,0:T(8,128)(2,1)S(1)}, bf16[256,512]{1,0:T(8,128)(2,1)S(1)}) custom-call(bf16[256,2048]{1,0:T(8,128)(2,1)S(1)} %bitcast.12, bf16[256,2048]{1,0:T(8,128)(2,1)S(1)} %bitcast.13, f32[2,256,128]{2,1,0:T(8,128)S(1)} %bitcast_add_fusion.table_ref, bf16[128,128]{1,0:T(8,128)(2,1)S(1)} %copy-done.12), custom_call_target="tpu_custom_call" | custom-call | flops 268435456 | bytes 4194304 | tf_op jit(solution)/shard_map/rotate/pallas_call | solution.py:386
  62.0 1.3 collective-permute-start.4
  63.3 4.6 %collective-permute-start = (bf16[256,512]{1,0:T(8,128)(2,1)S(1)}, bf16[256,512]{1,0:T(8,128)(2,1)S(1)}, u32[]{:S(2)}, u32[]{:S(2)}) collective-permute-start(bf16[256,512]{1,0:T(8,128)(2,1)S(1)} %get-tuple-element.23.refs_2_), channel_id=1, source_target_pairs={{0,1},{1,2},{2,3},{4,5},{5,6},{6,7},{8,9},{9,10},{10,11},{12,13},{... | collective-permute-start | bytes 786440 | tf_op jit(solution)/shard_map/ppermute | solution.py:275
  67.9 0.7 copy-done.9
  68.6 4.0 %collective-permute-done.4.refs_4_ = bf16[256,512]{1,0:T(8,128)(2,1)S(1)} collective-permute-done((bf16[256,512]{1,0:T(8,128)(2,1)S(1)}, bf16[256,512]{1,0:T(8,128)(2,1)S(1)}, u32[]{:S(2)}, u32[]{:S(2)}) %collective-permute-start.4) | collective-permute-done | bytes 262176 | tf_op jit(solution)/shard_map/ppermute | solution.py:275
  72.6 1.3 collective-permute-start.16
  73.9 0.0 collective-permute-done.refs_2_
  73.9 5.4 %collective-permute-start.14 = (bf16[256,1536]{1,0:T(8,128)(2,1)S(1)}, bf16[256,1536]{1,0:T(8,128)(2,1)}, u32[]{:S(2)}, u32[]{:S(2)}) collective-permute-start(bf16[256,1536]{1,0:T(8,128)(2,1)S(1)} %get-tuple-element.30.refs_2_), channel_id=1, source_target_pairs={{0,1},{1,2},{2,3},{4,5},{5,6},{6,7},{8,9},{9,10},{10,11},{12,13},{... | collective-permute-start | bytes 2359304 | tf_op jit(solution)/shard_map/ppermute | solution.py:275
  79.3 0.9 copy-done.3
  80.2 0.0 collective-permute-done.6.refs_5_
  80.2 1.3 collective-permute-start.7
  81.5 0.0 collective-permute-done.2.refs_3_
  81.5 5.6 %collective-permute-start.3 = (bf16[256,2048]{1,0:T(8,128)(2,1)}, bf16[256,2048]{1,0:T(8,128)(2,1)}, u32[]{:S(2)}, u32[]{:S(2)}) collective-permute-start(bf16[256,2048]{1,0:T(8,128)(2,1)} %collective-permute-done.2.refs_3_), channel_id=1, source_target_pairs={{0,1},{1,2},{2,3},{4,5},{5,6},{6,7},{8,9},{9,10},{10,11},{12,13},{... | collective-permute-start | bytes 3145736 | tf_op jit(solution)/shard_map/ppermute | solution.py:275
  87.1 7.9 %collective-permute-done.16.refs_4_ = bf16[256,1536]{1,0:T(8,128)(2,1)} collective-permute-done((bf16[256,1536]{1,0:T(8,128)(2,1)S(1)}, bf16[256,1536]{1,0:T(8,128)(2,1)}, u32[]{:S(2)}, u32[]{:S(2)}) %collective-permute-start.16) | collective-permute-done | bytes 786464 | tf_op jit(solution)/shard_map/ppermute | solution.py:275
  95.0 1.3 collective-permute-start.17
  96.3 0.1 collective-permute-done.14.refs_2_
  96.4 5.4 %collective-permute-start.15 = (bf16[256,1536]{1,0:T(8,128)(2,1)}, bf16[256,1536]{1,0:T(8,128)(2,1)}, u32[]{:S(2)}, u32[]{:S(2)}) collective-permute-start(bf16[256,1536]{1,0:T(8,128)(2,1)} %collective-permute-done.14.refs_2_), channel_id=1, source_target_pairs={{0,1},{1,2},{2,3},{4,5},{5,6},{6,7},{8,9},{9,10},{10,11},{12,13},{... | collective-permute-start | bytes 2359304 | tf_op jit(solution)/shard_map/ppermute | solution.py:275
  101.8 0.1 add_convert_fusion.refs_0_
  101.9 1.0 copy-done.10
  102.9 2.6 %shard_map.190 = (f32[4,128,256]{2,1,0:T(8,128)S(1)}, f32[4,2,256]{2,1,0:T(2,128)S(1)}) custom-call(s32[4]{0:T(128)S(1)} %add_convert_fusion.refs_0_, bf16[256,2048]{1,0:T(8,128)(2,1)S(1)} %get-tuple-element.22.refs_1_, bf16[256,512]{1,0:T(8,128)(2,1)S(1)} %copy-done.10, bf16[256,2048]{1,0:T(8,128)(2,1)} %bitcast.8.refs_3_, f32[1,64,128]{2,1,0:T(8,128)S(1)} %copy-done), custom_call_target="tpu_custom_call" | custom-call | flops 134217728 | bytes 1572864 | tf_op jit(solution)/shard_map/pallas_call | solution.py:254
  105.5 4.3 %shard_map.193 = (f32[12,128,256]{2,1,0:T(8,128)S(1)}, f32[12,2,256]{2,1,0:T(2,128)S(1)}) custom-call(s32[4]{0:T(128)S(1)} %add_convert_fusion.refs_0_, bf16[256,2048]{1,0:T(8,128)(2,1)S(1)} %get-tuple-element.22.refs_1_, bf16[256,1536]{1,0:T(8,128)(2,1)S(1)} %copy-done.4, bf16[256,2048]{1,0:T(8,128)(2,1)} %bitcast.8.refs_3_, f32[1,64,128]{2,1,0:T(8,128)S(1)} %copy-done), custom_call_target="tpu_custom_call" | custom-call | flops 402653184 | bytes 4718592 | tf_op jit(solution)/shard_map/pallas_call | solution.py:254
  109.8 23.7 %collective-permute-done.17.refs_4_ = bf16[256,1536]{1,0:T(8,128)(2,1)} collective-permute-done((bf16[256,1536]{1,0:T(8,128)(2,1)}, bf16[256,1536]{1,0:T(8,128)(2,1)}, u32[]{:S(2)}, u32[]{:S(2)}) %collective-permute-start.17) | collective-permute-done | bytes 786464 | tf_op jit(solution)/shard_map/ppermute | solution.py:275
  133.5 1.3 collective-permute-start.5
  134.8 0.0 collective-permute-done.13.refs_3_
  134.8 4.6 %collective-permute-start.1 = (bf16[256,512]{1,0:T(8,128)(2,1)S(1)}, bf16[256,512]{1,0:T(8,128)(2,1)S(1)}, u32[]{:S(2)}, u32[]{:S(2)}) collective-permute-start(bf16[256,512]{1,0:T(8,128)(2,1)S(1)} %copy-done.8), channel_id=1, source_target_pairs={{0,1},{1,2},{2,3},{4,5},{5,6},{6,7},{8,9},{9,10},{10,11},{12,13},{... | collective-permute-start | bytes 786440 | tf_op jit(solution)/shard_map/ppermute | solution.py:275
  139.3 2.9 %shard_map.191 = (f32[4,128,256]{2,1,0:T(8,128)S(1)}, f32[4,2,256]{2,1,0:T(2,128)S(1)}) custom-call(s32[4]{0:T(128)S(1)} %add_convert_fusion.refs_0_, bf16[256,2048]{1,0:T(8,128)(2,1)S(1)} %get-tuple-element.22.refs_1_, bf16[256,512]{1,0:T(8,128)(2,1)S(1)} %copy-done.8, ...), custom_call_target="tpu_custom_call", output_to_operand_aliasing={{0}: (8, {}), {1}: (9, {})} | custom-call | flops 268435456 | bytes 2097152 | tf_op jit(solution)/shard_map/pallas_call | solution.py:254
  142.3 5.2 %shard_map.194 = (f32[12,128,256]{2,1,0:T(8,128)S(1)}, f32[12,2,256]{2,1,0:T(2,128)S(1)}) custom-call(s32[4]{0:T(128)S(1)} %add_convert_fusion.refs_0_, bf16[256,2048]{1,0:T(8,128)(2,1)S(1)} %get-tuple-element.22.refs_1_, bf16[256,1536]{1,0:T(8,128)(2,1)} %collective-permute-done.14.refs_2_, ...), custom_call_target="tpu_custom_call", output_to_operand_aliasing={{0}: (8, {}), {1}: (9, {})} | custom-call | flops 805306368 | bytes 6291456 | tf_op jit(solution)/shard_map/pallas_call | solution.py:254
  147.5 3.5 %shard_map.192 = (f32[4,128,256]{2,1,0:T(8,128)S(1)}, f32[4,2,256]{2,1,0:T(2,128)S(1)}) custom-call(s32[4]{0:T(128)S(1)} %add_convert_fusion.refs_0_, bf16[256,2048]{1,0:T(8,128)(2,1)S(1)} %get-tuple-element.22.refs_1_, bf16[2,256,2048]{2,1,0:T(8,128)(2,1)S(1)} %pad_maximum_fusion.refs_2_, ...), custom_call_target="tpu_custom_call", output_to_operand_aliasing={{0}: (4, {}), {1}: (5, {})} | custom-call | flops 268435456 | bytes 2097152 | tf_op jit(solution)/shard_map/pallas_call | solution.py:254
  150.9 0.0 copy-start.5
  150.9 0.0 copy-start.6
  151.0 6.3 %shard_map.195 = (f32[12,128,256]{2,1,0:T(8,128)S(1)}, f32[12,2,256]{2,1,0:T(2,128)S(1)}) custom-call(s32[4]{0:T(128)S(1)} %add_convert_fusion.refs_0_, bf16[256,2048]{1,0:T(8,128)(2,1)S(1)} %get-tuple-element.22.refs_1_, bf16[2,256,2048]{2,1,0:T(8,128)(2,1)S(1)} %pad_maximum_fusion.refs_2_, ...), custom_call_target="tpu_custom_call", output_to_operand_aliasing={{0}: (4, {}), {1}: (5, {})} | custom-call | flops 805306368 | bytes 6291456 | tf_op jit(solution)/shard_map/pallas_call | solution.py:254
  157.3 0.0 collective-permute-done.15.refs_2_
  157.3 0.0 collective-permute-done.7.refs_5_
  157.3 0.0 collective-permute-done.3.refs_3_
  157.3 8.0 %shard_map.196 = (bf16[256,2048]{1,0:T(8,128)(2,1)}, f32[12,128,256]{2,1,0:T(8,128)S(1)}, f32[12,2,256]{2,1,0:T(2,128)S(1)}) custom-call(s32[4]{0:T(128)S(1)} %add_convert_fusion.refs_0_, bf16[256,2048]{1,0:T(8,128)(2,1)S(1)} %get-tuple-element.22.refs_1_, ...), custom_call_target="tpu_custom_call", output_to_operand_aliasing={{1}: (8, {}), {2}: (9, {})} | custom-call | flops 805306368 | bytes 6291456 | tf_op jit(solution)/shard_map/pallas_call | solution.py:254
  165.3 0.0 collective-permute-done.5.refs_4_
  165.3 0.0 collective-permute-done.1.refs_2_
  165.3 4.3 %shard_map.197 = (bf16[256,2048]{1,0:T(8,128)(2,1)}, f32[4,128,256]{2,1,0:T(8,128)S(1)}, f32[4,2,256]{2,1,0:T(2,128)S(1)}) custom-call(s32[4]{0:T(128)S(1)} %add_convert_fusion.refs_0_, bf16[256,2048]{1,0:T(8,128)(2,1)S(1)} %get-tuple-element.22.refs_1_, ...), custom_call_target="tpu_custom_call", output_to_operand_aliasing={{1}: (8, {}), {2}: (9, {}), {0}: (10, {})} | custom-call | flops 268435456 | bytes 2097152 | tf_op jit(solution)/shard_map/pallas_call | solution.py:254
  (23 shorter events, 0.1 us)
Async XLA Ops:
  0.0 44.6 %copy-start.15 = (f32[2,64,128]{2,1,0:T(8,128)S(1)}, f32[2,64,128]{2,1,0:T(8,128)}, u32[]{:S(2)}) copy-start(f32[2,64,128]{2,1,0:T(8,128)} %constant.48.clone) | copy-start | bytes 196612
  0.0 8.0 %collective-permute-start.8 = (bf16[16,2048]{1,0:T(8,128)(2,1)}, bf16[16,2048]{1,0:T(8,128)(2,1)S(1)}, u32[]{:S(2)}, u32[]{:S(2)}) collective-permute-start(bf16[16,2048]{1,0:T(8,128)(2,1)} %refs_0_.1), channel_id=1, source_target_pairs={{0,2},{1,3},{2,0},{3,1},{4,6},{5,7},{6,4},{7,5},{8,10},{9,11},{10,... | collective-permute-start | bytes 196616 | tf_op jit(solution)/shard_map/ppermute | solution.py:287
  4.1 6.7 %collective-permute-start.9 = (bf16[16,2048]{1,0:T(8,128)(2,1)}, bf16[16,2048]{1,0:T(8,128)(2,1)S(1)}, u32[]{:S(2)}, u32[]{:S(2)}) collective-permute-start(bf16[16,2048]{1,0:T(8,128)(2,1)} %refs_1_.1), channel_id=1, source_target_pairs={{0,2},{1,3},{2,0},{3,1},{4,6},{5,7},{6,4},{7,5},{8,10},{9,11},{10,... | collective-permute-start | bytes 196616 | tf_op jit(solution)/shard_map/ppermute | solution.py:287
  10.7 0.8 copy-start.11
  11.5 0.8 copy-start.13
  12.3 0.8 copy-start.14
  13.6 7.2 %collective-permute-start.10 = (bf16[2,32,2048]{2,1,0:T(8,128)(2,1)S(1)}, bf16[2,32,2048]{2,1,0:T(8,128)(2,1)S(1)}, u32[]{:S(2)}, u32[]{:S(2)}) collective-permute-start(bf16[2,32,2048]{2,1,0:T(8,128)(2,1)S(1)} %join.1), channel_id=1, source_target_pairs={{0,1},{1,0},{2,3},{3,2},{4,5},{5,4},{6,7},{7,6},{8,9},{9,8},{10,11... | collective-permute-start | bytes 786440 | tf_op jit(solution)/shard_map/ppermute | solution.py:287
  20.8 13.7 %collective-permute-start.11 = (bf16[2,64,2048]{2,1,0:T(8,128)(2,1)S(1)}, bf16[2,64,2048]{2,1,0:T(8,128)(2,1)S(1)}, u32[]{:S(2)}, u32[]{:S(2)}) collective-permute-start(bf16[2,64,2048]{2,1,0:T(8,128)(2,1)S(1)} %pad_maximum_fusion.2), channel_id=1, source_target_pairs={{0,16},{4,20},{8,24},{12,28},{16,0},{20,4},{24,8},{28,12},{1,17},{... | collective-permute-start | bytes 1572872 | tf_op jit(solution)/shard_map/ppermute | solution.py:287
  34.6 23.6 %collective-permute-start.12 = (bf16[2,128,2048]{2,1,0:T(8,128)(2,1)S(1)}, bf16[2,128,2048]{2,1,0:T(8,128)(2,1)}, u32[]{:S(2)}, u32[]{:S(2)}) collective-permute-start(bf16[2,128,2048]{2,1,0:T(8,128)(2,1)S(1)} %pad_maximum_fusion.1), channel_id=1, source_target_pairs={{0,8},{4,12},{8,0},{12,4},{16,24},{20,28},{24,16},{28,20},{1,9},{5... | collective-permute-start | bytes 3145736 | tf_op jit(solution)/shard_map/ppermute | solution.py:287
  36.4 43.8 %collective-permute-start.6 = (bf16[256,2048]{1,0:T(8,128)(2,1)}, bf16[256,2048]{1,0:T(8,128)(2,1)}, u32[]{:S(2)}, u32[]{:S(2)}) collective-permute-start(bf16[256,2048]{1,0:T(8,128)(2,1)} %bitcast.8.refs_3_), channel_id=1, source_target_pairs={{1,0},{2,1},{3,2},{5,4},{6,5},{7,6},{9,8},{10,9},{11,10},{13,12},{... | collective-permute-start | bytes 3145736 | tf_op jit(solution)/shard_map/ppermute | solution.py:275
  37.7 43.8 %collective-permute-start.2 = (bf16[256,2048]{1,0:T(8,128)(2,1)}, bf16[256,2048]{1,0:T(8,128)(2,1)}, u32[]{:S(2)}, u32[]{:S(2)}) collective-permute-start(bf16[256,2048]{1,0:T(8,128)(2,1)} %bitcast.8.refs_3_), channel_id=1, source_target_pairs={{0,1},{1,2},{2,3},{4,5},{5,6},{6,7},{8,9},{9,10},{10,11},{12,13},{... | collective-permute-start | bytes 3145736 | tf_op jit(solution)/shard_map/ppermute | solution.py:275
  44.7 15.1 %copy-start.1 = (bf16[1,4,64,2048]{3,2,1,0:T(8,128)(2,1)S(1)}, bf16[1,4,64,2048]{3,2,1,0:T(8,128)(2,1)}, u32[]{:S(2)}) copy-start(bf16[1,4,64,2048]{3,2,1,0:T(8,128)(2,1)} %param.20) | copy-start | bytes 3145732
  44.7 15.1 %copy-start.2 = (bf16[1,4,64,2048]{3,2,1,0:T(8,128)(2,1)S(1)}, bf16[1,4,64,2048]{3,2,1,0:T(8,128)(2,1)}, u32[]{:S(2)}) copy-start(bf16[1,4,64,2048]{3,2,1,0:T(8,128)(2,1)} %param.21) | copy-start | bytes 3145732
  44.7 15.1 %copy-start.12 = (bf16[128,128]{1,0:T(8,128)(2,1)S(1)}, bf16[128,128]{1,0:T(8,128)(2,1)}, u32[]{:S(2)}) copy-start(bf16[128,128]{1,0:T(8,128)(2,1)} %constant.44.clone.partners_ref.refs_6_) | copy-start | bytes 98308
  59.6 42.2 %copy-start = (f32[1,64,128]{2,1,0:T(8,128)S(1)}, f32[1,64,128]{2,1,0:T(8,128)}, u32[]{:S(2)}) copy-start(f32[1,64,128]{2,1,0:T(8,128)} %constant.49.clone.refs_4_.refs_6_.refs_7_) | copy-start | bytes 98308
  59.7 75.1 %collective-permute-start.13 = (bf16[2,256,2048]{2,1,0:T(8,128)(2,1)S(1)}, bf16[2,256,2048]{2,1,0:T(8,128)(2,1)}, u32[]{:S(2)}, u32[]{:S(2)}) collective-permute-start(bf16[2,256,2048]{2,1,0:T(8,128)(2,1)S(1)} %pad_maximum_fusion.refs_2_), channel_id=1, source_target_pairs={{0,4},{4,0},{8,12},{12,8},{16,20},{20,16},{24,28},{28,24},{1,5},{5... | collective-permute-start | bytes 6291464 | tf_op jit(solution)/shard_map/ppermute | solution.py:287
  62.0 10.6 %collective-permute-start.4 = (bf16[256,512]{1,0:T(8,128)(2,1)S(1)}, bf16[256,512]{1,0:T(8,128)(2,1)S(1)}, u32[]{:S(2)}, u32[]{:S(2)}) collective-permute-start(bf16[256,512]{1,0:T(8,128)(2,1)S(1)} %get-tuple-element.23.refs_2_), channel_id=1, source_target_pairs={{1,0},{2,1},{3,2},{5,4},{6,5},{7,6},{9,8},{10,9},{11,10},{13,12},{... | collective-permute-start | bytes 786440 | tf_op jit(solution)/shard_map/ppermute | solution.py:275
  63.3 10.6 %collective-permute-start = (bf16[256,512]{1,0:T(8,128)(2,1)S(1)}, bf16[256,512]{1,0:T(8,128)(2,1)S(1)}, u32[]{:S(2)}, u32[]{:S(2)}) collective-permute-start(bf16[256,512]{1,0:T(8,128)(2,1)S(1)} %get-tuple-element.23.refs_2_), channel_id=1, source_target_pairs={{0,1},{1,2},{2,3},{4,5},{5,6},{6,7},{8,9},{9,10},{10,11},{12,13},{... | collective-permute-start | bytes 786440 | tf_op jit(solution)/shard_map/ppermute | solution.py:275
  67.9 0.7 copy-start.9
  72.6 22.4 %collective-permute-start.16 = (bf16[256,1536]{1,0:T(8,128)(2,1)S(1)}, bf16[256,1536]{1,0:T(8,128)(2,1)}, u32[]{:S(2)}, u32[]{:S(2)}) collective-permute-start(bf16[256,1536]{1,0:T(8,128)(2,1)S(1)} %get-tuple-element.30.refs_2_), channel_id=1, source_target_pairs={{1,0},{2,1},{3,2},{5,4},{6,5},{7,6},{9,8},{10,9},{11,10},{13,12},{... | collective-permute-start | bytes 2359304 | tf_op jit(solution)/shard_map/ppermute | solution.py:275
  73.9 22.5 %copy-start.7 = (bf16[256,512]{1,0:T(8,128)(2,1)}, bf16[256,512]{1,0:T(8,128)(2,1)S(1)}, u32[]{:S(2)}) copy-start(bf16[256,512]{1,0:T(8,128)(2,1)S(1)} %collective-permute-done.refs_2_) | copy-start | bytes 786436
  73.9 22.5 %collective-permute-start.14 = (bf16[256,1536]{1,0:T(8,128)(2,1)S(1)}, bf16[256,1536]{1,0:T(8,128)(2,1)}, u32[]{:S(2)}, u32[]{:S(2)}) collective-permute-start(bf16[256,1536]{1,0:T(8,128)(2,1)S(1)} %get-tuple-element.30.refs_2_), channel_id=1, source_target_pairs={{0,1},{1,2},{2,3},{4,5},{5,6},{6,7},{8,9},{9,10},{10,11},{12,13},{... | collective-permute-start | bytes 2359304 | tf_op jit(solution)/shard_map/ppermute | solution.py:275
  79.3 0.9 copy-start.3
  80.2 77.1 %collective-permute-start.7 = (bf16[256,2048]{1,0:T(8,128)(2,1)}, bf16[256,2048]{1,0:T(8,128)(2,1)}, u32[]{:S(2)}, u32[]{:S(2)}) collective-permute-start(bf16[256,2048]{1,0:T(8,128)(2,1)} %collective-permute-done.6.refs_5_), channel_id=1, source_target_pairs={{1,0},{2,1},{3,2},{5,4},{6,5},{7,6},{9,8},{10,9},{11,10},{13,12},{... | collective-permute-start | bytes 3145736 | tf_op jit(solution)/shard_map/ppermute | solution.py:275
  81.5 75.8 %collective-permute-start.3 = (bf16[256,2048]{1,0:T(8,128)(2,1)}, bf16[256,2048]{1,0:T(8,128)(2,1)}, u32[]{:S(2)}, u32[]{:S(2)}) collective-permute-start(bf16[256,2048]{1,0:T(8,128)(2,1)} %collective-permute-done.2.refs_3_), channel_id=1, source_target_pairs={{0,1},{1,2},{2,3},{4,5},{5,6},{6,7},{8,9},{9,10},{10,11},{12,13},{... | collective-permute-start | bytes 3145736 | tf_op jit(solution)/shard_map/ppermute | solution.py:275
  95.0 38.5 %collective-permute-start.17 = (bf16[256,1536]{1,0:T(8,128)(2,1)}, bf16[256,1536]{1,0:T(8,128)(2,1)}, u32[]{:S(2)}, u32[]{:S(2)}) collective-permute-start(bf16[256,1536]{1,0:T(8,128)(2,1)} %collective-permute-done.16.refs_4_), channel_id=1, source_target_pairs={{1,0},{2,1},{3,2},{5,4},{6,5},{7,6},{9,8},{10,9},{11,10},{13,12},{... | collective-permute-start | bytes 2359304 | tf_op jit(solution)/shard_map/ppermute | solution.py:275
  96.4 60.9 %collective-permute-start.15 = (bf16[256,1536]{1,0:T(8,128)(2,1)}, bf16[256,1536]{1,0:T(8,128)(2,1)}, u32[]{:S(2)}, u32[]{:S(2)}) collective-permute-start(bf16[256,1536]{1,0:T(8,128)(2,1)} %collective-permute-done.14.refs_2_), channel_id=1, source_target_pairs={{0,1},{1,2},{2,3},{4,5},{5,6},{6,7},{8,9},{9,10},{10,11},{12,13},{... | collective-permute-start | bytes 2359304 | tf_op jit(solution)/shard_map/ppermute | solution.py:275
  101.8 3.7 %copy-start.4 = (bf16[256,1536]{1,0:T(8,128)(2,1)S(1)}, bf16[256,1536]{1,0:T(8,128)(2,1)}, u32[]{:S(2)}) copy-start(bf16[256,1536]{1,0:T(8,128)(2,1)} %copy-done.3) | copy-start | bytes 2359300
  101.9 1.0 copy-start.10
  102.9 31.9 %copy-start.8 = (bf16[256,512]{1,0:T(8,128)(2,1)S(1)}, bf16[256,512]{1,0:T(8,128)(2,1)}, u32[]{:S(2)}) copy-start(bf16[256,512]{1,0:T(8,128)(2,1)} %copy-done.7) | copy-start | bytes 786436
  133.5 31.8 %collective-permute-start.5 = (bf16[256,512]{1,0:T(8,128)(2,1)S(1)}, bf16[256,512]{1,0:T(8,128)(2,1)S(1)}, u32[]{:S(2)}, u32[]{:S(2)}) collective-permute-start(bf16[256,512]{1,0:T(8,128)(2,1)S(1)} %collective-permute-done.4.refs_4_), channel_id=1, source_target_pairs={{1,0},{2,1},{3,2},{5,4},{6,5},{7,6},{9,8},{10,9},{11,10},{13,12},{... | collective-permute-start | bytes 786440 | tf_op jit(solution)/shard_map/ppermute | solution.py:275
  134.8 30.5 %collective-permute-start.1 = (bf16[256,512]{1,0:T(8,128)(2,1)S(1)}, bf16[256,512]{1,0:T(8,128)(2,1)S(1)}, u32[]{:S(2)}, u32[]{:S(2)}) collective-permute-start(bf16[256,512]{1,0:T(8,128)(2,1)S(1)} %copy-done.8), channel_id=1, source_target_pairs={{0,1},{1,2},{2,3},{4,5},{5,6},{6,7},{8,9},{9,10},{10,11},{12,13},{... | collective-permute-start | bytes 786440 | tf_op jit(solution)/shard_map/ppermute | solution.py:275
  150.9 6.4 %copy-start.5 = (f32[2,64,128]{2,1,0:T(8,128)S(1)}, f32[2,64,128]{2,1,0:T(8,128)}, u32[]{:S(2)}) copy-start(f32[2,64,128]{2,1,0:T(8,128)} %constant.51.clone.refs_7_) | copy-start | bytes 196612
  150.9 6.4 %copy-start.6 = (f32[2,64,128]{2,1,0:T(8,128)S(1)}, f32[2,64,128]{2,1,0:T(8,128)}, u32[]{:S(2)}) copy-start(f32[2,64,128]{2,1,0:T(8,128)} %constant.50.clone.refs_6_) | copy-start | bytes 196612

commit v2 on v1

--- a/solution.py
+++ b/solution.py
@@ -114,7 +114,7 @@
 
 def attend_kernel(stages, first, last, group, lanes, *refs):
     refs = list(refs)
-    valid_ref, q_ref = refs.pop(0), refs.pop(0)
+    q_ref = refs.pop(0)
 
     def pull(block):
         if block.stacked:
@@ -138,58 +138,63 @@
         return pl.ds(pl.multiple_of((unit * group + head + offset) * HD, HD), HD)
 
     def stage(blocks, sources, mask_refs, have):
-        def scores(head, start):
-            q = q_ref[pl.ds(start, lanes), span_of(head, blocks[0].head)]
-            found = []
-            for block, (k_ref, _) in zip(blocks, sources):
-                low, high = block.rows(start // lanes, k_ref.shape[0])
-                k = k_ref[low:high, span_of(head, block.head - block.keys_head)]
-                found.append(
-                    lax.dot_general(
-                        k, q, (((1,), (1,)), ((), ())), preferred_element_type=jnp.float32
-                    )
+        def scores(head):
+            q = q_ref[:, span_of(head, blocks[0].head)]
+            return [
+                lax.dot_general(
+                    k_ref[:, span_of(head, block.head - block.keys_head)], q,
+                    (((1,), (1,)), ((), ())), preferred_element_type=jnp.float32,
                 )
-            return found
-
-        def update(head, start, found):
+                for block, (k_ref, _) in zip(blocks, sources)
+            ]
+
+        def update(head, found):
             at = unit * group + head
-            here = pl.ds(start, lanes)
             if have:
-                top = ml_ref[at, 0:1, here]
-                total = ml_ref[at, 1:2, here]
-                summed = acc_ref[at, :, here]
+                top, total, summed = ml_ref[at, 0:1], ml_ref[at, 1:2], acc_ref[at]
             started = have
             for s, block, (k_ref, v_ref), mask_ref in zip(found, blocks, sources, mask_refs):
-                low, high = block.rows(start // lanes, k_ref.shape[0])
-                if mask_ref is not None:
-                    names = block.plan[start // lanes][2]
-                    s = s + jnp.concatenate([mask_ref[n] for n in names], axis=0)
-                peak = jnp.max(s, axis=0, keepdims=True)
-                if started:
-                    peak = jnp.maximum(peak, top)
-                p = jnp.exp2((s - peak) * EXP_SCALE)
-                part = jnp.sum(p, axis=0, keepdims=True)
-                v = v_ref[low:high, span_of(head, block.head - block.values_head)]
+                count = k_ref.shape[0]
+                peaks, parts, weights = [], [], []
+                for start in range(0, tokens, lanes):
+                    here = slice(start, start + lanes)
+                    low, high = block.rows(start // lanes, count)
+                    seen = s[low:high, here]
+                    if mask_ref is not None:
+                        names = block.plan[start // lanes][2]
+                        seen = seen + jnp.concatenate([mask_ref[n] for n in names], axis=0)
+                    peak = jnp.max(seen, axis=0, keepdims=True)
+                    if started:
+                        peak = jnp.maximum(peak, top[:, here])
+                    p = jnp.exp2((seen - peak) * EXP_SCALE)
+                    peaks.append(peak)
+                    parts.append(jnp.sum(p, axis=0, keepdims=True))
+                    p = [p.astype(jnp.bfloat16)]
+                    if low:
+                        p.insert(0, jnp.zeros((low, lanes), jnp.bfloat16))
+                    if high < count:
+                        p.append(jnp.zeros((count - high, lanes), jnp.bfloat16))
+                    weights.append(jnp.concatenate(p, axis=0) if len(p) > 1 else p[0])
+                v = v_ref[:, span_of(head, block.head - block.values_head)]
                 pv = lax.dot_general(
-                    v, p.astype(jnp.bfloat16), (((0,), (0,)), ((), ())),
+                    v, jnp.concatenate(weights, axis=1), (((0,), (0,)), ((), ())),
                     preferred_element_type=jnp.float32,
                 )
+                peak, part = jnp.concatenate(peaks, axis=1), jnp.concatenate(parts, axis=1)
                 if started:
                     alpha = jnp.exp2((top - peak) * EXP_SCALE)
                     part = part + total * alpha
                     pv = pv + summed * alpha
                 top, total, summed, started = peak, part, pv, True
-            ml_ref[at, 0:1, here] = top
-            ml_ref[at, 1:2, here] = total
-            acc_ref[at, :, here] = summed
-
-        work = [(head, start) for head in range(group) for start in range(0, tokens, lanes)]
-        ahead = scores(*work[0])
-        for index, item in enumerate(work):
+            ml_ref[at, 0:1], ml_ref[at, 1:2], acc_ref[at] = top, total, summed
+
+        ahead = scores(0)
+        for head in range(group):
             found = ahead
-            if index + 1 < len(work):
-                ahead = scores(*work[index + 1])
-            update(*item, found)
+            if head + 1 < group:
+                ahead = scores(head + 1)
+            update(head, found)
+
 
     have = not first
     for (flag, blocks), sources, mask_refs in zip(stages, pulled, masks):
@@ -197,7 +202,8 @@
         if flag is None:
             step()
         else:
-            pl.when(valid_ref[flag] != 0)(step)
+            there = lax.axis_index("row") + flag
+            pl.when((there >= 0) & (there < lax.axis_size("row")))(step)
         have = True
     if last is not None:
         for head in range(group):
@@ -224,7 +230,7 @@
     return pltpu.with_memory_space_constraint(x, pltpu.VMEM)
 
 
-def attend(valid, q, state, sources, stages, tiles, heads, group, out=None, last=False):
+def attend(q, state, sources, stages, tiles, heads, group, out=None, last=False):
     tokens, width = q.shape
     lanes = 128 if tokens % 128 == 0 else tokens
     first_head = stages[0][1][0].head
@@ -233,7 +239,7 @@
     whole = pl.BlockSpec(memory_space=pltpu.VMEM)
     aliases = {}
     if state is not None:
-        aliases = {len(operands) + 1 + i: i + last for i in range(2)}
+        aliases = {len(operands) + i: i + last for i in range(2)}
         operands += [resident(a) for a in state]
     specs = [whole] * len(operands)
     out_shape = [
@@ -244,10 +250,10 @@
     if last:
         out_shape.insert(0, jax.ShapeDtypeStruct((tokens, width), jnp.bfloat16))
         out_specs.insert(
-            0, pl.BlockSpec((tokens, group * HD), lambda g, _: (0, first_head // group + g))
+            0, pl.BlockSpec((tokens, group * HD), lambda g: (0, first_head // group + g))
         )
         if out is not None:
-            aliases[len(operands) + 1] = 0
+            aliases[len(operands)] = 0
             operands.append(out)
             specs.append(pl.BlockSpec(memory_space=pl.ANY))
     keys_seen = sum(source[0].shape[-2] for source in sources)
@@ -256,9 +262,9 @@
             attend_kernel, stages, state is None, (out is not None) if last else None, group, lanes
         ),
         out_shape=out_shape,
-        grid_spec=pltpu.PrefetchScalarGridSpec(
-            num_scalar_prefetch=1, grid=(heads // group,), in_specs=specs, out_specs=out_specs
-        ),
+        grid=(heads // group,),
+        in_specs=specs,
+        out_specs=out_specs,
         input_output_aliases=aliases,
         compiler_params=pltpu.CompilerParams(vmem_limit_bytes=KERNEL_VMEM),
         cost_estimate=pl.CostEstimate(
@@ -266,7 +272,7 @@
             bytes_accessed=(4 * keys_seen + 8 * tokens) * heads * HD,
             transcendentals=tokens * keys_seen * heads,
         ),
-    )(valid, *operands)
+    )(*operands)
 
 
 def passed_along(x, axis, by):
@@ -350,11 +356,6 @@
     in_view = (rows_here[:, :, None] + jnp.asarray(col_table)[:, None]).reshape(2, tokens, HD)
 
     reach = -(-RADIUS // rows_dev)
-    flags = []
-    for d in range(1, reach + 1):
-        flags += [row_index - d >= 0, row_index + d < row_count]
-    valid = jnp.stack(flags).astype(jnp.int32)
-
     outputs = []
     for v in range(view_dev):
         values = target_values[v].reshape(tokens, width)
@@ -406,12 +407,11 @@
             def stage_of(d):
                 tiles, plan = mask_tiles(rows_dev, cols, d * rows_dev, lanes)
                 block = Block(plan, first, first, 0, cols)
-                flag = 2 * (abs(d) - 1) + (d > 0) if d else None
-                return (met[f"keys{c}", d], met["values", d]), (flag, (block,)), tiles
+                return (met[f"keys{c}", d], met["values", d]), (d or None, (block,)), tiles
 
             def run(state, picked, **more):
                 sources, stages, tiles = zip(*map(stage_of, picked))
-                return attend(valid, q_rot, state, sources, stages, tiles, count, group, **more)
+                return attend(q_rot, state, sources, stages, tiles, count, group, **more)
 
             state = run(None, [0])
             near = [d for far in range(1, reach) for d in (-far, far)]
@@ -419,7 +419,7 @@
                 state = run(state, near)
             block = Block((), first, 0, 0, cols, True)
             state = attend(
-                valid, q_rot, state, [(x,) for x in cond_held],
+                q_rot, state, [(x,) for x in cond_held],
                 [(None, (block,) * len(cond_held))], [], count, group,
             )
             out, *_ = run(state, [-reach, reach], out=out, last=True)

time: 173 us -> 157 us (0.908)
  Pallas kernels: 39.6 us -> 19.6 us
  waiting for transfers between devices: 72.7 us -> 82.7 us
  starting transfers between devices: 48.2 us -> 44.4 us
  local copies, waits for them, and re-layouts: 7.2 us -> 4.62 us
    pallas_call x8, Pallas kernels: 37.1 us -> 17 us  [attend(): pl.pallas_call(functools.partial(attend_kernel, stages, state is None, ou...]
    ppermute x12, waiting for transfers between devices: 35.7 us -> 44.6 us  [passed_along(): return lax.ppermute(x, axis, pairs)]
    ppermute x12, starting transfers between devices: 38.8 us -> 35.1 us  [passed_along(): return lax.ppermute(x, axis, pairs)]
    unnamed x32 -> x26, local copies, waits for them, and re-layouts: 5.08 us -> 2.49 us
  transfers between devices with their start and end apart: 18 -> 18, of which waited for: 9 -> 9; matrix products, arithmetic and copies ran while one was open for 2% -> 2% of each run, Pallas kernels for 21% -> 11%
where the time goes in v2:
time: 157 us; the launch traced here: 154 us
  waiting for transfers between devices  82.7 us (53%)
  starting transfers between devices  44.4 us (28%)
  Pallas kernels  19.6 us (12%)
  local copies, waits for them, and re-layouts  4.62 us (3%)
  other arithmetic  2.76 us (2%)
    ppermute x12, waiting for transfers between devices, passed_along(): return lax.ppermute(x, axis, pairs)  44.6 us
    ppermute x6, waiting for transfers between devices, swapped(): lax.ppermute(x, axis, [(i, i ^ distance) for i in range(lax.axis_size(axi...  38.1 us
    ppermute x12, starting transfers between devices, passed_along(): return lax.ppermute(x, axis, pairs)  35.1 us
    pallas_call x8, Pallas kernels, attend(): pl.pallas_call(functools.partial(attend_kernel, stages, state is None, ou...  17 us
    ppermute x6, starting transfers between devices, swapped(): lax.ppermute(x, axis, [(i, i ^ distance) for i in range(lax.axis_size(axi...  9.29 us
  transfers between devices with their start and end apart: 18, of which 9 were waited for; matrix products, arithmetic and copies ran while one was open for 2% of the time, Pallas kernels for 11%

profile of v2, /device:TPU:0, one launch (start us, length us, event | category | flops | bytes accessed | tf_op | source)
XLA Modules:
  0.0 154.3 jit_solution(12382779915169818209)
XLA Ops:
  0.0 4.1 %collective-permute-start.8 = (bf16[16,2048]{1,0:T(8,128)(2,1)}, bf16[16,2048]{1,0:T(8,128)(2,1)S(1)}, u32[]{:S(2)}, u32[]{:S(2)}) collective-permute-start(bf16[16,2048]{1,0:T(8,128)(2,1)} %refs_0_.1), channel_id=1, source_target_pairs={{0,2},{1,3},{2,0},{3,1},{4,6},{5,7},{6,4},{7,5},{8,10},{9,11},{10,... | collective-permute-start | bytes 196616 | tf_op jit(solution)/shard_map/ppermute | solution.py:293
  4.1 0.1 collective-permute-start.9
  4.1 0.7 constant_dynamic-slice_fusion
  4.9 3.1 %collective-permute-done.8.refs_3_ = bf16[16,2048]{1,0:T(8,128)(2,1)S(1)} collective-permute-done((bf16[16,2048]{1,0:T(8,128)(2,1)}, bf16[16,2048]{1,0:T(8,128)(2,1)S(1)}, u32[]{:S(2)}, u32[]{:S(2)}) %collective-permute-start.8) | collective-permute-done | bytes 65568 | tf_op jit(solution)/shard_map/ppermute | solution.py:293
  8.0 2.8 %collective-permute-done.9.refs_4_ = bf16[16,2048]{1,0:T(8,128)(2,1)S(1)} collective-permute-done((bf16[16,2048]{1,0:T(8,128)(2,1)}, bf16[16,2048]{1,0:T(8,128)(2,1)S(1)}, u32[]{:S(2)}, u32[]{:S(2)}) %collective-permute-start.9) | collective-permute-done | bytes 65568 | tf_op jit(solution)/shard_map/ppermute | solution.py:293
  10.7 0.8 copy-done.6
  11.5 0.8 copy-done.8
  12.3 0.8 copy-done.9
  13.2 0.4 join.1
  13.6 0.7 collective-permute-start.10
  14.3 6.5 %collective-permute-done.10 = bf16[2,32,2048]{2,1,0:T(8,128)(2,1)S(1)} collective-permute-done((bf16[2,32,2048]{2,1,0:T(8,128)(2,1)S(1)}, bf16[2,32,2048]{2,1,0:T(8,128)(2,1)S(1)}, u32[]{:S(2)}, u32[]{:S(2)}) %collective-permute-start.10) | collective-permute-done | bytes 262176 | tf_op jit(solution)/shard_map/ppermute | solution.py:293
  20.8 2.7 %collective-permute-start.11 = (bf16[2,64,2048]{2,1,0:T(8,128)(2,1)S(1)}, bf16[2,64,2048]{2,1,0:T(8,128)(2,1)S(1)}, u32[]{:S(2)}, u32[]{:S(2)}) collective-permute-start(bf16[2,64,2048]{2,1,0:T(8,128)(2,1)S(1)} %pad_maximum_fusion.2), channel_id=1, source_target_pairs={{0,16},{4,20},{8,24},{12,28},{16,0},{20,4},{24,8},{28,12},{1,17},{... | collective-permute-start | bytes 1572872 | tf_op jit(solution)/shard_map/ppermute | solution.py:293
  23.5 11.0 %collective-permute-done.11 = bf16[2,64,2048]{2,1,0:T(8,128)(2,1)S(1)} collective-permute-done((bf16[2,64,2048]{2,1,0:T(8,128)(2,1)S(1)}, bf16[2,64,2048]{2,1,0:T(8,128)(2,1)S(1)}, u32[]{:S(2)}, u32[]{:S(2)}) %collective-permute-start.11) | collective-permute-done | bytes 524320 | tf_op jit(solution)/shard_map/ppermute | solution.py:293
  34.5 1.1 pad_maximum_fusion.1
  35.6 1.7 %collective-permute-start.12 = (bf16[2,128,2048]{2,1,0:T(8,128)(2,1)}, bf16[2,128,2048]{2,1,0:T(8,128)(2,1)}, u32[]{:S(2)}, u32[]{:S(2)}) collective-permute-start(bf16[2,128,2048]{2,1,0:T(8,128)(2,1)} %pad_maximum_fusion.1), channel_id=1, source_target_pairs={{0,8},{4,12},{8,0},{12,4},{16,24},{20,28},{24,16},{28,20},{1,9},{5... | collective-permute-start | bytes 3145736 | tf_op jit(solution)/shard_map/ppermute | solution.py:293
  37.3 0.0 copy-done.10
  37.3 0.0 copy-done.11
  37.4 0.0 copy-done
  37.4 1.3 collective-permute-start.6
  38.6 4.6 %collective-permute-start.2 = (bf16[256,2048]{1,0:T(8,128)(2,1)S(1)}, bf16[256,2048]{1,0:T(8,128)(2,1)S(1)}, u32[]{:S(2)}, u32[]{:S(2)}) collective-permute-start(bf16[256,2048]{1,0:T(8,128)(2,1)S(1)} %bitcast.9), channel_id=1, source_target_pairs={{0,1},{1,2},{2,3},{4,5},{5,6},{6,7},{8,9},{9,10},{10,11},{12,13},{... | collective-permute-start | bytes 3145736 | tf_op jit(solution)/shard_map/ppermute | solution.py:281
  43.3 0.7 dynamic-slice_bitcast_fusion
  44.0 0.7 constant_dynamic-slice_fusion.2
  44.7 0.0 copy-done.12
  44.7 0.0 copy-start.2
  44.7 0.0 copy-start.3
  44.7 0.0 copy-start.7
  44.7 14.7 %collective-permute-done.12 = bf16[2,128,2048]{2,1,0:T(8,128)(2,1)} collective-permute-done((bf16[2,128,2048]{2,1,0:T(8,128)(2,1)}, bf16[2,128,2048]{2,1,0:T(8,128)(2,1)}, u32[]{:S(2)}, u32[]{:S(2)}) %collective-permute-start.12) | collective-permute-done | bytes 1048608 | tf_op jit(solution)/shard_map/ppermute | solution.py:293
  59.4 1.6 %pad_maximum_fusion.refs_1_ = bf16[2,256,2048]{2,1,0:T(8,128)(2,1)S(1)} fusion(bf16[2,128,2048]{2,1,0:T(8,128)(2,1)} %collective-permute-done.12, bf16[2,64,2048]{2,1,0:T(8,128)(2,1)} %copy-done.11, bf16[2,32,2048]{2,1,0:T(8,128)(2,1)} %copy-done.10, bf16[2,32,2048]{2,1,0:T(8,128)(2,1)S(1)} %join.1), kind=kLoop, calls=%fused_computation | loop fusion | flops 8388608 | bytes 4194304 | tf_op jit(solution)/shard_map/concatenate | solution.py:287
  61.0 0.0 copy-start.1
  61.0 0.1 collective-permute-start.13
  61.1 2.2 %rotate.1 = (bf16[256,2048]{1,0:T(8,128)(2,1)S(1)}, bf16[256,1536]{1,0:T(8,128)(2,1)S(1)}, bf16[256,512]{1,0:T(8,128)(2,1)S(1)}) custom-call(bf16[256,2048]{1,0:T(8,128)(2,1)S(1)} %bitcast.12, bf16[256,2048]{1,0:T(8,128)(2,1)S(1)} %bitcast.13, f32[2,256,128]{2,1,0:T(8,128)S(1)} %bitcast_add_fusion.table_ref, bf16[128,128]{1,0:T(8,128)(2,1)S(1)} %copy-done.7), custom_call_target="tpu_custom_call" | custom-call | flops 268435456 | bytes 4194304 | tf_op jit(solution)/shard_map/rotate/pallas_call | solution.py:387
  63.3 1.3 collective-permute-start.4
  64.6 4.6 %collective-permute-start = (bf16[256,512]{1,0:T(8,128)(2,1)S(1)}, bf16[256,512]{1,0:T(8,128)(2,1)S(1)}, u32[]{:S(2)}, u32[]{:S(2)}) collective-permute-start(bf16[256,512]{1,0:T(8,128)(2,1)S(1)} %get-tuple-element.23.refs_1_), channel_id=1, source_target_pairs={{0,1},{1,2},{2,3},{4,5},{5,6},{6,7},{8,9},{9,10},{10,11},{12,13},{... | collective-permute-start | bytes 786440 | tf_op jit(solution)/shard_map/ppermute | solution.py:281
  69.2 4.7 %collective-permute-done.4.refs_3_ = bf16[256,512]{1,0:T(8,128)(2,1)S(1)} collective-permute-done((bf16[256,512]{1,0:T(8,128)(2,1)S(1)}, bf16[256,512]{1,0:T(8,128)(2,1)S(1)}, u32[]{:S(2)}, u32[]{:S(2)}) %collective-permute-start.4) | collective-permute-done | bytes 262176 | tf_op jit(solution)/shard_map/ppermute | solution.py:281
  73.9 1.3 collective-permute-start.16
  75.2 0.0 collective-permute-done.refs_1_
  75.2 4.6 %collective-permute-start.14 = (bf16[256,1536]{1,0:T(8,128)(2,1)S(1)}, bf16[256,1536]{1,0:T(8,128)(2,1)S(1)}, u32[]{:S(2)}, u32[]{:S(2)}) collective-permute-start(bf16[256,1536]{1,0:T(8,128)(2,1)S(1)} %get-tuple-element.30.refs_1_), channel_id=1, source_target_pairs={{0,1},{1,2},{2,3},{4,5},{5,6},{6,7},{8,9},{9,10},{10,11},{12,13},{... | collective-permute-start | bytes 2359304 | tf_op jit(solution)/shard_map/ppermute | solution.py:281
  79.8 0.0 collective-permute-done.6.refs_4_
  79.8 1.3 collective-permute-start.7
  81.1 0.0 collective-permute-done.2.refs_2_
  81.2 4.6 %collective-permute-start.3 = (bf16[256,2048]{1,0:T(8,128)(2,1)S(1)}, bf16[256,2048]{1,0:T(8,128)(2,1)S(1)}, u32[]{:S(2)}, u32[]{:S(2)}) collective-permute-start(bf16[256,2048]{1,0:T(8,128)(2,1)S(1)} %collective-permute-done.2.refs_2_), channel_id=1, source_target_pairs={{0,1},{1,2},{2,3},{4,5},{5,6},{6,7},{8,9},{9,10},{10,11},{12,13},{... | collective-permute-start | bytes 3145736 | tf_op jit(solution)/shard_map/ppermute | solution.py:281
  85.8 10.5 %collective-permute-done.16.refs_3_ = bf16[256,1536]{1,0:T(8,128)(2,1)S(1)} collective-permute-done((bf16[256,1536]{1,0:T(8,128)(2,1)S(1)}, bf16[256,1536]{1,0:T(8,128)(2,1)S(1)}, u32[]{:S(2)}, u32[]{:S(2)}) %collective-permute-start.16) | collective-permute-done | bytes 786464 | tf_op jit(solution)/shard_map/ppermute | solution.py:281
  96.2 1.3 collective-permute-start.17
  97.5 0.2 collective-permute-done.14.refs_1_
  97.7 4.4 %collective-permute-start.15 = (bf16[256,1536]{1,0:T(8,128)(2,1)S(1)}, bf16[256,1536]{1,0:T(8,128)(2,1)S(1)}, u32[]{:S(2)}, u32[]{:S(2)}) collective-permute-start(bf16[256,1536]{1,0:T(8,128)(2,1)S(1)} %collective-permute-done.14.refs_1_), channel_id=1, source_target_pairs={{0,1},{1,2},{2,3},{4,5},{5,6},{6,7},{8,9},{9,10},{10,11},{12,13},{... | collective-permute-start | bytes 2359304 | tf_op jit(solution)/shard_map/ppermute | solution.py:281
  102.1 0.8 shard_map.190
  103.0 2.5 %shard_map.193 = (f32[12,128,256]{2,1,0:T(8,128)S(1)}, f32[12,2,256]{2,1,0:T(2,128)S(1)}) custom-call(bf16[256,2048]{1,0:T(8,128)(2,1)S(1)} %get-tuple-element.22.refs_0_, bf16[256,1536]{1,0:T(8,128)(2,1)S(1)} %get-tuple-element.30.refs_1_, bf16[256,2048]{1,0:T(8,128)(2,1)S(1)} %bitcast.11, f32[1,64,128]{2,1,0:T(8,128)S(1)} %copy-done.1), custom_call_target="tpu_custom_call" | custom-call | flops 402653184 | bytes 4718592 | tf_op jit(solution)/shard_map/pallas_call | solution.py:260
  105.5 29.2 %collective-permute-done.17.refs_3_ = bf16[256,1536]{1,0:T(8,128)(2,1)S(1)} collective-permute-done((bf16[256,1536]{1,0:T(8,128)(2,1)S(1)}, bf16[256,1536]{1,0:T(8,128)(2,1)S(1)}, u32[]{:S(2)}, u32[]{:S(2)}) %collective-permute-start.17) | collective-permute-done | bytes 786464 | tf_op jit(solution)/shard_map/ppermute | solution.py:281
  134.7 1.3 collective-permute-start.5
  136.0 0.0 collective-permute-done.13.refs_2_
  136.0 4.6 %collective-permute-start.1 = (bf16[256,512]{1,0:T(8,128)(2,1)S(1)}, bf16[256,512]{1,0:T(8,128)(2,1)S(1)}, u32[]{:S(2)}, u32[]{:S(2)}) collective-permute-start(bf16[256,512]{1,0:T(8,128)(2,1)S(1)} %collective-permute-done.refs_1_), channel_id=1, source_target_pairs={{0,1},{1,2},{2,3},{4,5},{5,6},{6,7},{8,9},{9,10},{10,11},{12,13},{... | collective-permute-start | bytes 786440 | tf_op jit(solution)/shard_map/ppermute | solution.py:281
  140.6 0.9 shard_map.191
  141.5 2.7 %shard_map.194 = (f32[12,128,256]{2,1,0:T(8,128)S(1)}, f32[12,2,256]{2,1,0:T(2,128)S(1)}) custom-call(bf16[256,2048]{1,0:T(8,128)(2,1)S(1)} %get-tuple-element.22.refs_0_, bf16[256,1536]{1,0:T(8,128)(2,1)S(1)} %collective-permute-done.14.refs_1_, bf16[256,2048]{1,0:T(8,128)(2,1)S(1)} %collective-permute-done.2.refs_2_, ...), custom_call_target="tpu_custom_call", output_to_operand_aliasing={{0}: (7, {}), {1}: (8, {})} | custom-call | flops 805306368 | bytes 6291456 | tf_op jit(solution)/shard_map/pallas_call | solution.py:260
  144.2 1.2 shard_map.192
  145.4 0.0 copy-start.4
  145.4 0.0 copy-start.5
  145.4 3.7 %shard_map.195 = (f32[12,128,256]{2,1,0:T(8,128)S(1)}, f32[12,2,256]{2,1,0:T(2,128)S(1)}) custom-call(bf16[256,2048]{1,0:T(8,128)(2,1)S(1)} %get-tuple-element.22.refs_0_, bf16[2,256,2048]{2,1,0:T(8,128)(2,1)S(1)} %pad_maximum_fusion.refs_1_, ...), custom_call_target="tpu_custom_call", output_to_operand_aliasing={{0}: (3, {}), {1}: (4, {})} | custom-call | flops 805306368 | bytes 6291456 | tf_op jit(solution)/shard_map/pallas_call | solution.py:260
  149.1 0.0 collective-permute-done.15.refs_1_
  149.1 0.0 collective-permute-done.7.refs_4_
  149.1 0.0 collective-permute-done.3.refs_2_
  149.1 3.6 %shard_map.196 = (bf16[256,2048]{1,0:T(8,128)(2,1)}, f32[12,128,256]{2,1,0:T(8,128)S(1)}, f32[12,2,256]{2,1,0:T(2,128)S(1)}) custom-call(bf16[256,2048]{1,0:T(8,128)(2,1)S(1)} %get-tuple-element.22.refs_0_, bf16[256,1536]{1,0:T(8,128)(2,1)S(1)} %collective-permute-done.15.refs_1_, ...), custom_call_target="tpu_custom_call", output_to_operand_aliasing={{1}: (7, {}), {2}: (8, {})} | custom-call | flops 805306368 | bytes 6291456 | tf_op jit(solution)/shard_map/pallas_call | solution.py:260
  152.7 0.0 collective-permute-done.5.refs_3_
  152.7 0.0 collective-permute-done.1.refs_1_
  152.7 1.6 %shard_map.197 = (bf16[256,2048]{1,0:T(8,128)(2,1)}, f32[4,128,256]{2,1,0:T(8,128)S(1)}, f32[4,2,256]{2,1,0:T(2,128)S(1)}) custom-call(bf16[256,2048]{1,0:T(8,128)(2,1)S(1)} %get-tuple-element.22.refs_0_, bf16[256,512]{1,0:T(8,128)(2,1)S(1)} %collective-permute-done.1.refs_1_, ...), custom_call_target="tpu_custom_call", output_to_operand_aliasing={{1}: (7, {}), {2}: (8, {}), {0}: (9, {})} | custom-call | flops 268435456 | bytes 2097152 | tf_op jit(solution)/shard_map/pallas_call | solution.py:260
  (16 shorter events, 0.1 us)
Async XLA Ops:
  0.0 37.4 %copy-start = (bf16[1,4,64,2048]{3,2,1,0:T(8,128)(2,1)S(1)}, bf16[1,4,64,2048]{3,2,1,0:T(8,128)(2,1)}, u32[]{:S(2)}) copy-start(bf16[1,4,64,2048]{3,2,1,0:T(8,128)(2,1)} %param.22) | copy-start | bytes 3145732
  0.0 8.0 %collective-permute-start.8 = (bf16[16,2048]{1,0:T(8,128)(2,1)}, bf16[16,2048]{1,0:T(8,128)(2,1)S(1)}, u32[]{:S(2)}, u32[]{:S(2)}) collective-permute-start(bf16[16,2048]{1,0:T(8,128)(2,1)} %refs_0_.1), channel_id=1, source_target_pairs={{0,2},{1,3},{2,0},{3,1},{4,6},{5,7},{6,4},{7,5},{8,10},{9,11},{10,... | collective-permute-start | bytes 196616 | tf_op jit(solution)/shard_map/ppermute | solution.py:293
  4.1 6.7 %collective-permute-start.9 = (bf16[16,2048]{1,0:T(8,128)(2,1)}, bf16[16,2048]{1,0:T(8,128)(2,1)S(1)}, u32[]{:S(2)}, u32[]{:S(2)}) collective-permute-start(bf16[16,2048]{1,0:T(8,128)(2,1)} %refs_1_.1), channel_id=1, source_target_pairs={{0,2},{1,3},{2,0},{3,1},{4,6},{5,7},{6,4},{7,5},{8,10},{9,11},{10,... | collective-permute-start | bytes 196616 | tf_op jit(solution)/shard_map/ppermute | solution.py:293
  10.7 0.8 copy-start.6
  11.5 0.8 copy-start.8
  12.3 0.8 copy-start.9
  13.2 31.5 %copy-start.12 = (f32[2,64,128]{2,1,0:T(8,128)S(1)}, f32[2,64,128]{2,1,0:T(8,128)}, u32[]{:S(2)}) copy-start(f32[2,64,128]{2,1,0:T(8,128)} %constant.44.clone) | copy-start | bytes 196612
  13.6 7.2 %collective-permute-start.10 = (bf16[2,32,2048]{2,1,0:T(8,128)(2,1)S(1)}, bf16[2,32,2048]{2,1,0:T(8,128)(2,1)S(1)}, u32[]{:S(2)}, u32[]{:S(2)}) collective-permute-start(bf16[2,32,2048]{2,1,0:T(8,128)(2,1)S(1)} %join.1), channel_id=1, source_target_pairs={{0,1},{1,0},{2,3},{3,2},{4,5},{5,4},{6,7},{7,6},{8,9},{9,8},{10,11... | collective-permute-start | bytes 786440 | tf_op jit(solution)/shard_map/ppermute | solution.py:293
  20.8 16.6 %copy-start.10 = (bf16[2,32,2048]{2,1,0:T(8,128)(2,1)}, bf16[2,32,2048]{2,1,0:T(8,128)(2,1)S(1)}, u32[]{:S(2)}) copy-start(bf16[2,32,2048]{2,1,0:T(8,128)(2,1)S(1)} %collective-permute-done.10) | copy-start | bytes 786436
  20.8 13.7 %collective-permute-start.11 = (bf16[2,64,2048]{2,1,0:T(8,128)(2,1)S(1)}, bf16[2,64,2048]{2,1,0:T(8,128)(2,1)S(1)}, u32[]{:S(2)}, u32[]{:S(2)}) collective-permute-start(bf16[2,64,2048]{2,1,0:T(8,128)(2,1)S(1)} %pad_maximum_fusion.2), channel_id=1, source_target_pairs={{0,16},{4,20},{8,24},{12,28},{16,0},{20,4},{24,8},{28,12},{1,17},{... | collective-permute-start | bytes 1572872 | tf_op jit(solution)/shard_map/ppermute | solution.py:293
  34.5 2.8 %copy-start.11 = (bf16[2,64,2048]{2,1,0:T(8,128)(2,1)}, bf16[2,64,2048]{2,1,0:T(8,128)(2,1)S(1)}, u32[]{:S(2)}) copy-start(bf16[2,64,2048]{2,1,0:T(8,128)(2,1)S(1)} %collective-permute-done.11) | copy-start | bytes 1572868
  35.6 23.8 %collective-permute-start.12 = (bf16[2,128,2048]{2,1,0:T(8,128)(2,1)}, bf16[2,128,2048]{2,1,0:T(8,128)(2,1)}, u32[]{:S(2)}, u32[]{:S(2)}) collective-permute-start(bf16[2,128,2048]{2,1,0:T(8,128)(2,1)} %pad_maximum_fusion.1), channel_id=1, source_target_pairs={{0,8},{4,12},{8,0},{12,4},{16,24},{20,28},{24,16},{28,20},{1,9},{5... | collective-permute-start | bytes 3145736 | tf_op jit(solution)/shard_map/ppermute | solution.py:293
  37.4 42.5 %collective-permute-start.6 = (bf16[256,2048]{1,0:T(8,128)(2,1)S(1)}, bf16[256,2048]{1,0:T(8,128)(2,1)S(1)}, u32[]{:S(2)}, u32[]{:S(2)}) collective-permute-start(bf16[256,2048]{1,0:T(8,128)(2,1)S(1)} %bitcast.8), channel_id=1, source_target_pairs={{1,0},{2,1},{3,2},{5,4},{6,5},{7,6},{9,8},{10,9},{11,10},{13,12},{... | collective-permute-start | bytes 3145736 | tf_op jit(solution)/shard_map/ppermute | solution.py:281
  38.6 42.5 %collective-permute-start.2 = (bf16[256,2048]{1,0:T(8,128)(2,1)S(1)}, bf16[256,2048]{1,0:T(8,128)(2,1)S(1)}, u32[]{:S(2)}, u32[]{:S(2)}) collective-permute-start(bf16[256,2048]{1,0:T(8,128)(2,1)S(1)} %bitcast.9), channel_id=1, source_target_pairs={{0,1},{1,2},{2,3},{4,5},{5,6},{6,7},{8,9},{9,10},{10,11},{12,13},{... | collective-permute-start | bytes 3145736 | tf_op jit(solution)/shard_map/ppermute | solution.py:281
  44.7 16.4 %copy-start.2 = (bf16[1,4,64,2048]{3,2,1,0:T(8,128)(2,1)S(1)}, bf16[1,4,64,2048]{3,2,1,0:T(8,128)(2,1)}, u32[]{:S(2)}) copy-start(bf16[1,4,64,2048]{3,2,1,0:T(8,128)(2,1)} %param.20) | copy-start | bytes 3145732
  44.7 16.4 %copy-start.3 = (bf16[1,4,64,2048]{3,2,1,0:T(8,128)(2,1)S(1)}, bf16[1,4,64,2048]{3,2,1,0:T(8,128)(2,1)}, u32[]{:S(2)}) copy-start(bf16[1,4,64,2048]{3,2,1,0:T(8,128)(2,1)} %param.21) | copy-start | bytes 3145732
  44.7 16.4 %copy-start.7 = (bf16[128,128]{1,0:T(8,128)(2,1)S(1)}, bf16[128,128]{1,0:T(8,128)(2,1)}, u32[]{:S(2)}) copy-start(bf16[128,128]{1,0:T(8,128)(2,1)} %constant.40.clone.partners_ref.refs_6_) | copy-start | bytes 98308
  61.0 41.2 %copy-start.1 = (f32[1,64,128]{2,1,0:T(8,128)S(1)}, f32[1,64,128]{2,1,0:T(8,128)}, u32[]{:S(2)}) copy-start(f32[1,64,128]{2,1,0:T(8,128)} %constant.45.clone.refs_3_.refs_5_.refs_6_) | copy-start | bytes 98308
  61.0 75.0 %collective-permute-start.13 = (bf16[2,256,2048]{2,1,0:T(8,128)(2,1)S(1)}, bf16[2,256,2048]{2,1,0:T(8,128)(2,1)S(1)}, u32[]{:S(2)}, u32[]{:S(2)}) collective-permute-start(bf16[2,256,2048]{2,1,0:T(8,128)(2,1)S(1)} %pad_maximum_fusion.refs_1_), channel_id=1, source_target_pairs={{0,4},{4,0},{8,12},{12,8},{16,20},{20,16},{24,28},{28,24},{1,5},{5... | collective-permute-start | bytes 6291464 | tf_op jit(solution)/shard_map/ppermute | solution.py:293
  63.3 10.6 %collective-permute-start.4 = (bf16[256,512]{1,0:T(8,128)(2,1)S(1)}, bf16[256,512]{1,0:T(8,128)(2,1)S(1)}, u32[]{:S(2)}, u32[]{:S(2)}) collective-permute-start(bf16[256,512]{1,0:T(8,128)(2,1)S(1)} %get-tuple-element.23.refs_1_), channel_id=1, source_target_pairs={{1,0},{2,1},{3,2},{5,4},{6,5},{7,6},{9,8},{10,9},{11,10},{13,12},{... | collective-permute-start | bytes 786440 | tf_op jit(solution)/shard_map/ppermute | solution.py:281
  64.6 10.6 %collective-permute-start = (bf16[256,512]{1,0:T(8,128)(2,1)S(1)}, bf16[256,512]{1,0:T(8,128)(2,1)S(1)}, u32[]{:S(2)}, u32[]{:S(2)}) collective-permute-start(bf16[256,512]{1,0:T(8,128)(2,1)S(1)} %get-tuple-element.23.refs_1_), channel_id=1, source_target_pairs={{0,1},{1,2},{2,3},{4,5},{5,6},{6,7},{8,9},{9,10},{10,11},{12,13},{... | collective-permute-start | bytes 786440 | tf_op jit(solution)/shard_map/ppermute | solution.py:281
  73.9 22.3 %collective-permute-start.16 = (bf16[256,1536]{1,0:T(8,128)(2,1)S(1)}, bf16[256,1536]{1,0:T(8,128)(2,1)S(1)}, u32[]{:S(2)}, u32[]{:S(2)}) collective-permute-start(bf16[256,1536]{1,0:T(8,128)(2,1)S(1)} %get-tuple-element.30.refs_1_), channel_id=1, source_target_pairs={{1,0},{2,1},{3,2},{5,4},{6,5},{7,6},{9,8},{10,9},{11,10},{13,12},{... | collective-permute-start | bytes 2359304 | tf_op jit(solution)/shard_map/ppermute | solution.py:281
  75.2 22.5 %collective-permute-start.14 = (bf16[256,1536]{1,0:T(8,128)(2,1)S(1)}, bf16[256,1536]{1,0:T(8,128)(2,1)S(1)}, u32[]{:S(2)}, u32[]{:S(2)}) collective-permute-start(bf16[256,1536]{1,0:T(8,128)(2,1)S(1)} %get-tuple-element.30.refs_1_), channel_id=1, source_target_pairs={{0,1},{1,2},{2,3},{4,5},{5,6},{6,7},{8,9},{9,10},{10,11},{12,13},{... | collective-permute-start | bytes 2359304 | tf_op jit(solution)/shard_map/ppermute | solution.py:281
  79.8 69.2 %collective-permute-start.7 = (bf16[256,2048]{1,0:T(8,128)(2,1)S(1)}, bf16[256,2048]{1,0:T(8,128)(2,1)S(1)}, u32[]{:S(2)}, u32[]{:S(2)}) collective-permute-start(bf16[256,2048]{1,0:T(8,128)(2,1)S(1)} %collective-permute-done.6.refs_4_), channel_id=1, source_target_pairs={{1,0},{2,1},{3,2},{5,4},{6,5},{7,6},{9,8},{10,9},{11,10},{13,12},{... | collective-permute-start | bytes 3145736 | tf_op jit(solution)/shard_map/ppermute | solution.py:281
  81.2 67.9 %collective-permute-start.3 = (bf16[256,2048]{1,0:T(8,128)(2,1)S(1)}, bf16[256,2048]{1,0:T(8,128)(2,1)S(1)}, u32[]{:S(2)}, u32[]{:S(2)}) collective-permute-start(bf16[256,2048]{1,0:T(8,128)(2,1)S(1)} %collective-permute-done.2.refs_2_), channel_id=1, source_target_pairs={{0,1},{1,2},{2,3},{4,5},{5,6},{6,7},{8,9},{9,10},{10,11},{12,13},{... | collective-permute-start | bytes 3145736 | tf_op jit(solution)/shard_map/ppermute | solution.py:281
  96.2 38.5 %collective-permute-start.17 = (bf16[256,1536]{1,0:T(8,128)(2,1)S(1)}, bf16[256,1536]{1,0:T(8,128)(2,1)S(1)}, u32[]{:S(2)}, u32[]{:S(2)}) collective-permute-start(bf16[256,1536]{1,0:T(8,128)(2,1)S(1)} %collective-permute-done.16.refs_3_), channel_id=1, source_target_pairs={{1,0},{2,1},{3,2},{5,4},{6,5},{7,6},{9,8},{10,9},{11,10},{13,12},{... | collective-permute-start | bytes 2359304 | tf_op jit(solution)/shard_map/ppermute | solution.py:281
  97.7 51.4 %collective-permute-start.15 = (bf16[256,1536]{1,0:T(8,128)(2,1)S(1)}, bf16[256,1536]{1,0:T(8,128)(2,1)S(1)}, u32[]{:S(2)}, u32[]{:S(2)}) collective-permute-start(bf16[256,1536]{1,0:T(8,128)(2,1)S(1)} %collective-permute-done.14.refs_1_), channel_id=1, source_target_pairs={{0,1},{1,2},{2,3},{4,5},{5,6},{6,7},{8,9},{9,10},{10,11},{12,13},{... | collective-permute-start | bytes 2359304 | tf_op jit(solution)/shard_map/ppermute | solution.py:281
  134.7 18.0 %collective-permute-start.5 = (bf16[256,512]{1,0:T(8,128)(2,1)S(1)}, bf16[256,512]{1,0:T(8,128)(2,1)S(1)}, u32[]{:S(2)}, u32[]{:S(2)}) collective-permute-start(bf16[256,512]{1,0:T(8,128)(2,1)S(1)} %collective-permute-done.4.refs_3_), channel_id=1, source_target_pairs={{1,0},{2,1},{3,2},{5,4},{6,5},{7,6},{9,8},{10,9},{11,10},{13,12},{... | collective-permute-start | bytes 786440 | tf_op jit(solution)/shard_map/ppermute | solution.py:281
  136.0 16.7 %collective-permute-start.1 = (bf16[256,512]{1,0:T(8,128)(2,1)S(1)}, bf16[256,512]{1,0:T(8,128)(2,1)S(1)}, u32[]{:S(2)}, u32[]{:S(2)}) collective-permute-start(bf16[256,512]{1,0:T(8,128)(2,1)S(1)} %collective-permute-done.refs_1_), channel_id=1, source_target_pairs={{0,1},{1,2},{2,3},{4,5},{5,6},{6,7},{8,9},{9,10},{10,11},{12,13},{... | collective-permute-start | bytes 786440 | tf_op jit(solution)/shard_map/ppermute | solution.py:281
  145.4 3.8 %copy-start.4 = (f32[2,64,128]{2,1,0:T(8,128)S(1)}, f32[2,64,128]{2,1,0:T(8,128)}, u32[]{:S(2)}) copy-start(f32[2,64,128]{2,1,0:T(8,128)} %constant.47.clone.refs_6_) | copy-start | bytes 196612
  145.4 3.7 %copy-start.5 = (f32[2,64,128]{2,1,0:T(8,128)S(1)}, f32[2,64,128]{2,1,0:T(8,128)}, u32[]{:S(2)}) copy-start(f32[2,64,128]{2,1,0:T(8,128)} %constant.46.clone.refs_5_) | copy-start | bytes 196612

commit v3 on v2

--- a/solution.py
+++ b/solution.py
@@ -70,25 +70,30 @@
         out_ref[1, here] = values_ref[...]
 
 
-def rotate_kernel(chunks, group, q_ref, k_ref, table_ref, partners_ref, qo_ref, *ko_refs):
-    unit = pl.program_id(0)
-
-    def turn(source, start):
+def rotate_kernel(chunks, q_ref, k_ref, table_ref, partners_ref, qo_ref, lent_ref, *ko_refs):
+    def turn(source, head):
         return rotated(
-            source[:, pl.ds(start, HD)], partners_ref[...], table_ref[0], table_ref[1]
+            source[:, pl.ds(head * HD, HD)], partners_ref[...], table_ref[0], table_ref[1]
         )
 
-    for head in range(group):
-        qo_ref[:, pl.ds(pl.multiple_of((unit * group + head) * HD, HD), HD)] = turn(
-            q_ref, head * HD
-        )
-    for (first, count), ko_ref in zip(chunks, ko_refs):
-
-        @pl.when((unit * group >= first) & (unit * group < first + count))
-        def _(first=first, ko_ref=ko_ref):
-            for head in range(group):
-                start = pl.multiple_of((unit * group - first + head) * HD, HD)
-                ko_ref[:, pl.ds(start, HD)] = turn(k_ref, head * HD)
+    for (first, count, _), ko_ref in zip(chunks, ko_refs):
+        for head in range(count):
+            ko_ref[:, pl.ds(head * HD, HD)] = turn(k_ref, first + head)
+    for head in range(q_ref.shape[1] // HD):
+        qo_ref[:, pl.ds(head * HD, HD)] = turn(q_ref, head)
+    lent_ref[...] = qo_ref[:, pl.ds(chunks[-1][0] * HD, chunks[-1][1] * HD)]
+
+
+def head_chunks(heads):
+    unit = heads // 8
+    if heads % 8:
+        return ((0, heads, 1),)
+    counts, groups = (6 * unit, 2 * unit), (6 * unit, 2 * unit)
+    chunks, first = [], 0
+    for count, group in zip(counts, groups):
+        chunks.append((first, count, group))
+        first += count
+    return tuple(chunks)
 
 
 def mask_tiles(rows, cols, row_shift, lanes):
@@ -112,7 +117,7 @@
     return np.where(np.stack(tiles), 0.0, NEG).astype(np.float32), tuple(plan)
 
 
-def attend_kernel(stages, first, last, group, lanes, *refs):
+def attend_kernel(stages, first, last, group, lanes, merge, share, *refs):
     refs = list(refs)
     q_ref = refs.pop(0)
 
@@ -126,11 +131,16 @@
     masks = [[refs.pop(0) if b.plan else None for b in blocks] for _, blocks in stages]
     if not first:
         acc_in, ml_in = refs.pop(0), refs.pop(0)
+    if merge is not None:
+        part_ref, part_ml_ref = refs.pop(0), refs.pop(0)
     if last is not None:
         if last:
             refs.pop(0)
         out_ref = refs.pop(0)
-    acc_ref, ml_ref = refs
+    if share:
+        share_ref, ml_ref, acc_ref = refs
+    else:
+        acc_ref, ml_ref = refs
     tokens = q_ref.shape[0]
     unit = pl.program_id(0)
 
@@ -202,9 +212,25 @@
         if flag is None:
             step()
         else:
-            there = lax.axis_index("row") + flag
-            pl.when((there >= 0) & (there < lax.axis_size("row")))(step)
-        have = True
+            pl.when(flag(lax.axis_index("row"), lax.axis_size("row")))(step)
+        have = not share
+    if merge is not None:
+
+        @pl.when(merge(lax.axis_index("row"), lax.axis_size("row")))
+        def _():
+            for head in range(group):
+                at = unit * group + head
+                top, met = ml_ref[at, 0:1], part_ml_ref[at, 0:1]
+                peak = jnp.maximum(top, met)
+                ours = jnp.exp2((top - peak) * EXP_SCALE)
+                theirs = jnp.exp2((met - peak) * EXP_SCALE) * part_ml_ref[at, 1:2]
+                ml_ref[at, 1:2] = ml_ref[at, 1:2] * ours + theirs
+                acc_ref[at] = acc_ref[at] * ours + part_ref[at].astype(jnp.float32) * theirs
+
+    if share:
+        for head in range(group):
+            at = unit * group + head
+            share_ref[at] = (acc_ref[at] * (1.0 / ml_ref[at, 1:2])).astype(share_ref.dtype)
     if last is not None:
         for head in range(group):
             at = unit * group + head
@@ -230,7 +256,7 @@
     return pltpu.with_memory_space_constraint(x, pltpu.VMEM)
 
 
-def attend(q, state, sources, stages, tiles, heads, group, out=None, last=False):
+def attend(q, state, sources, stages, tiles, heads, group, out=None, last=False, merge=None, part=(), share=False):
     tokens, width = q.shape
     lanes = 128 if tokens % 128 == 0 else tokens
     first_head = stages[0][1][0].head
@@ -241,12 +267,20 @@
     if state is not None:
         aliases = {len(operands) + i: i + last for i in range(2)}
         operands += [resident(a) for a in state]
+    operands += [resident(a) for a in part]
     specs = [whole] * len(operands)
     out_shape = [
         pltpu.VMEM((heads, HD, tokens), jnp.float32),
         pltpu.VMEM((heads, 2, tokens), jnp.float32),
     ]
     out_specs = [whole] * 2
+    scratch = []
+    if share:
+        out_shape = [
+            jax.ShapeDtypeStruct((heads, HD, tokens), jnp.bfloat16),
+            jax.ShapeDtypeStruct((heads, 2, tokens), jnp.float32),
+        ]
+        scratch = [pltpu.VMEM((heads, HD, tokens), jnp.float32)]
     if last:
         out_shape.insert(0, jax.ShapeDtypeStruct((tokens, width), jnp.bfloat16))
         out_specs.insert(
@@ -259,12 +293,14 @@
     keys_seen = sum(source[0].shape[-2] for source in sources)
     return pl.pallas_call(
         functools.partial(
-            attend_kernel, stages, state is None, (out is not None) if last else None, group, lanes
+            attend_kernel, stages, state is None, (out is not None) if last else None, group, lanes,
+            merge, share,
         ),
         out_shape=out_shape,
         grid=(heads // group,),
         in_specs=specs,
         out_specs=out_specs,
+        scratch_shapes=scratch,
         input_output_aliases=aliases,
         compiler_params=pltpu.CompilerParams(vmem_limit_bytes=KERNEL_VMEM),
         cost_estimate=pl.CostEstimate(
@@ -275,9 +311,14 @@
     )(*operands)
 
 
-def passed_along(x, axis, by):
+def passed_along(x, axis, by, distance, edges=True):
     length = lax.axis_size(axis)
-    pairs = [(i, i + by) for i in range(length) if 0 <= i + by < length]
+    ends = (-1, length) if edges else (0, length - 1)
+    pairs = [
+        (i, i + by)
+        for i in range(length)
+        if ends[0] < i + by < ends[1] and 0 <= i + by - by * distance < length
+    ]
     return lax.ppermute(x, axis, pairs)
 
 
@@ -314,9 +355,7 @@
     view_index = lax.axis_index("view")
     ctok_dev = cond_keys.shape[0]
     ctok = ctok_dev * view_count * row_count
-    group = 4 if heads % 4 == 0 else 1
-    last_heads = group if heads > group else 0
-    chunks = [(0, heads - last_heads)] + [(heads - last_heads, last_heads)] * (last_heads > 0)
+    chunks = head_chunks(heads)
 
     partners = jnp.asarray(partner_matrix(), jnp.bfloat16)
     view_table = axis_table(0, view_count * view_dev + 1)
@@ -360,69 +399,111 @@
     for v in range(view_dev):
         values = target_values[v].reshape(tokens, width)
         whole = pl.BlockSpec(memory_space=pltpu.VMEM)
-        lane_block = pl.BlockSpec((tokens, group * HD), lambda g: (0, g))
         rotate = pl.pallas_call(
-            functools.partial(rotate_kernel, chunks, group),
+            functools.partial(rotate_kernel, chunks),
             out_shape=[
                 pltpu.VMEM((tokens, width), jnp.bfloat16),
+                jax.ShapeDtypeStruct((tokens, chunks[-1][1] * HD), jnp.bfloat16),
                 *(
                     jax.ShapeDtypeStruct((tokens, count * HD), jnp.bfloat16)
-                    for _, count in chunks
+                    for _, count, _ in chunks
                 ),
             ],
-            grid=(heads // group,),
-            in_specs=[
-                lane_block,
-                lane_block,
-                pl.BlockSpec((2, tokens, HD), lambda g: (0, 0, 0)),
-                pl.BlockSpec((HD, HD), lambda g: (0, 0)),
-            ],
-            out_specs=[whole] * (1 + len(chunks)),
+            in_specs=[whole] * 4,
+            out_specs=[whole] * (2 + len(chunks)),
             compiler_params=pltpu.CompilerParams(vmem_limit_bytes=KERNEL_VMEM),
             cost_estimate=pl.CostEstimate(
                 flops=4 * tokens * width * HD, bytes_accessed=8 * tokens * width, transcendentals=0
             ),
             name="rotate",
         )
-        q_rot, *k_rot = rotate(
-            queries[v].reshape(tokens, width),
-            target_keys[v].reshape(tokens, width),
-            tables[:, v : v + 1] + in_view,
-            partners,
+        q_rot, q_lent, *k_rot = rotate(
+            resident(queries[v].reshape(tokens, width)),
+            resident(target_keys[v].reshape(tokens, width)),
+            resident(tables[:, v : v + 1] + in_view),
+            resident(partners),
         )
 
-        travels = {"values": values} | {f"keys{c}": k for c, k in enumerate(k_rot)}
+        lend = row_count >= 4 and reach == 2 and len(chunks) > 1
+        lent = len(chunks) - 1
         met = {}
-        for what, block in travels.items():
+
+        def travel(what, block, near_only=False):
+            met[what, 0] = block
             above = below = block
-            for d in range(1, reach + 1):
-                above = passed_along(above, "row", 1)
-                below = passed_along(below, "row", -1)
+            for d in range(1, 2 if near_only else reach + 1):
+                edges = not (lend and d == reach and what in (f"keys{lent}", f"values{lent}"))
+                above = passed_along(above, "row", 1, d, edges)
+                below = passed_along(below, "row", -1, d, edges)
                 met[what, -d], met[what, d] = above, below
-            met[what, 0] = block
+
+        for c, keys in enumerate(k_rot):
+            travel(f"keys{c}", keys)
+        if lend:
+            travel("values", values, near_only=True)
+            for c, (first, count, _) in enumerate(chunks):
+                span = slice(first * HD, (first + count) * HD)
+                for sign, by in ((-1, 1), (1, -1)):
+                    edges = c != lent
+                    met[f"values{c}", 2 * sign] = passed_along(
+                        met["values", sign][:, span], "row", by, 2, edges
+                    )
+        else:
+            travel("values", values)
+
+        def block_of(c, d, shift=None):
+            first = chunks[c][0]
+            tiles, plan = mask_tiles(rows_dev, cols, (d if shift is None else shift) * rows_dev, lanes)
+            split = (f"values{c}", d) in met
+            pair = met[f"keys{c}", d], met[f"values{c}" if split else "values", d]
+            return pair, Block(plan, first, first, first if split else 0, cols), tiles
+
+        def within(d):
+            return lambda index, size: (index + d >= 0) & (index + d < size)
+
+        part = ()
+        if lend:
+            first, count, group = chunks[lent]
+            last_row = row_count - 1
+            asked = lax.ppermute(q_lent, "row", [(0, 1), (last_row, last_row - 1)])
+            pairs, blocks, tiles = zip(block_of(lent, 1, 2), block_of(lent, -1, -2))
+            blocks = [b._replace(head=0, keys_head=0, values_head=-first) for b in blocks]
+            stages = [
+                (lambda index, size: index == 1, (blocks[0],)),
+                (lambda index, size: index == size - 2, (blocks[1],)),
+            ]
+            quotients, totals = attend(asked, None, pairs, stages, tiles, count, group, share=True)
+            back = [(1, 0), (last_row - 1, last_row)]
+            part = (lax.ppermute(quotients, "row", back),)
+            part += (lax.ppermute(totals, "row", back),)
 
         out = None
-        for c, (first, count) in enumerate(chunks):
-
-            def stage_of(d):
-                tiles, plan = mask_tiles(rows_dev, cols, d * rows_dev, lanes)
-                block = Block(plan, first, first, 0, cols)
-                return (met[f"keys{c}", d], met["values", d]), (d or None, (block,)), tiles
-
-            def run(state, picked, **more):
-                sources, stages, tiles = zip(*map(stage_of, picked))
-                return attend(q_rot, state, sources, stages, tiles, count, group, **more)
-
-            state = run(None, [0])
+        for c, (first, count, group) in enumerate(chunks):
+
+            def run(state, picked, flags, **more):
+                pairs, blocks, tiles = zip(*(block_of(c, d) for d in picked))
+                stages = [(flag, (block,)) for flag, block in zip(flags, blocks)]
+                return attend(q_rot, state, pairs, stages, tiles, count, group, **more)
+
+            state = run(None, [0], [None])
             near = [d for far in range(1, reach) for d in (-far, far)]
             if near:
-                state = run(state, near)
+                state = run(state, near, [within(d) for d in near])
             block = Block((), first, 0, 0, cols, True)
             state = attend(
                 q_rot, state, [(x,) for x in cond_held],
                 [(None, (block,) * len(cond_held))], [], count, group,
             )
-            out, *_ = run(state, [-reach, reach], out=out, last=True)
+            flags, more = [within(-reach), within(reach)], {}
+            if lend and c == lent:
+                flags = [
+                    lambda index, size: (index >= reach) & (index < size - 1),
+                    lambda index, size: (index > 0) & (index < size - reach),
+                ]
+                more = dict(
+                    merge=lambda index, size: (index == 0) | (index == size - 1), part=part
+                )
+            out, *_ = run(state, [-reach, reach], flags, out=out, last=True, **more)
         outputs.append(out.reshape(rows_dev, cols, width))
     return jnp.stack(outputs) if view_dev > 1 else outputs[0][None]
 

time: 157 us -> 161 us (1.025)
  waiting for transfers between devices: 82.7 us -> 97.3 us
  starting transfers between devices: 44.4 us -> 38.9 us
  Pallas kernels: 19.6 us -> 15.7 us
    ppermute x0 -> x3, waiting for transfers between devices: none -> 16.4 us  [the longest x1 11.5 us: local(): part += (lax.ppermute(totals, 'row', back),)]
    ppermute x12 -> x14, starting transfers between devices: 35.1 us -> 24.1 us  [passed_along(): return lax.ppermute(x, axis, pairs)]
    ppermute x0 -> x3, starting transfers between devices: none -> 5.51 us  [the longest x1 2.94 us: local(): asked = lax.ppermute(q_lent, 'row', [(0, 1), (last_row, last_row - 1)])]
    pallas_call x8 -> x9, Pallas kernels: 17 us -> 14.3 us  [attend(): pl.pallas_call(functools.partial(attend_kernel, stages, state is None, ou...]
    ppermute x12 -> x14, waiting for transfers between devices: 44.6 us -> 42.9 us  [passed_along(): return lax.ppermute(x, axis, pairs)]
  transfers between devices with their start and end apart: 18 -> 23, of which waited for: 9 -> 12; matrix products, arithmetic and copies ran while one was open for 2% -> 2% of each run, Pallas kernels for 11% -> 9%
where the time goes in v3:
time: 161 us; the launch traced here: 160 us
  waiting for transfers between devices  97.3 us (60%)
  starting transfers between devices  38.9 us (24%)
  Pallas kernels  15.7 us (10%)
  local copies, waits for them, and re-layouts  4.76 us (3%)
  other arithmetic  2.73 us (2%)
    ppermute x14, waiting for transfers between devices, passed_along(): return lax.ppermute(x, axis, pairs)  42.9 us
    ppermute x6, waiting for transfers between devices, swapped(): lax.ppermute(x, axis, [(i, i ^ distance) for i in range(lax.axis_size(axi...  38.1 us
    ppermute x14, starting transfers between devices, passed_along(): return lax.ppermute(x, axis, pairs)  24.1 us
    pallas_call x9, Pallas kernels, attend(): pl.pallas_call(functools.partial(attend_kernel, stages, state is None, ou...  14.3 us
    ppermute x1, waiting for transfers between devices, local(): part += (lax.ppermute(totals, 'row', back),)  11.5 us
    ppermute x6, starting transfers between devices, swapped(): lax.ppermute(x, axis, [(i, i ^ distance) for i in range(lax.axis_size(axi...  9.29 us
    ppermute x1, waiting for transfers between devices, local(): asked = lax.ppermute(q_lent, 'row', [(0, 1), (last_row, last_row - 1)])  4.89 us
  transfers between devices with their start and end apart: 23, of which 12 were waited for; matrix products, arithmetic and copies ran while one was open for 2% of the time, Pallas kernels for 9%

profile of v3, /device:TPU:0, one launch (start us, length us, event | category | flops | bytes accessed | tf_op | source)
XLA Modules:
  0.0 159.9 jit_solution(10029958580541749746)
XLA Ops:
  0.0 4.1 %collective-permute-start.8 = (bf16[16,2048]{1,0:T(8,128)(2,1)}, bf16[16,2048]{1,0:T(8,128)(2,1)S(1)}, u32[]{:S(2)}, u32[]{:S(2)}) collective-permute-start(bf16[16,2048]{1,0:T(8,128)(2,1)} %refs_0_.1), channel_id=1, source_target_pairs={{0,2},{1,3},{2,0},{3,1},{4,6},{5,7},{6,4},{7,5},{8,10},{9,11},{10,... | collective-permute-start | bytes 196616 | tf_op jit(solution)/shard_map/ppermute | solution.py:334
  4.1 0.1 collective-permute-start.9
  4.1 0.7 constant_dynamic-slice_fusion
  4.9 3.1 %collective-permute-done.8.refs_3_ = bf16[16,2048]{1,0:T(8,128)(2,1)S(1)} collective-permute-done((bf16[16,2048]{1,0:T(8,128)(2,1)}, bf16[16,2048]{1,0:T(8,128)(2,1)S(1)}, u32[]{:S(2)}, u32[]{:S(2)}) %collective-permute-start.8) | collective-permute-done | bytes 65568 | tf_op jit(solution)/shard_map/ppermute | solution.py:334
  8.0 2.8 %collective-permute-done.9.refs_4_ = bf16[16,2048]{1,0:T(8,128)(2,1)S(1)} collective-permute-done((bf16[16,2048]{1,0:T(8,128)(2,1)}, bf16[16,2048]{1,0:T(8,128)(2,1)S(1)}, u32[]{:S(2)}, u32[]{:S(2)}) %collective-permute-start.9) | collective-permute-done | bytes 65568 | tf_op jit(solution)/shard_map/ppermute | solution.py:334
  10.7 0.8 copy-done.6
  11.5 0.8 copy-done.8
  12.3 0.8 copy-done.9
  13.2 0.4 join.1
  13.6 0.7 collective-permute-start.10
  14.3 6.5 %collective-permute-done.10 = bf16[2,32,2048]{2,1,0:T(8,128)(2,1)S(1)} collective-permute-done((bf16[2,32,2048]{2,1,0:T(8,128)(2,1)S(1)}, bf16[2,32,2048]{2,1,0:T(8,128)(2,1)S(1)}, u32[]{:S(2)}, u32[]{:S(2)}) %collective-permute-start.10) | collective-permute-done | bytes 262176 | tf_op jit(solution)/shard_map/ppermute | solution.py:334
  20.8 2.7 %collective-permute-start.11 = (bf16[2,64,2048]{2,1,0:T(8,128)(2,1)S(1)}, bf16[2,64,2048]{2,1,0:T(8,128)(2,1)S(1)}, u32[]{:S(2)}, u32[]{:S(2)}) collective-permute-start(bf16[2,64,2048]{2,1,0:T(8,128)(2,1)S(1)} %pad_maximum_fusion.2), channel_id=1, source_target_pairs={{0,16},{4,20},{8,24},{12,28},{16,0},{20,4},{24,8},{28,12},{1,17},{... | collective-permute-start | bytes 1572872 | tf_op jit(solution)/shard_map/ppermute | solution.py:334
  23.5 11.0 %collective-permute-done.11 = bf16[2,64,2048]{2,1,0:T(8,128)(2,1)S(1)} collective-permute-done((bf16[2,64,2048]{2,1,0:T(8,128)(2,1)S(1)}, bf16[2,64,2048]{2,1,0:T(8,128)(2,1)S(1)}, u32[]{:S(2)}, u32[]{:S(2)}) %collective-permute-start.11) | collective-permute-done | bytes 524320 | tf_op jit(solution)/shard_map/ppermute | solution.py:334
  34.5 1.1 pad_maximum_fusion.1
  35.6 1.7 %collective-permute-start.12 = (bf16[2,128,2048]{2,1,0:T(8,128)(2,1)}, bf16[2,128,2048]{2,1,0:T(8,128)(2,1)}, u32[]{:S(2)}, u32[]{:S(2)}) collective-permute-start(bf16[2,128,2048]{2,1,0:T(8,128)(2,1)} %pad_maximum_fusion.1), channel_id=1, source_target_pairs={{0,8},{4,12},{8,0},{12,4},{16,24},{20,28},{24,16},{28,20},{1,9},{5... | collective-permute-start | bytes 3145736 | tf_op jit(solution)/shard_map/ppermute | solution.py:334
  37.3 1.3 collective-permute-start.6
  38.6 4.6 %collective-permute-start.2 = (bf16[256,2048]{1,0:T(8,128)(2,1)S(1)}, bf16[256,2048]{1,0:T(8,128)(2,1)S(1)}, u32[]{:S(2)}, u32[]{:S(2)}) collective-permute-start(bf16[256,2048]{1,0:T(8,128)(2,1)S(1)} %bitcast.9), channel_id=1, source_target_pairs={{0,1},{1,2},{2,3},{4,5},{5,6},{6,7},{8,9},{9,10},{10,11},{12,13},{... | collective-permute-start | bytes 3145736 | tf_op jit(solution)/shard_map/ppermute | solution.py:322
  43.3 0.7 dynamic-slice_bitcast_fusion
  43.9 0.7 constant_dynamic-slice_fusion.2
  44.7 0.0 copy-start.2
  44.7 0.0 copy-start.3
  44.7 0.0 copy-start.7
  44.7 14.7 %collective-permute-done.12 = bf16[2,128,2048]{2,1,0:T(8,128)(2,1)} collective-permute-done((bf16[2,128,2048]{2,1,0:T(8,128)(2,1)}, bf16[2,128,2048]{2,1,0:T(8,128)(2,1)}, u32[]{:S(2)}, u32[]{:S(2)}) %collective-permute-start.12) | collective-permute-done | bytes 1048608 | tf_op jit(solution)/shard_map/ppermute | solution.py:334
  59.4 1.6 pad_maximum_fusion.refs_1_
  60.9 0.1 collective-permute-start.13
  61.1 1.1 rotate.1
  62.1 0.0 copy-start.1
  62.2 2.9 %collective-permute-start.14 = (bf16[256,512]{1,0:T(8,128)(2,1)S(1)}, bf16[256,512]{1,0:T(8,128)(2,1)S(1)}, u32[]{:S(2)}, u32[]{:S(2)}) collective-permute-start(bf16[256,512]{1,0:T(8,128)(2,1)S(1)} %get-tuple-element.33), channel_id=1, source_target_pairs={{0,1},{3,2},{4,5},{7,6},{8,9},{11,10},{12,13},{15,14},{16,17},{19,... | collective-permute-start | bytes 786440 | tf_op jit(solution)/shard_map/ppermute | solution.py:468
  65.1 1.3 collective-permute-start.20
  66.4 4.9 %collective-permute-done.14.refs_0_ = bf16[256,512]{1,0:T(8,128)(2,1)S(1)} collective-permute-done((bf16[256,512]{1,0:T(8,128)(2,1)S(1)}, bf16[256,512]{1,0:T(8,128)(2,1)S(1)}, u32[]{:S(2)}, u32[]{:S(2)}) %collective-permute-start.14) | collective-permute-done | bytes 262176 | tf_op jit(solution)/shard_map/ppermute | solution.py:468
  71.3 4.4 %collective-permute-start.17 = (bf16[256,1536]{1,0:T(8,128)(2,1)S(1)}, bf16[256,1536]{1,0:T(8,128)(2,1)S(1)}, u32[]{:S(2)}, u32[]{:S(2)}) collective-permute-start(bf16[256,1536]{1,0:T(8,128)(2,1)S(1)} %get-tuple-element.36.refs_1_), channel_id=1, source_target_pairs={{0,1},{1,2},{2,3},{4,5},{5,6},{6,7},{8,9},{9,10},{10,11},{12,13},{... | collective-permute-start | bytes 2359304 | tf_op jit(solution)/shard_map/ppermute | solution.py:322
  75.7 10.9 %collective-permute-done.20.refs_3_ = bf16[256,1536]{1,0:T(8,128)(2,1)S(1)} collective-permute-done((bf16[256,1536]{1,0:T(8,128)(2,1)S(1)}, bf16[256,1536]{1,0:T(8,128)(2,1)S(1)}, u32[]{:S(2)}, u32[]{:S(2)}) %collective-permute-start.20) | collective-permute-done | bytes 786464 | tf_op jit(solution)/shard_map/ppermute | solution.py:322
  86.7 1.3 collective-permute-start.4
  87.9 0.0 collective-permute-done.6.refs_4_.refs_2_
  88.0 4.6 %collective-permute-start = (bf16[256,512]{1,0:T(8,128)(2,1)S(1)}, bf16[256,512]{1,0:T(8,128)(2,1)S(1)}, u32[]{:S(2)}, u32[]{:S(2)}) collective-permute-start(bf16[256,512]{1,0:T(8,128)(2,1)S(1)} %get-tuple-element.26.refs_1_), channel_id=1, source_target_pairs={{0,1},{1,2},{2,3},{4,5},{5,6},{6,7},{8,9},{9,10},{10,11},{12,13},{... | collective-permute-start | bytes 786440 | tf_op jit(solution)/shard_map/ppermute | solution.py:322
  92.5 0.0 collective-permute-done.2.refs_2_.refs_4_
  92.5 1.3 collective-permute-start.21
  93.8 0.1 slice.19
  93.9 0.1 slice.18
  94.0 0.7 collective-permute-start.18
  94.7 1.4 collective-permute-done.4.refs_3_.refs_1_
  96.1 1.3 collective-permute-start.22
  97.4 0.5 collective-permute-done.refs_1_.refs_3_
  97.9 0.7 collective-permute-start.19
  98.6 0.0 copy-start.4
  98.6 0.0 copy-start.5
  98.6 0.8 shard_map.208
  99.4 2.0 %shard_map.212 = (f32[12,128,256]{2,1,0:T(8,128)S(1)}, f32[12,2,256]{2,1,0:T(2,128)S(1)}) custom-call(bf16[256,2048]{1,0:T(8,128)(2,1)S(1)} %get-tuple-element.25.refs_0_, bf16[256,1536]{1,0:T(8,128)(2,1)S(1)} %get-tuple-element.36.refs_1_, bf16[256,2048]{1,0:T(8,128)(2,1)S(1)} %bitcast.11, f32[1,64,128]{2,1,0:T(8,128)S(1)} %copy-done.1), custom_call_target="tpu_custom_call" | custom-call | flops 402653184 | bytes 4718592 | tf_op jit(solution)/shard_map/pallas_call | solution.py:294
  101.4 16.0 %collective-permute-done.21.refs_3_ = bf16[256,1536]{1,0:T(8,128)(2,1)S(1)} collective-permute-done((bf16[256,1536]{1,0:T(8,128)(2,1)S(1)}, bf16[256,1536]{1,0:T(8,128)(2,1)S(1)}, u32[]{:S(2)}, u32[]{:S(2)}) %collective-permute-start.21) | collective-permute-done | bytes 786464 | tf_op jit(solution)/shard_map/ppermute | solution.py:322
  117.4 0.7 collective-permute-start.5
  118.1 0.1 shard_map.211
  118.3 0.7 collective-permute-start.1
  118.9 14.0 %collective-permute-done.22.refs_4_ = bf16[256,1536]{1,0:T(8,128)(2,1)S(1)} collective-permute-done((bf16[256,1536]{1,0:T(8,128)(2,1)S(1)}, bf16[256,1536]{1,0:T(8,128)(2,1)S(1)}, u32[]{:S(2)}, u32[]{:S(2)}) %collective-permute-start.22) | collective-permute-done | bytes 786464 | tf_op jit(solution)/shard_map/ppermute | solution.py:322
  132.9 0.7 collective-permute-start.7
  133.6 0.7 collective-permute-start.3
  134.3 1.3 collective-permute-start.15
  135.6 0.9 shard_map.209
  136.5 2.4 %shard_map.213 = (f32[12,128,256]{2,1,0:T(8,128)S(1)}, f32[12,2,256]{2,1,0:T(2,128)S(1)}) custom-call(bf16[256,2048]{1,0:T(8,128)(2,1)S(1)} %get-tuple-element.25.refs_0_, bf16[256,1536]{1,0:T(8,128)(2,1)S(1)} %collective-permute-done.17.refs_1_, ...), custom_call_target="tpu_custom_call", output_to_operand_aliasing={{0}: (7, {}), {1}: (8, {})} | custom-call | flops 805306368 | bytes 6291456 | tf_op jit(solution)/shard_map/pallas_call | solution.py:294
  138.9 3.0 %shard_map.214 = (f32[12,128,256]{2,1,0:T(8,128)S(1)}, f32[12,2,256]{2,1,0:T(2,128)S(1)}) custom-call(bf16[256,2048]{1,0:T(8,128)(2,1)S(1)} %get-tuple-element.25.refs_0_, bf16[2,256,2048]{2,1,0:T(8,128)(2,1)S(1)} %pad_maximum_fusion.refs_1_, ...), custom_call_target="tpu_custom_call", output_to_operand_aliasing={{0}: (3, {}), {1}: (4, {})} | custom-call | flops 805306368 | bytes 6291456 | tf_op jit(solution)/shard_map/pallas_call | solution.py:294
  141.9 3.1 %shard_map.215 = (bf16[256,2048]{1,0:T(8,128)(2,1)}, f32[12,128,256]{2,1,0:T(8,128)S(1)}, f32[12,2,256]{2,1,0:T(2,128)S(1)}) custom-call(bf16[256,2048]{1,0:T(8,128)(2,1)S(1)} %get-tuple-element.25.refs_0_, bf16[256,1536]{1,0:T(8,128)(2,1)S(1)} %collective-permute-done.18.refs_1_, ...), custom_call_target="tpu_custom_call", output_to_operand_aliasing={{1}: (7, {}), {2}: (8, {})} | custom-call | flops 805306368 | bytes 6291456 | tf_op jit(solution)/shard_map/pallas_call | solution.py:294
  145.0 1.3 collective-permute-start.16
  146.3 1.2 shard_map.210
  147.4 11.5 %collective-permute-done.16.refs_10_ = f32[4,2,256]{2,1,0:T(2,128)S(1)} collective-permute-done((f32[4,2,256]{2,1,0:T(2,128)S(1)}, f32[4,2,256]{2,1,0:T(2,128)S(1)}, u32[]{:S(2)}, u32[]{:S(2)}) %collective-permute-start.16) | collective-permute-done | bytes 8224 | tf_op jit(solution)/shard_map/ppermute | solution.py:478
  158.9 1.0 shard_map.216
  (31 shorter events, 0.2 us)
Async XLA Ops:
  0.0 37.3 %copy-start = (bf16[1,4,64,2048]{3,2,1,0:T(8,128)(2,1)S(1)}, bf16[1,4,64,2048]{3,2,1,0:T(8,128)(2,1)}, u32[]{:S(2)}) copy-start(bf16[1,4,64,2048]{3,2,1,0:T(8,128)(2,1)} %param.24) | copy-start | bytes 3145732
  0.0 8.0 %collective-permute-start.8 = (bf16[16,2048]{1,0:T(8,128)(2,1)}, bf16[16,2048]{1,0:T(8,128)(2,1)S(1)}, u32[]{:S(2)}, u32[]{:S(2)}) collective-permute-start(bf16[16,2048]{1,0:T(8,128)(2,1)} %refs_0_.1), channel_id=1, source_target_pairs={{0,2},{1,3},{2,0},{3,1},{4,6},{5,7},{6,4},{7,5},{8,10},{9,11},{10,... | collective-permute-start | bytes 196616 | tf_op jit(solution)/shard_map/ppermute | solution.py:334
  4.1 6.7 %collective-permute-start.9 = (bf16[16,2048]{1,0:T(8,128)(2,1)}, bf16[16,2048]{1,0:T(8,128)(2,1)S(1)}, u32[]{:S(2)}, u32[]{:S(2)}) collective-permute-start(bf16[16,2048]{1,0:T(8,128)(2,1)} %refs_1_.1), channel_id=1, source_target_pairs={{0,2},{1,3},{2,0},{3,1},{4,6},{5,7},{6,4},{7,5},{8,10},{9,11},{10,... | collective-permute-start | bytes 196616 | tf_op jit(solution)/shard_map/ppermute | solution.py:334
  10.7 0.8 copy-start.6
  11.5 0.8 copy-start.8
  12.3 0.8 copy-start.9
  13.2 31.5 %copy-start.12 = (f32[2,64,128]{2,1,0:T(8,128)S(1)}, f32[2,64,128]{2,1,0:T(8,128)}, u32[]{:S(2)}) copy-start(f32[2,64,128]{2,1,0:T(8,128)} %constant.44.clone) | copy-start | bytes 196612
  13.6 7.2 %collective-permute-start.10 = (bf16[2,32,2048]{2,1,0:T(8,128)(2,1)S(1)}, bf16[2,32,2048]{2,1,0:T(8,128)(2,1)S(1)}, u32[]{:S(2)}, u32[]{:S(2)}) collective-permute-start(bf16[2,32,2048]{2,1,0:T(8,128)(2,1)S(1)} %join.1), channel_id=1, source_target_pairs={{0,1},{1,0},{2,3},{3,2},{4,5},{5,4},{6,7},{7,6},{8,9},{9,8},{10,11... | collective-permute-start | bytes 786440 | tf_op jit(solution)/shard_map/ppermute | solution.py:334
  20.8 16.6 %copy-start.10 = (bf16[2,32,2048]{2,1,0:T(8,128)(2,1)}, bf16[2,32,2048]{2,1,0:T(8,128)(2,1)S(1)}, u32[]{:S(2)}) copy-start(bf16[2,32,2048]{2,1,0:T(8,128)(2,1)S(1)} %collective-permute-done.10) | copy-start | bytes 786436
  20.8 13.7 %collective-permute-start.11 = (bf16[2,64,2048]{2,1,0:T(8,128)(2,1)S(1)}, bf16[2,64,2048]{2,1,0:T(8,128)(2,1)S(1)}, u32[]{:S(2)}, u32[]{:S(2)}) collective-permute-start(bf16[2,64,2048]{2,1,0:T(8,128)(2,1)S(1)} %pad_maximum_fusion.2), channel_id=1, source_target_pairs={{0,16},{4,20},{8,24},{12,28},{16,0},{20,4},{24,8},{28,12},{1,17},{... | collective-permute-start | bytes 1572872 | tf_op jit(solution)/shard_map/ppermute | solution.py:334
  34.5 2.8 %copy-start.11 = (bf16[2,64,2048]{2,1,0:T(8,128)(2,1)}, bf16[2,64,2048]{2,1,0:T(8,128)(2,1)S(1)}, u32[]{:S(2)}) copy-start(bf16[2,64,2048]{2,1,0:T(8,128)(2,1)S(1)} %collective-permute-done.11) | copy-start | bytes 1572868
  35.6 23.8 %collective-permute-start.12 = (bf16[2,128,2048]{2,1,0:T(8,128)(2,1)}, bf16[2,128,2048]{2,1,0:T(8,128)(2,1)}, u32[]{:S(2)}, u32[]{:S(2)}) collective-permute-start(bf16[2,128,2048]{2,1,0:T(8,128)(2,1)} %pad_maximum_fusion.1), channel_id=1, source_target_pairs={{0,8},{4,12},{8,0},{12,4},{16,24},{20,28},{24,16},{28,20},{1,9},{5... | collective-permute-start | bytes 3145736 | tf_op jit(solution)/shard_map/ppermute | solution.py:334
  37.3 50.6 %collective-permute-start.6 = (bf16[256,2048]{1,0:T(8,128)(2,1)S(1)}, bf16[256,2048]{1,0:T(8,128)(2,1)S(1)}, u32[]{:S(2)}, u32[]{:S(2)}) collective-permute-start(bf16[256,2048]{1,0:T(8,128)(2,1)S(1)} %bitcast.8), channel_id=1, source_target_pairs={{1,0},{2,1},{3,2},{5,4},{6,5},{7,6},{9,8},{10,9},{11,10},{13,12},{... | collective-permute-start | bytes 3145736 | tf_op jit(solution)/shard_map/ppermute | solution.py:322
  38.6 53.9 %collective-permute-start.2 = (bf16[256,2048]{1,0:T(8,128)(2,1)S(1)}, bf16[256,2048]{1,0:T(8,128)(2,1)S(1)}, u32[]{:S(2)}, u32[]{:S(2)}) collective-permute-start(bf16[256,2048]{1,0:T(8,128)(2,1)S(1)} %bitcast.9), channel_id=1, source_target_pairs={{0,1},{1,2},{2,3},{4,5},{5,6},{6,7},{8,9},{9,10},{10,11},{12,13},{... | collective-permute-start | bytes 3145736 | tf_op jit(solution)/shard_map/ppermute | solution.py:322
  44.7 16.4 %copy-start.2 = (bf16[1,4,64,2048]{3,2,1,0:T(8,128)(2,1)S(1)}, bf16[1,4,64,2048]{3,2,1,0:T(8,128)(2,1)}, u32[]{:S(2)}) copy-start(bf16[1,4,64,2048]{3,2,1,0:T(8,128)(2,1)} %param.22) | copy-start | bytes 3145732
  44.7 16.4 %copy-start.3 = (bf16[1,4,64,2048]{3,2,1,0:T(8,128)(2,1)S(1)}, bf16[1,4,64,2048]{3,2,1,0:T(8,128)(2,1)}, u32[]{:S(2)}) copy-start(bf16[1,4,64,2048]{3,2,1,0:T(8,128)(2,1)} %param.23) | copy-start | bytes 3145732
  44.7 16.4 %copy-start.7 = (bf16[128,128]{1,0:T(8,128)(2,1)S(1)}, bf16[128,128]{1,0:T(8,128)(2,1)}, u32[]{:S(2)}) copy-start(bf16[128,128]{1,0:T(8,128)(2,1)} %constant.40.clone.partners_ref.refs_6_) | copy-start | bytes 98308
  60.9 73.4 %collective-permute-start.13 = (bf16[2,256,2048]{2,1,0:T(8,128)(2,1)S(1)}, bf16[2,256,2048]{2,1,0:T(8,128)(2,1)S(1)}, u32[]{:S(2)}, u32[]{:S(2)}) collective-permute-start(bf16[2,256,2048]{2,1,0:T(8,128)(2,1)S(1)} %pad_maximum_fusion.refs_1_), channel_id=1, source_target_pairs={{0,4},{4,0},{8,12},{12,8},{16,20},{20,16},{24,28},{28,24},{1,5},{5... | collective-permute-start | bytes 6291464 | tf_op jit(solution)/shard_map/ppermute | solution.py:334
  62.1 36.4 %copy-start.1 = (f32[1,64,128]{2,1,0:T(8,128)S(1)}, f32[1,64,128]{2,1,0:T(8,128)}, u32[]{:S(2)}) copy-start(f32[1,64,128]{2,1,0:T(8,128)} %constant.47.clone.refs_3_.refs_5_.refs_6_) | copy-start | bytes 98308
  62.2 9.1 %collective-permute-start.14 = (bf16[256,512]{1,0:T(8,128)(2,1)S(1)}, bf16[256,512]{1,0:T(8,128)(2,1)S(1)}, u32[]{:S(2)}, u32[]{:S(2)}) collective-permute-start(bf16[256,512]{1,0:T(8,128)(2,1)S(1)} %get-tuple-element.33), channel_id=1, source_target_pairs={{0,1},{3,2},{4,5},{7,6},{8,9},{11,10},{12,13},{15,14},{16,17},{19,... | collective-permute-start | bytes 786440 | tf_op jit(solution)/shard_map/ppermute | solution.py:468
  65.1 21.6 %collective-permute-start.20 = (bf16[256,1536]{1,0:T(8,128)(2,1)S(1)}, bf16[256,1536]{1,0:T(8,128)(2,1)S(1)}, u32[]{:S(2)}, u32[]{:S(2)}) collective-permute-start(bf16[256,1536]{1,0:T(8,128)(2,1)S(1)} %get-tuple-element.36.refs_1_), channel_id=1, source_target_pairs={{1,0},{2,1},{3,2},{5,4},{6,5},{7,6},{9,8},{10,9},{11,10},{13,12},{... | collective-permute-start | bytes 2359304 | tf_op jit(solution)/shard_map/ppermute | solution.py:322
  71.3 22.7 %collective-permute-start.17 = (bf16[256,1536]{1,0:T(8,128)(2,1)S(1)}, bf16[256,1536]{1,0:T(8,128)(2,1)S(1)}, u32[]{:S(2)}, u32[]{:S(2)}) collective-permute-start(bf16[256,1536]{1,0:T(8,128)(2,1)S(1)} %get-tuple-element.36.refs_1_), channel_id=1, source_target_pairs={{0,1},{1,2},{2,3},{4,5},{5,6},{6,7},{8,9},{9,10},{10,11},{12,13},{... | collective-permute-start | bytes 2359304 | tf_op jit(solution)/shard_map/ppermute | solution.py:322
  86.7 9.4 %collective-permute-start.4 = (bf16[256,512]{1,0:T(8,128)(2,1)S(1)}, bf16[256,512]{1,0:T(8,128)(2,1)S(1)}, u32[]{:S(2)}, u32[]{:S(2)}) collective-permute-start(bf16[256,512]{1,0:T(8,128)(2,1)S(1)} %get-tuple-element.26.refs_1_), channel_id=1, source_target_pairs={{1,0},{2,1},{3,2},{5,4},{6,5},{7,6},{9,8},{10,9},{11,10},{13,12},{... | collective-permute-start | bytes 786440 | tf_op jit(solution)/shard_map/ppermute | solution.py:322
  88.0 9.9 %collective-permute-start = (bf16[256,512]{1,0:T(8,128)(2,1)S(1)}, bf16[256,512]{1,0:T(8,128)(2,1)S(1)}, u32[]{:S(2)}, u32[]{:S(2)}) collective-permute-start(bf16[256,512]{1,0:T(8,128)(2,1)S(1)} %get-tuple-element.26.refs_1_), channel_id=1, source_target_pairs={{0,1},{1,2},{2,3},{4,5},{5,6},{6,7},{8,9},{9,10},{10,11},{12,13},{... | collective-permute-start | bytes 786440 | tf_op jit(solution)/shard_map/ppermute | solution.py:322
  92.5 24.9 %collective-permute-start.21 = (bf16[256,1536]{1,0:T(8,128)(2,1)S(1)}, bf16[256,1536]{1,0:T(8,128)(2,1)S(1)}, u32[]{:S(2)}, u32[]{:S(2)}) collective-permute-start(bf16[256,1536]{1,0:T(8,128)(2,1)S(1)} %collective-permute-done.20.refs_3_), channel_id=1, source_target_pairs={{1,0},{2,1},{5,4},{6,5},{9,8},{10,9},{13,12},{14,13},{17,16},{18,1... | collective-permute-start | bytes 2359304 | tf_op jit(solution)/shard_map/ppermute | solution.py:322
  94.0 24.3 %collective-permute-start.18 = (bf16[256,1536]{1,0:T(8,128)(2,1)S(1)}, bf16[256,1536]{1,0:T(8,128)(2,1)S(1)}, u32[]{:S(2)}, u32[]{:S(2)}) collective-permute-start(bf16[256,1536]{1,0:T(8,128)(2,1)S(1)} %collective-permute-done.17.refs_1_), channel_id=1, source_target_pairs={{1,2},{2,3},{5,6},{6,7},{9,10},{10,11},{13,14},{14,15},{17,18},{18... | collective-permute-start | bytes 2359304 | tf_op jit(solution)/shard_map/ppermute | solution.py:322
  96.1 36.8 %collective-permute-start.22 = (bf16[256,1536]{1,0:T(8,128)(2,1)S(1)}, bf16[256,1536]{1,0:T(8,128)(2,1)S(1)}, u32[]{:S(2)}, u32[]{:S(2)}) collective-permute-start(bf16[256,1536]{1,0:T(8,128)(2,1)S(1)} %slice.19), channel_id=1, source_target_pairs={{1,0},{2,1},{5,4},{6,5},{9,8},{10,9},{13,12},{14,13},{17,16},{18,1... | collective-permute-start | bytes 2359304 | tf_op jit(solution)/shard_map/ppermute | solution.py:322
  97.9 35.8 %collective-permute-start.19 = (bf16[256,1536]{1,0:T(8,128)(2,1)S(1)}, bf16[256,1536]{1,0:T(8,128)(2,1)S(1)}, u32[]{:S(2)}, u32[]{:S(2)}) collective-permute-start(bf16[256,1536]{1,0:T(8,128)(2,1)S(1)} %slice.18), channel_id=1, source_target_pairs={{1,2},{2,3},{5,6},{6,7},{9,10},{10,11},{13,14},{14,15},{17,18},{18... | collective-permute-start | bytes 2359304 | tf_op jit(solution)/shard_map/ppermute | solution.py:322
  98.6 19.5 %copy-start.4 = (f32[2,64,128]{2,1,0:T(8,128)S(1)}, f32[2,64,128]{2,1,0:T(8,128)}, u32[]{:S(2)}) copy-start(f32[2,64,128]{2,1,0:T(8,128)} %constant.46.clone.refs_6_.refs_5_) | copy-start | bytes 196612
  98.6 19.5 %copy-start.5 = (f32[2,64,128]{2,1,0:T(8,128)S(1)}, f32[2,64,128]{2,1,0:T(8,128)}, u32[]{:S(2)}) copy-start(f32[2,64,128]{2,1,0:T(8,128)} %constant.45.clone.refs_5_.refs_6_) | copy-start | bytes 196612
  117.4 27.5 %collective-permute-start.5 = (bf16[256,512]{1,0:T(8,128)(2,1)S(1)}, bf16[256,512]{1,0:T(8,128)(2,1)S(1)}, u32[]{:S(2)}, u32[]{:S(2)}) collective-permute-start(bf16[256,512]{1,0:T(8,128)(2,1)S(1)} %collective-permute-done.4.refs_3_.refs_1_), channel_id=1, source_target_pairs={{2,1},{6,5},{10,9},{14,13},{18,17},{22,21},{26,25},{30,29}} | collective-permute-start | bytes 786440 | tf_op jit(solution)/shard_map/ppermute | solution.py:322
  118.3 29.2 %collective-permute-start.1 = (bf16[256,512]{1,0:T(8,128)(2,1)S(1)}, bf16[256,512]{1,0:T(8,128)(2,1)S(1)}, u32[]{:S(2)}, u32[]{:S(2)}) collective-permute-start(bf16[256,512]{1,0:T(8,128)(2,1)S(1)} %collective-permute-done.refs_1_.refs_3_), channel_id=1, source_target_pairs={{1,2},{5,6},{9,10},{13,14},{17,18},{21,22},{25,26},{29,30}} | collective-permute-start | bytes 786440 | tf_op jit(solution)/shard_map/ppermute | solution.py:322
  132.9 26.0 %collective-permute-start.7 = (bf16[256,512]{1,0:T(8,128)(2,1)S(1)}, bf16[256,512]{1,0:T(8,128)(2,1)S(1)}, u32[]{:S(2)}, u32[]{:S(2)}) collective-permute-start(bf16[256,512]{1,0:T(8,128)(2,1)S(1)} %slice.17), channel_id=1, source_target_pairs={{2,1},{6,5},{10,9},{14,13},{18,17},{22,21},{26,25},{30,29}} | collective-permute-start | bytes 786440 | tf_op jit(solution)/shard_map/ppermute | solution.py:322
  133.6 25.3 %collective-permute-start.3 = (bf16[256,512]{1,0:T(8,128)(2,1)S(1)}, bf16[256,512]{1,0:T(8,128)(2,1)S(1)}, u32[]{:S(2)}, u32[]{:S(2)}) collective-permute-start(bf16[256,512]{1,0:T(8,128)(2,1)S(1)} %slice.16), channel_id=1, source_target_pairs={{1,2},{5,6},{9,10},{13,14},{17,18},{21,22},{25,26},{29,30}} | collective-permute-start | bytes 786440 | tf_op jit(solution)/shard_map/ppermute | solution.py:322
  134.3 24.6 %collective-permute-start.15 = (bf16[4,128,256]{2,1,0:T(8,128)(2,1)S(1)}, bf16[4,128,256]{2,1,0:T(8,128)(2,1)S(1)}, u32[]{:S(2)}, u32[]{:S(2)}) collective-permute-start(bf16[4,128,256]{2,1,0:T(8,128)(2,1)S(1)} %get-tuple-element.34), channel_id=1, source_target_pairs={{1,0},{2,3},{5,4},{6,7},{9,8},{10,11},{13,12},{14,15},{17,16},{18,... | collective-permute-start | bytes 786440 | tf_op jit(solution)/shard_map/ppermute | solution.py:477
  145.0 13.9 %collective-permute-start.16 = (f32[4,2,256]{2,1,0:T(2,128)S(1)}, f32[4,2,256]{2,1,0:T(2,128)S(1)}, u32[]{:S(2)}, u32[]{:S(2)}) collective-permute-start(f32[4,2,256]{2,1,0:T(2,128)S(1)} %get-tuple-element.35), channel_id=1, source_target_pairs={{1,0},{2,3},{5,4},{6,7},{9,8},{10,11},{13,12},{14,15},{17,16},{18,... | collective-permute-start | bytes 24584 | tf_op jit(solution)/shard_map/ppermute | solution.py:478

commit v4 on v3

--- a/solution.py
+++ b/solution.py
@@ -88,7 +88,7 @@
     unit = heads // 8
     if heads % 8:
         return ((0, heads, 1),)
-    counts, groups = (6 * unit, 2 * unit), (6 * unit, 2 * unit)
+    counts, groups = (4 * unit, 4 * unit), (4 * unit, 2 * unit)
     chunks, first = [], 0
     for count, group in zip(counts, groups):
         chunks.append((first, count, group))
@@ -106,7 +106,7 @@
     tiles, plan = [], []
     for start in range(0, tokens, lanes):
         parts = [inside[r * cols : (r + 1) * cols, start : start + lanes] for r in range(rows)]
-        used = [r for r in range(rows) if parts[r].any()]
+        used = [r for r in range(rows) if parts[r].any()] or [0]
         names = []
         for r in range(used[0], used[-1] + 1):
             found = [i for i, tile in enumerate(tiles) if (tile == parts[r]).all()]
@@ -117,7 +117,7 @@
     return np.where(np.stack(tiles), 0.0, NEG).astype(np.float32), tuple(plan)
 
 
-def attend_kernel(stages, first, last, group, lanes, merge, share, *refs):
+def attend_kernel(stages, first, last, group, lanes, merge, share, base, *refs):
     refs = list(refs)
     q_ref = refs.pop(0)
 
@@ -159,7 +159,7 @@
             ]
 
         def update(head, found):
-            at = unit * group + head
+            at = base + unit * group + head
             if have:
                 top, total, summed = ml_ref[at, 0:1], ml_ref[at, 1:2], acc_ref[at]
             started = have
@@ -219,7 +219,7 @@
         @pl.when(merge(lax.axis_index("row"), lax.axis_size("row")))
         def _():
             for head in range(group):
-                at = unit * group + head
+                at = base + unit * group + head
                 top, met = ml_ref[at, 0:1], part_ml_ref[at, 0:1]
                 peak = jnp.maximum(top, met)
                 ours = jnp.exp2((top - peak) * EXP_SCALE)
@@ -229,11 +229,11 @@
 
     if share:
         for head in range(group):
-            at = unit * group + head
+            at = base + unit * group + head
             share_ref[at] = (acc_ref[at] * (1.0 / ml_ref[at, 1:2])).astype(share_ref.dtype)
     if last is not None:
         for head in range(group):
-            at = unit * group + head
+            at = base + unit * group + head
             scaled = acc_ref[at] * (1.0 / ml_ref[at, 1:2, :])
             out_ref[:, pl.ds(head * HD, HD)] = scaled.astype(out_ref.dtype).T
 
@@ -256,7 +256,10 @@
     return pltpu.with_memory_space_constraint(x, pltpu.VMEM)
 
 
-def attend(q, state, sources, stages, tiles, heads, group, out=None, last=False, merge=None, part=(), share=False):
+def attend(
+    q, state, sources, stages, tiles, heads, group, out=None, last=False, merge=None, part=(), share=False,
+    base=0,
+):
     tokens, width = q.shape
     lanes = 128 if tokens % 128 == 0 else tokens
     first_head = stages[0][1][0].head
@@ -269,9 +272,10 @@
         operands += [resident(a) for a in state]
     operands += [resident(a) for a in part]
     specs = [whole] * len(operands)
+    held = heads if state is None else state[0].shape[0]
     out_shape = [
-        pltpu.VMEM((heads, HD, tokens), jnp.float32),
-        pltpu.VMEM((heads, 2, tokens), jnp.float32),
+        pltpu.VMEM((held, HD, tokens), jnp.float32),
+        pltpu.VMEM((held, 2, tokens), jnp.float32),
     ]
     out_specs = [whole] * 2
     scratch = []
@@ -294,7 +298,7 @@
     return pl.pallas_call(
         functools.partial(
             attend_kernel, stages, state is None, (out is not None) if last else None, group, lanes,
-            merge, share,
+            merge, share, base,
         ),
         out_shape=out_shape,
         grid=(heads // group,),
@@ -432,13 +436,12 @@
             met[what, 0] = block
             above = below = block
             for d in range(1, 2 if near_only else reach + 1):
-                edges = not (lend and d == reach and what in (f"keys{lent}", f"values{lent}"))
-                above = passed_along(above, "row", 1, d, edges)
-                below = passed_along(below, "row", -1, d, edges)
+                above = passed_along(above, "row", 1, d)
+                below = passed_along(below, "row", -1, d)
                 met[what, -d], met[what, d] = above, below
 
         for c, keys in enumerate(k_rot):
-            travel(f"keys{c}", keys)
+            travel(f"keys{c}", keys, near_only=lend and c == lent)
         if lend:
             travel("values", values, near_only=True)
             for c, (first, count, _) in enumerate(chunks):
@@ -448,15 +451,24 @@
                     met[f"values{c}", 2 * sign] = passed_along(
                         met["values", sign][:, span], "row", by, 2, edges
                     )
+            halves = [(half * chunks[lent][2], chunks[lent][2]) for half in range(chunks[lent][1] // chunks[lent][2])]
+            for half, (offset, count) in enumerate(halves):
+                span = slice(offset * HD, (offset + count) * HD)
+                for sign, by in ((-1, 1), (1, -1)):
+                    met[f"half{half}", 2 * sign] = passed_along(met[f"keys{lent}", sign][:, span], "row", by, 2, False)
         else:
             travel("values", values)
 
-        def block_of(c, d, shift=None):
+        def block_of(c, d, shift=None, half=None):
             first = chunks[c][0]
             tiles, plan = mask_tiles(rows_dev, cols, (d if shift is None else shift) * rows_dev, lanes)
             split = (f"values{c}", d) in met
-            pair = met[f"keys{c}", d], met[f"values{c}" if split else "values", d]
-            return pair, Block(plan, first, first, first if split else 0, cols), tiles
+            held = met[f"values{c}" if split else "values", d]
+            values_head = first if split else 0
+            if half is not None:
+                head = first + halves[half][0]
+                return (met[f"half{half}", d], held), Block(plan, head, head, values_head, cols), tiles
+            return (met[f"keys{c}", d], held), Block(plan, first, first, values_head, cols), tiles
 
         def within(d):
             return lambda index, size: (index + d >= 0) & (index + d < size)
@@ -494,16 +506,21 @@
                 q_rot, state, [(x,) for x in cond_held],
                 [(None, (block,) * len(cond_held))], [], count, group,
             )
-            flags, more = [within(-reach), within(reach)], {}
-            if lend and c == lent:
-                flags = [
-                    lambda index, size: (index >= reach) & (index < size - 1),
-                    lambda index, size: (index > 0) & (index < size - reach),
-                ]
-                more = dict(
-                    merge=lambda index, size: (index == 0) | (index == size - 1), part=part
+            if not (lend and c == lent):
+                out, *_ = run(state, [-reach, reach], [within(-reach), within(reach)], out=out, last=True)
+                continue
+            flags = [
+                lambda index, size: (index >= reach) & (index < size - 1),
+                lambda index, size: (index > 0) & (index < size - reach),
+            ]
+            for half, (offset, count) in enumerate(halves):
+                pairs, blocks, tiles = zip(*(block_of(c, d, None, half) for d in (-reach, reach)))
+                stages = [(flag, (block,)) for flag, block in zip(flags, blocks)]
+                out, *state = attend(
+                    q_rot, state, pairs, stages, tiles, count, group, out=out,
+                    last=True, base=offset, part=part,
+                    merge=lambda index, size: (index == 0) | (index == size - 1),
                 )
-            out, *_ = run(state, [-reach, reach], flags, out=out, last=True, **more)
         outputs.append(out.reshape(rows_dev, cols, width))
     return jnp.stack(outputs) if view_dev > 1 else outputs[0][None]
 

time: 161 us -> 187 us (1.16)
  the two profiles are of different devices: /device:TPU:0 before, /device:TPU:20 now
where the time goes in v4:
time: 187 us; the launch traced here: 186 us
  waiting for transfers between devices  94.2 us (50%)
  starting transfers between devices  60.1 us (32%)
  Pallas kernels  23.4 us (13%)
  local copies, waits for them, and re-layouts  5.72 us (3%)
  other arithmetic  2.52 us (1%)
    ppermute x16, waiting for transfers between devices, passed_along(): return lax.ppermute(x, axis, pairs)  48.7 us
    ppermute x16, starting transfers between devices, passed_along(): return lax.ppermute(x, axis, pairs)  47.1 us
    ppermute x6, waiting for transfers between devices, swapped(): lax.ppermute(x, axis, [(i, i ^ distance) for i in range(lax.axis_size(axi...  36.6 us
    pallas_call x10, Pallas kernels, attend(): pl.pallas_call(functools.partial(attend_kernel, stages, state is None, ou...  21.9 us
    ppermute x6, starting transfers between devices, swapped(): lax.ppermute(x, axis, [(i, i ^ distance) for i in range(lax.axis_size(axi...  9.18 us
    ppermute x1, waiting for transfers between devices, local(): asked = lax.ppermute(q_lent, 'row', [(0, 1), (last_row, last_row - 1)])  8.84 us
  transfers between devices with their start and end apart: 25, of which 11 were waited for; matrix products, arithmetic and copies ran while one was open for 2% of the time, Pallas kernels for 11%

profile of v4, /device:TPU:20, one launch (start us, length us, event | category | flops | bytes accessed | tf_op | source)
XLA Modules:
  0.0 186.5 jit_solution(17070425884637108562)
XLA Ops:
  0.0 0.3 collective-permute-start.10
  0.3 2.6 %collective-permute-start.11 = (bf16[16,2048]{1,0:T(8,128)(2,1)}, bf16[16,2048]{1,0:T(8,128)(2,1)S(1)}, u32[]{:S(2)}, u32[]{:S(2)}) collective-permute-start(bf16[16,2048]{1,0:T(8,128)(2,1)} %refs_1_.1), channel_id=1, source_target_pairs={{0,2},{1,3},{2,0},{3,1},{4,6},{5,7},{6,4},{7,5},{8,10},{9,11},{10,... | collective-permute-start | bytes 196616 | tf_op jit(solution)/shard_map/ppermute | solution.py:338
  2.9 0.7 constant_dynamic-slice_fusion
  3.7 2.1 %collective-permute-done.10.refs_3_ = bf16[16,2048]{1,0:T(8,128)(2,1)S(1)} collective-permute-done((bf16[16,2048]{1,0:T(8,128)(2,1)}, bf16[16,2048]{1,0:T(8,128)(2,1)S(1)}, u32[]{:S(2)}, u32[]{:S(2)}) %collective-permute-start.10) | collective-permute-done | bytes 65568 | tf_op jit(solution)/shard_map/ppermute | solution.py:338
  5.7 0.8 collective-permute-done.11.refs_4_
  6.6 0.8 copy-done.6
  7.3 0.8 copy-done.8
  8.2 0.8 copy-done.9
  9.0 0.4 join.1
  9.4 0.0 copy-start.7
  9.4 4.1 %collective-permute-start.12 = (bf16[2,32,2048]{2,1,0:T(8,128)(2,1)S(1)}, bf16[2,32,2048]{2,1,0:T(8,128)(2,1)S(1)}, u32[]{:S(2)}, u32[]{:S(2)}) collective-permute-start(bf16[2,32,2048]{2,1,0:T(8,128)(2,1)S(1)} %join.1), channel_id=1, source_target_pairs={{0,1},{1,0},{2,3},{3,2},{4,5},{5,4},{6,7},{7,6},{8,9},{9,8},{10,11... | collective-permute-start | bytes 786440 | tf_op jit(solution)/shard_map/ppermute | solution.py:338
  13.5 6.5 %collective-permute-done.12 = bf16[2,32,2048]{2,1,0:T(8,128)(2,1)S(1)} collective-permute-done((bf16[2,32,2048]{2,1,0:T(8,128)(2,1)S(1)}, bf16[2,32,2048]{2,1,0:T(8,128)(2,1)S(1)}, u32[]{:S(2)}, u32[]{:S(2)}) %collective-permute-start.12) | collective-permute-done | bytes 262176 | tf_op jit(solution)/shard_map/ppermute | solution.py:338
  20.1 0.6 collective-permute-start.13
  20.6 12.8 %collective-permute-done.13 = bf16[2,64,2048]{2,1,0:T(8,128)(2,1)S(1)} collective-permute-done((bf16[2,64,2048]{2,1,0:T(8,128)(2,1)S(1)}, bf16[2,64,2048]{2,1,0:T(8,128)(2,1)S(1)}, u32[]{:S(2)}, u32[]{:S(2)}) %collective-permute-start.13) | collective-permute-done | bytes 524320 | tf_op jit(solution)/shard_map/ppermute | solution.py:338
  33.4 0.8 copy-done.12
  34.2 1.0 pad_maximum_fusion.1
  35.2 1.5 collective-permute-start.14
  36.7 0.8 dynamic-slice_bitcast_fusion
  37.5 0.7 constant_dynamic-slice_fusion.2
  38.3 1.1 rotate.1
  39.4 3.4 %collective-permute-start.19 = (bf16[256,1024]{1,0:T(8,128)(2,1)S(1)}, bf16[256,1024]{1,0:T(8,128)(2,1)S(1)}, u32[]{:S(2)}, u32[]{:S(2)}) collective-permute-start(bf16[256,1024]{1,0:T(8,128)(2,1)S(1)} %get-tuple-element.39.refs_1_), channel_id=1, source_target_pairs={{0,1},{1,2},{2,3},{4,5},{5,6},{6,7},{8,9},{9,10},{10,11},{12,13},{... | collective-permute-start | bytes 1572872 | tf_op jit(solution)/shard_map/ppermute | solution.py:326
  42.8 1.9 %collective-permute-start.2 = (bf16[256,2048]{1,0:T(8,128)(2,1)S(1)}, bf16[256,2048]{1,0:T(8,128)(2,1)S(1)}, u32[]{:S(2)}, u32[]{:S(2)}) collective-permute-start(bf16[256,2048]{1,0:T(8,128)(2,1)S(1)} %bitcast.8), channel_id=1, source_target_pairs={{0,1},{1,2},{2,3},{4,5},{5,6},{6,7},{8,9},{9,10},{10,11},{12,13},{... | collective-permute-start | bytes 3145736 | tf_op jit(solution)/shard_map/ppermute | solution.py:326
  44.7 14.5 %collective-permute-done.14 = bf16[2,128,2048]{2,1,0:T(8,128)(2,1)} collective-permute-done((bf16[2,128,2048]{2,1,0:T(8,128)(2,1)}, bf16[2,128,2048]{2,1,0:T(8,128)(2,1)}, u32[]{:S(2)}, u32[]{:S(2)}) %collective-permute-start.14) | collective-permute-done | bytes 1048608 | tf_op jit(solution)/shard_map/ppermute | solution.py:338
  59.2 1.4 pad_maximum_fusion.refs_1_
  60.6 0.1 collective-permute-start.15
  60.7 1.9 %collective-permute-start.22 = (bf16[256,1024]{1,0:T(8,128)(2,1)S(1)}, bf16[256,1024]{1,0:T(8,128)(2,1)S(1)}, u32[]{:S(2)}, u32[]{:S(2)}) collective-permute-start(bf16[256,1024]{1,0:T(8,128)(2,1)S(1)} %get-tuple-element.39.refs_1_), channel_id=1, source_target_pairs={{1,0},{2,1},{3,2},{5,4},{6,5},{7,6},{9,8},{10,9},{11,10},{13,12},{... | collective-permute-start | bytes 1572872 | tf_op jit(solution)/shard_map/ppermute | solution.py:326
  62.6 4.0 %collective-permute-start = (bf16[256,1024]{1,0:T(8,128)(2,1)S(1)}, bf16[256,1024]{1,0:T(8,128)(2,1)S(1)}, u32[]{:S(2)}, u32[]{:S(2)}) collective-permute-start(bf16[256,1024]{1,0:T(8,128)(2,1)S(1)} %get-tuple-element.29.refs_1_), channel_id=1, source_target_pairs={{0,1},{1,2},{2,3},{4,5},{5,6},{6,7},{8,9},{9,10},{10,11},{12,13},{... | collective-permute-start | bytes 1572872 | tf_op jit(solution)/shard_map/ppermute | solution.py:326
  66.6 0.0 collective-permute-done.19.refs_1_
  66.6 1.9 %collective-permute-start.6 = (bf16[256,2048]{1,0:T(8,128)(2,1)S(1)}, bf16[256,2048]{1,0:T(8,128)(2,1)S(1)}, u32[]{:S(2)}, u32[]{:S(2)}) collective-permute-start(bf16[256,2048]{1,0:T(8,128)(2,1)S(1)} %bitcast.9), channel_id=1, source_target_pairs={{1,0},{2,1},{3,2},{5,4},{6,5},{7,6},{9,8},{10,9},{11,10},{13,12},{... | collective-permute-start | bytes 3145736 | tf_op jit(solution)/shard_map/ppermute | solution.py:326
  68.5 8.9 %collective-permute-done.22.refs_3_ = bf16[256,1024]{1,0:T(8,128)(2,1)S(1)} collective-permute-done((bf16[256,1024]{1,0:T(8,128)(2,1)S(1)}, bf16[256,1024]{1,0:T(8,128)(2,1)S(1)}, u32[]{:S(2)}, u32[]{:S(2)}) %collective-permute-start.22) | collective-permute-done | bytes 524320 | tf_op jit(solution)/shard_map/ppermute | solution.py:326
  77.4 1.9 %collective-permute-start.4 = (bf16[256,1024]{1,0:T(8,128)(2,1)S(1)}, bf16[256,1024]{1,0:T(8,128)(2,1)S(1)}, u32[]{:S(2)}, u32[]{:S(2)}) collective-permute-start(bf16[256,1024]{1,0:T(8,128)(2,1)S(1)} %get-tuple-element.29.refs_1_), channel_id=1, source_target_pairs={{1,0},{2,1},{3,2},{5,4},{6,5},{7,6},{9,8},{10,9},{11,10},{13,12},{... | collective-permute-start | bytes 1572872 | tf_op jit(solution)/shard_map/ppermute | solution.py:326
  79.3 7.8 %collective-permute-done.refs_1_.refs_3_ = bf16[256,1024]{1,0:T(8,128)(2,1)S(1)} collective-permute-done((bf16[256,1024]{1,0:T(8,128)(2,1)S(1)}, bf16[256,1024]{1,0:T(8,128)(2,1)S(1)}, u32[]{:S(2)}, u32[]{:S(2)}) %collective-permute-start) | collective-permute-done | bytes 524320 | tf_op jit(solution)/shard_map/ppermute | solution.py:326
  87.1 1.3 collective-permute-start.16
  88.5 1.3 collective-permute-start.8
  89.8 0.1 fusion.1
  89.9 0.0 copy-start.2
  89.9 0.0 copy-start.3
  89.9 21.2 %collective-permute-done.4.refs_3_.refs_1_ = bf16[256,1024]{1,0:T(8,128)(2,1)S(1)} collective-permute-done((bf16[256,1024]{1,0:T(8,128)(2,1)S(1)}, bf16[256,1024]{1,0:T(8,128)(2,1)S(1)}, u32[]{:S(2)}, u32[]{:S(2)}) %collective-permute-start.4) | collective-permute-done | bytes 524320 | tf_op jit(solution)/shard_map/ppermute | solution.py:326
  111.1 1.9 %collective-permute-start.20 = (bf16[256,1024]{1,0:T(8,128)(2,1)S(1)}, bf16[256,1024]{1,0:T(8,128)(2,1)S(1)}, u32[]{:S(2)}, u32[]{:S(2)}) collective-permute-start(bf16[256,1024]{1,0:T(8,128)(2,1)S(1)} %collective-permute-done.19.refs_1_), channel_id=1, source_target_pairs={{1,2},{2,3},{5,6},{6,7},{9,10},{10,11},{13,14},{14,15},{17,18},{18... | collective-permute-start | bytes 1572872 | tf_op jit(solution)/shard_map/ppermute | solution.py:326
  113.0 8.8 %collective-permute-done.16.refs_0_ = bf16[256,1024]{1,0:T(8,128)(2,1)S(1)} collective-permute-done((bf16[256,1024]{1,0:T(8,128)(2,1)S(1)}, bf16[256,1024]{1,0:T(8,128)(2,1)S(1)}, u32[]{:S(2)}, u32[]{:S(2)}) %collective-permute-start.16) | collective-permute-done | bytes 524320 | tf_op jit(solution)/shard_map/ppermute | solution.py:480
  121.9 1.3 collective-permute-start.23
  123.2 1.9 %collective-permute-start.21 = (bf16[256,1024]{1,0:T(8,128)(2,1)S(1)}, bf16[256,1024]{1,0:T(8,128)(2,1)S(1)}, u32[]{:S(2)}, u32[]{:S(2)}) collective-permute-start(bf16[256,1024]{1,0:T(8,128)(2,1)S(1)} %get-tuple-element.53), channel_id=1, source_target_pairs={{1,2},{2,3},{5,6},{6,7},{9,10},{10,11},{13,14},{14,15},{17,18},{18... | collective-permute-start | bytes 1572872 | tf_op jit(solution)/shard_map/ppermute | solution.py:326
  125.2 4.0 %collective-permute-start.9 = (bf16[256,512]{1,0:T(8,128)(2,1)S(1)}, bf16[256,512]{1,0:T(8,128)(2,1)S(1)}, u32[]{:S(2)}, u32[]{:S(2)}) collective-permute-start(bf16[256,512]{1,0:T(8,128)(2,1)S(1)} %get-tuple-element.57), channel_id=1, source_target_pairs={{2,1},{6,5},{10,9},{14,13},{18,17},{22,21},{26,25},{30,29}} | collective-permute-start | bytes 786440 | tf_op jit(solution)/shard_map/ppermute | solution.py:326
  129.1 0.1 fusion
  129.2 0.0 copy-start.1
  129.2 10.8 %collective-permute-done.9.refs_3_ = bf16[256,512]{1,0:T(8,128)(2,1)S(1)} collective-permute-done((bf16[256,512]{1,0:T(8,128)(2,1)S(1)}, bf16[256,512]{1,0:T(8,128)(2,1)S(1)}, u32[]{:S(2)}, u32[]{:S(2)}) %collective-permute-start.9) | collective-permute-done | bytes 262176 | tf_op jit(solution)/shard_map/ppermute | solution.py:326
  140.0 4.4 %collective-permute-start.24 = (bf16[256,1024]{1,0:T(8,128)(2,1)S(1)}, bf16[256,1024]{1,0:T(8,128)(2,1)S(1)}, u32[]{:S(2)}, u32[]{:S(2)}) collective-permute-start(bf16[256,1024]{1,0:T(8,128)(2,1)S(1)} %get-tuple-element.51), channel_id=1, source_target_pairs={{1,0},{2,1},{5,4},{6,5},{9,8},{10,9},{13,12},{14,13},{17,16},{18,1... | collective-permute-start | bytes 1572872 | tf_op jit(solution)/shard_map/ppermute | solution.py:326
  144.4 1.7 shard_map.229
  146.2 1.3 collective-permute-start.18
  147.5 1.3 collective-permute-start.17
  148.8 0.1 collective-permute-done.18.refs_10_
  148.9 1.3 collective-permute-start.3
  150.2 10.1 %collective-permute-start.7 = (bf16[256,1024]{1,0:T(8,128)(2,1)S(1)}, bf16[256,1024]{1,0:T(8,128)(2,1)S(1)}, u32[]{:S(2)}, u32[]{:S(2)}) collective-permute-start(bf16[256,1024]{1,0:T(8,128)(2,1)S(1)} %get-tuple-element.52), channel_id=1, source_target_pairs={{2,1},{6,5},{10,9},{14,13},{18,17},{22,21},{26,25},{30,29}} | collective-permute-start | bytes 1572872 | tf_op jit(solution)/shard_map/ppermute | solution.py:326
  160.3 1.4 shard_map.230
  161.7 1.7 shard_map.226
  163.4 1.3 collective-permute-start.1
  164.8 4.6 %collective-permute-start.5 = (bf16[256,512]{1,0:T(8,128)(2,1)S(1)}, bf16[256,512]{1,0:T(8,128)(2,1)S(1)}, u32[]{:S(2)}, u32[]{:S(2)}) collective-permute-start(bf16[256,512]{1,0:T(8,128)(2,1)S(1)} %get-tuple-element.58), channel_id=1, source_target_pairs={{2,1},{6,5},{10,9},{14,13},{18,17},{22,21},{26,25},{30,29}} | collective-permute-start | bytes 786440 | tf_op jit(solution)/shard_map/ppermute | solution.py:326
  169.3 3.2 %shard_map.231 = (f32[8,128,256]{2,1,0:T(8,128)S(1)}, f32[8,2,256]{2,1,0:T(2,128)S(1)}) custom-call(bf16[256,2048]{1,0:T(8,128)(2,1)S(1)} %get-tuple-element.28.refs_0_, bf16[256,1024]{1,0:T(8,128)(2,1)S(1)} %collective-permute-done.19.refs_1_, ...), custom_call_target="tpu_custom_call", output_to_operand_aliasing={{0}: (7, {}), {1}: (8, {})} | custom-call | flops 536870912 | bytes 4194304 | tf_op jit(solution)/shard_map/pallas_call | solution.py:298
  172.6 3.6 %shard_map.227 = (f32[8,128,256]{2,1,0:T(8,128)S(1)}, f32[8,2,256]{2,1,0:T(2,128)S(1)}) custom-call(bf16[256,2048]{1,0:T(8,128)(2,1)S(1)} %get-tuple-element.28.refs_0_, bf16[256,1024]{1,0:T(8,128)(2,1)S(1)} %collective-permute-done.refs_1_.refs_3_, ...), custom_call_target="tpu_custom_call", output_to_operand_aliasing={{0}: (7, {}), {1}: (8, {})} | custom-call | flops 536870912 | bytes 4194304 | tf_op jit(solution)/shard_map/pallas_call | solution.py:298
  176.2 2.1 %shard_map.232 = (f32[8,128,256]{2,1,0:T(8,128)S(1)}, f32[8,2,256]{2,1,0:T(2,128)S(1)}) custom-call(bf16[256,2048]{1,0:T(8,128)(2,1)S(1)} %get-tuple-element.28.refs_0_, bf16[2,256,2048]{2,1,0:T(8,128)(2,1)S(1)} %pad_maximum_fusion.refs_1_, bf16[2,256,2048]{2,1,0:T(8,128)(2,1)S(1)} %collective-permute-done.15.refs_2_, ...), custom_call_target="tpu_custom_call", output_to_operand_aliasing={{0}: (3, {}), {1}: (4, {})} | custom-call | flops 536870912 | bytes 4194304 | tf_op jit(solution)/shard_map/pallas_call | solution.py:298
  178.3 2.5 %shard_map.228 = (f32[8,128,256]{2,1,0:T(8,128)S(1)}, f32[8,2,256]{2,1,0:T(2,128)S(1)}) custom-call(bf16[256,2048]{1,0:T(8,128)(2,1)S(1)} %get-tuple-element.28.refs_0_, bf16[2,256,2048]{2,1,0:T(8,128)(2,1)S(1)} %pad_maximum_fusion.refs_1_, bf16[2,256,2048]{2,1,0:T(8,128)(2,1)S(1)} %collective-permute-done.15.refs_2_, ...), custom_call_target="tpu_custom_call", output_to_operand_aliasing={{0}: (3, {}), {1}: (4, {})} | custom-call | flops 536870912 | bytes 4194304 | tf_op jit(solution)/shard_map/pallas_call | solution.py:298
  180.7 2.4 %shard_map.233 = (bf16[256,2048]{1,0:T(8,128)(2,1)}, f32[8,128,256]{2,1,0:T(8,128)S(1)}, f32[8,2,256]{2,1,0:T(2,128)S(1)}) custom-call(bf16[256,2048]{1,0:T(8,128)(2,1)S(1)} %get-tuple-element.28.refs_0_, bf16[256,1024]{1,0:T(8,128)(2,1)S(1)} %collective-permute-done.20.refs_1_, ...), custom_call_target="tpu_custom_call", output_to_operand_aliasing={{1}: (7, {}), {2}: (8, {})} | custom-call | flops 536870912 | bytes 4194304 | tf_op jit(solution)/shard_map/pallas_call | solution.py:298
  183.2 1.6 shard_map.234
  184.8 1.6 shard_map.235
  (40 shorter events, 0.2 us)
Async XLA Ops:
  0.0 38.2 %copy-start.14 = (f32[2,64,128]{2,1,0:T(8,128)S(1)}, f32[2,64,128]{2,1,0:T(8,128)}, u32[]{:S(2)}) copy-start(f32[2,64,128]{2,1,0:T(8,128)} %constant.44.clone) | copy-start | bytes 196612
  0.0 5.7 %collective-permute-start.10 = (bf16[16,2048]{1,0:T(8,128)(2,1)}, bf16[16,2048]{1,0:T(8,128)(2,1)S(1)}, u32[]{:S(2)}, u32[]{:S(2)}) collective-permute-start(bf16[16,2048]{1,0:T(8,128)(2,1)} %refs_0_.1), channel_id=1, source_target_pairs={{0,2},{1,3},{2,0},{3,1},{4,6},{5,7},{6,4},{7,5},{8,10},{9,11},{10,... | collective-permute-start | bytes 196616 | tf_op jit(solution)/shard_map/ppermute | solution.py:338
  0.3 6.2 %collective-permute-start.11 = (bf16[16,2048]{1,0:T(8,128)(2,1)}, bf16[16,2048]{1,0:T(8,128)(2,1)S(1)}, u32[]{:S(2)}, u32[]{:S(2)}) collective-permute-start(bf16[16,2048]{1,0:T(8,128)(2,1)} %refs_1_.1), channel_id=1, source_target_pairs={{0,2},{1,3},{2,0},{3,1},{4,6},{5,7},{6,4},{7,5},{8,10},{9,11},{10,... | collective-permute-start | bytes 196616 | tf_op jit(solution)/shard_map/ppermute | solution.py:338
  6.6 0.8 copy-start.6
  7.3 0.8 copy-start.8
  8.2 0.8 copy-start.9
  9.4 28.9 %copy-start.4 = (bf16[1,4,64,2048]{3,2,1,0:T(8,128)(2,1)S(1)}, bf16[1,4,64,2048]{3,2,1,0:T(8,128)(2,1)}, u32[]{:S(2)}) copy-start(bf16[1,4,64,2048]{3,2,1,0:T(8,128)(2,1)} %param.24) | copy-start | bytes 3145732
  9.4 28.9 %copy-start.5 = (bf16[1,4,64,2048]{3,2,1,0:T(8,128)(2,1)S(1)}, bf16[1,4,64,2048]{3,2,1,0:T(8,128)(2,1)}, u32[]{:S(2)}) copy-start(bf16[1,4,64,2048]{3,2,1,0:T(8,128)(2,1)} %param.25) | copy-start | bytes 3145732
  9.4 28.9 %copy-start.7 = (bf16[128,128]{1,0:T(8,128)(2,1)S(1)}, bf16[128,128]{1,0:T(8,128)(2,1)}, u32[]{:S(2)}) copy-start(bf16[128,128]{1,0:T(8,128)(2,1)} %constant.40.clone.partners_ref.refs_6_) | copy-start | bytes 98308
  9.4 10.6 %collective-permute-start.12 = (bf16[2,32,2048]{2,1,0:T(8,128)(2,1)S(1)}, bf16[2,32,2048]{2,1,0:T(8,128)(2,1)S(1)}, u32[]{:S(2)}, u32[]{:S(2)}) collective-permute-start(bf16[2,32,2048]{2,1,0:T(8,128)(2,1)S(1)} %join.1), channel_id=1, source_target_pairs={{0,1},{1,0},{2,3},{3,2},{4,5},{5,4},{6,7},{7,6},{8,9},{9,8},{10,11... | collective-permute-start | bytes 786440 | tf_op jit(solution)/shard_map/ppermute | solution.py:338
  20.0 13.4 %copy-start.10 = (bf16[2,32,2048]{2,1,0:T(8,128)(2,1)}, bf16[2,32,2048]{2,1,0:T(8,128)(2,1)S(1)}, u32[]{:S(2)}) copy-start(bf16[2,32,2048]{2,1,0:T(8,128)(2,1)S(1)} %collective-permute-done.12) | copy-start | bytes 786436
  20.1 13.3 %collective-permute-start.13 = (bf16[2,64,2048]{2,1,0:T(8,128)(2,1)S(1)}, bf16[2,64,2048]{2,1,0:T(8,128)(2,1)S(1)}, u32[]{:S(2)}, u32[]{:S(2)}) collective-permute-start(bf16[2,64,2048]{2,1,0:T(8,128)(2,1)S(1)} %pad_maximum_fusion.2), channel_id=1, source_target_pairs={{0,16},{4,20},{8,24},{12,28},{16,0},{20,4},{24,8},{28,12},{1,17},{... | collective-permute-start | bytes 1572872 | tf_op jit(solution)/shard_map/ppermute | solution.py:338
  33.4 0.8 copy-start.12
  35.2 7.5 %copy-start = (bf16[1,4,64,2048]{3,2,1,0:T(8,128)(2,1)S(1)}, bf16[1,4,64,2048]{3,2,1,0:T(8,128)(2,1)}, u32[]{:S(2)}) copy-start(bf16[1,4,64,2048]{3,2,1,0:T(8,128)(2,1)} %param.26) | copy-start | bytes 3145732
  35.2 24.0 %collective-permute-start.14 = (bf16[2,128,2048]{2,1,0:T(8,128)(2,1)}, bf16[2,128,2048]{2,1,0:T(8,128)(2,1)}, u32[]{:S(2)}, u32[]{:S(2)}) collective-permute-start(bf16[2,128,2048]{2,1,0:T(8,128)(2,1)} %pad_maximum_fusion.1), channel_id=1, source_target_pairs={{0,8},{4,12},{8,0},{12,4},{16,24},{20,28},{24,16},{28,20},{1,9},{5... | collective-permute-start | bytes 3145736 | tf_op jit(solution)/shard_map/ppermute | solution.py:338
  36.7 22.5 %copy-start.11 = (bf16[2,32,2048]{2,1,0:T(8,128)(2,1)S(1)}, bf16[2,32,2048]{2,1,0:T(8,128)(2,1)}, u32[]{:S(2)}) copy-start(bf16[2,32,2048]{2,1,0:T(8,128)(2,1)} %copy-done.10) | copy-start | bytes 786436
  36.7 22.5 %copy-start.13 = (bf16[2,64,2048]{2,1,0:T(8,128)(2,1)S(1)}, bf16[2,64,2048]{2,1,0:T(8,128)(2,1)}, u32[]{:S(2)}) copy-start(bf16[2,64,2048]{2,1,0:T(8,128)(2,1)} %copy-done.12) | copy-start | bytes 1572868
  39.4 27.2 %collective-permute-start.19 = (bf16[256,1024]{1,0:T(8,128)(2,1)S(1)}, bf16[256,1024]{1,0:T(8,128)(2,1)S(1)}, u32[]{:S(2)}, u32[]{:S(2)}) collective-permute-start(bf16[256,1024]{1,0:T(8,128)(2,1)S(1)} %get-tuple-element.39.refs_1_), channel_id=1, source_target_pairs={{0,1},{1,2},{2,3},{4,5},{5,6},{6,7},{8,9},{9,10},{10,11},{12,13},{... | collective-permute-start | bytes 1572872 | tf_op jit(solution)/shard_map/ppermute | solution.py:326
  42.8 45.7 %collective-permute-start.2 = (bf16[256,2048]{1,0:T(8,128)(2,1)S(1)}, bf16[256,2048]{1,0:T(8,128)(2,1)S(1)}, u32[]{:S(2)}, u32[]{:S(2)}) collective-permute-start(bf16[256,2048]{1,0:T(8,128)(2,1)S(1)} %bitcast.8), channel_id=1, source_target_pairs={{0,1},{1,2},{2,3},{4,5},{5,6},{6,7},{8,9},{9,10},{10,11},{12,13},{... | collective-permute-start | bytes 3145736 | tf_op jit(solution)/shard_map/ppermute | solution.py:326
  60.6 104.1 %collective-permute-start.15 = (bf16[2,256,2048]{2,1,0:T(8,128)(2,1)S(1)}, bf16[2,256,2048]{2,1,0:T(8,128)(2,1)S(1)}, u32[]{:S(2)}, u32[]{:S(2)}) collective-permute-start(bf16[2,256,2048]{2,1,0:T(8,128)(2,1)S(1)} %pad_maximum_fusion.refs_1_), channel_id=1, source_target_pairs={{0,4},{4,0},{8,12},{12,8},{16,20},{20,16},{24,28},{28,24},{1,5},{5... | collective-permute-start | bytes 6291464 | tf_op jit(solution)/shard_map/ppermute | solution.py:338
  60.7 16.7 %collective-permute-start.22 = (bf16[256,1024]{1,0:T(8,128)(2,1)S(1)}, bf16[256,1024]{1,0:T(8,128)(2,1)S(1)}, u32[]{:S(2)}, u32[]{:S(2)}) collective-permute-start(bf16[256,1024]{1,0:T(8,128)(2,1)S(1)} %get-tuple-element.39.refs_1_), channel_id=1, source_target_pairs={{1,0},{2,1},{3,2},{5,4},{6,5},{7,6},{9,8},{10,9},{11,10},{13,12},{... | collective-permute-start | bytes 1572872 | tf_op jit(solution)/shard_map/ppermute | solution.py:326
  62.6 24.5 %collective-permute-start = (bf16[256,1024]{1,0:T(8,128)(2,1)S(1)}, bf16[256,1024]{1,0:T(8,128)(2,1)S(1)}, u32[]{:S(2)}, u32[]{:S(2)}) collective-permute-start(bf16[256,1024]{1,0:T(8,128)(2,1)S(1)} %get-tuple-element.29.refs_1_), channel_id=1, source_target_pairs={{0,1},{1,2},{2,3},{4,5},{5,6},{6,7},{8,9},{9,10},{10,11},{12,13},{... | collective-permute-start | bytes 1572872 | tf_op jit(solution)/shard_map/ppermute | solution.py:326
  66.6 58.6 %collective-permute-start.6 = (bf16[256,2048]{1,0:T(8,128)(2,1)S(1)}, bf16[256,2048]{1,0:T(8,128)(2,1)S(1)}, u32[]{:S(2)}, u32[]{:S(2)}) collective-permute-start(bf16[256,2048]{1,0:T(8,128)(2,1)S(1)} %bitcast.9), channel_id=1, source_target_pairs={{1,0},{2,1},{3,2},{5,4},{6,5},{7,6},{9,8},{10,9},{11,10},{13,12},{... | collective-permute-start | bytes 3145736 | tf_op jit(solution)/shard_map/ppermute | solution.py:326
  77.4 33.7 %collective-permute-start.4 = (bf16[256,1024]{1,0:T(8,128)(2,1)S(1)}, bf16[256,1024]{1,0:T(8,128)(2,1)S(1)}, u32[]{:S(2)}, u32[]{:S(2)}) collective-permute-start(bf16[256,1024]{1,0:T(8,128)(2,1)S(1)} %get-tuple-element.29.refs_1_), channel_id=1, source_target_pairs={{1,0},{2,1},{3,2},{5,4},{6,5},{7,6},{9,8},{10,9},{11,10},{13,12},{... | collective-permute-start | bytes 1572872 | tf_op jit(solution)/shard_map/ppermute | solution.py:326
  87.1 34.7 %collective-permute-start.16 = (bf16[256,1024]{1,0:T(8,128)(2,1)S(1)}, bf16[256,1024]{1,0:T(8,128)(2,1)S(1)}, u32[]{:S(2)}, u32[]{:S(2)}) collective-permute-start(bf16[256,1024]{1,0:T(8,128)(2,1)S(1)} %get-tuple-element.36), channel_id=1, source_target_pairs={{0,1},{3,2},{4,5},{7,6},{8,9},{11,10},{12,13},{15,14},{16,17},{19,... | collective-permute-start | bytes 1572872 | tf_op jit(solution)/shard_map/ppermute | solution.py:480
  88.5 34.7 %collective-permute-start.8 = (bf16[256,512]{1,0:T(8,128)(2,1)S(1)}, bf16[256,512]{1,0:T(8,128)(2,1)S(1)}, u32[]{:S(2)}, u32[]{:S(2)}) collective-permute-start(bf16[256,512]{1,0:T(8,128)(2,1)S(1)} %get-tuple-element.59), channel_id=1, source_target_pairs={{1,2},{5,6},{9,10},{13,14},{17,18},{21,22},{25,26},{29,30}} | collective-permute-start | bytes 786440 | tf_op jit(solution)/shard_map/ppermute | solution.py:326
  89.9 54.5 %copy-start.2 = (f32[2,64,128]{2,1,0:T(8,128)S(1)}, f32[2,64,128]{2,1,0:T(8,128)}, u32[]{:S(2)}) copy-start(f32[2,64,128]{2,1,0:T(8,128)} %constant.45.clone.refs_5_.refs_6_) | copy-start | bytes 196612
  89.9 54.5 %copy-start.3 = (f32[2,64,128]{2,1,0:T(8,128)S(1)}, f32[2,64,128]{2,1,0:T(8,128)}, u32[]{:S(2)}) copy-start(f32[2,64,128]{2,1,0:T(8,128)} %constant.46.clone.refs_6_.refs_5_) | copy-start | bytes 196612
  111.1 35.0 %collective-permute-start.20 = (bf16[256,1024]{1,0:T(8,128)(2,1)S(1)}, bf16[256,1024]{1,0:T(8,128)(2,1)S(1)}, u32[]{:S(2)}, u32[]{:S(2)}) collective-permute-start(bf16[256,1024]{1,0:T(8,128)(2,1)S(1)} %collective-permute-done.19.refs_1_), channel_id=1, source_target_pairs={{1,2},{2,3},{5,6},{6,7},{9,10},{10,11},{13,14},{14,15},{17,18},{18... | collective-permute-start | bytes 1572872 | tf_op jit(solution)/shard_map/ppermute | solution.py:326
  121.9 25.6 %collective-permute-start.23 = (bf16[256,1024]{1,0:T(8,128)(2,1)S(1)}, bf16[256,1024]{1,0:T(8,128)(2,1)S(1)}, u32[]{:S(2)}, u32[]{:S(2)}) collective-permute-start(bf16[256,1024]{1,0:T(8,128)(2,1)S(1)} %collective-permute-done.22.refs_3_), channel_id=1, source_target_pairs={{1,0},{2,1},{5,4},{6,5},{9,8},{10,9},{13,12},{14,13},{17,16},{18,1... | collective-permute-start | bytes 1572872 | tf_op jit(solution)/shard_map/ppermute | solution.py:326
  123.2 27.0 %collective-permute-start.21 = (bf16[256,1024]{1,0:T(8,128)(2,1)S(1)}, bf16[256,1024]{1,0:T(8,128)(2,1)S(1)}, u32[]{:S(2)}, u32[]{:S(2)}) collective-permute-start(bf16[256,1024]{1,0:T(8,128)(2,1)S(1)} %get-tuple-element.53), channel_id=1, source_target_pairs={{1,2},{2,3},{5,6},{6,7},{9,10},{10,11},{13,14},{14,15},{17,18},{18... | collective-permute-start | bytes 1572872 | tf_op jit(solution)/shard_map/ppermute | solution.py:326
  125.2 14.8 %collective-permute-start.9 = (bf16[256,512]{1,0:T(8,128)(2,1)S(1)}, bf16[256,512]{1,0:T(8,128)(2,1)S(1)}, u32[]{:S(2)}, u32[]{:S(2)}) collective-permute-start(bf16[256,512]{1,0:T(8,128)(2,1)S(1)} %get-tuple-element.57), channel_id=1, source_target_pairs={{2,1},{6,5},{10,9},{14,13},{18,17},{22,21},{26,25},{30,29}} | collective-permute-start | bytes 786440 | tf_op jit(solution)/shard_map/ppermute | solution.py:326
  129.2 31.1 %copy-start.1 = (f32[1,64,128]{2,1,0:T(8,128)S(1)}, f32[1,64,128]{2,1,0:T(8,128)}, u32[]{:S(2)}) copy-start(f32[1,64,128]{2,1,0:T(8,128)} %constant.47.clone.refs_3_.refs_5_.refs_6_) | copy-start | bytes 98308
  140.0 23.4 %collective-permute-start.24 = (bf16[256,1024]{1,0:T(8,128)(2,1)S(1)}, bf16[256,1024]{1,0:T(8,128)(2,1)S(1)}, u32[]{:S(2)}, u32[]{:S(2)}) collective-permute-start(bf16[256,1024]{1,0:T(8,128)(2,1)S(1)} %get-tuple-element.51), channel_id=1, source_target_pairs={{1,0},{2,1},{5,4},{6,5},{9,8},{10,9},{13,12},{14,13},{17,16},{18,1... | collective-permute-start | bytes 1572872 | tf_op jit(solution)/shard_map/ppermute | solution.py:326
  146.2 2.7 %collective-permute-start.18 = (f32[8,2,256]{2,1,0:T(2,128)S(1)}, f32[8,2,256]{2,1,0:T(2,128)S(1)}, u32[]{:S(2)}, u32[]{:S(2)}) collective-permute-start(f32[8,2,256]{2,1,0:T(2,128)S(1)} %get-tuple-element.38), channel_id=1, source_target_pairs={{1,0},{2,3},{5,4},{6,7},{9,8},{10,11},{13,12},{14,15},{17,16},{18,... | collective-permute-start | bytes 49160 | tf_op jit(solution)/shard_map/ppermute | solution.py:490
  147.5 35.7 %collective-permute-start.17 = (bf16[8,128,256]{2,1,0:T(8,128)(2,1)S(1)}, bf16[8,128,256]{2,1,0:T(8,128)(2,1)S(1)}, u32[]{:S(2)}, u32[]{:S(2)}) collective-permute-start(bf16[8,128,256]{2,1,0:T(8,128)(2,1)S(1)} %get-tuple-element.37), channel_id=1, source_target_pairs={{1,0},{2,3},{5,4},{6,7},{9,8},{10,11},{13,12},{14,15},{17,16},{18,... | collective-permute-start | bytes 1572872 | tf_op jit(solution)/shard_map/ppermute | solution.py:489
  148.9 34.3 %collective-permute-start.3 = (bf16[256,1024]{1,0:T(8,128)(2,1)S(1)}, bf16[256,1024]{1,0:T(8,128)(2,1)S(1)}, u32[]{:S(2)}, u32[]{:S(2)}) collective-permute-start(bf16[256,1024]{1,0:T(8,128)(2,1)S(1)} %get-tuple-element.54), channel_id=1, source_target_pairs={{1,2},{5,6},{9,10},{13,14},{17,18},{21,22},{25,26},{29,30}} | collective-permute-start | bytes 1572872 | tf_op jit(solution)/shard_map/ppermute | solution.py:326
  150.2 33.0 %collective-permute-start.7 = (bf16[256,1024]{1,0:T(8,128)(2,1)S(1)}, bf16[256,1024]{1,0:T(8,128)(2,1)S(1)}, u32[]{:S(2)}, u32[]{:S(2)}) collective-permute-start(bf16[256,1024]{1,0:T(8,128)(2,1)S(1)} %get-tuple-element.52), channel_id=1, source_target_pairs={{2,1},{6,5},{10,9},{14,13},{18,17},{22,21},{26,25},{30,29}} | collective-permute-start | bytes 1572872 | tf_op jit(solution)/shard_map/ppermute | solution.py:326
  163.4 21.4 %collective-permute-start.1 = (bf16[256,512]{1,0:T(8,128)(2,1)S(1)}, bf16[256,512]{1,0:T(8,128)(2,1)S(1)}, u32[]{:S(2)}, u32[]{:S(2)}) collective-permute-start(bf16[256,512]{1,0:T(8,128)(2,1)S(1)} %get-tuple-element.60), channel_id=1, source_target_pairs={{1,2},{5,6},{9,10},{13,14},{17,18},{21,22},{25,26},{29,30}} | collective-permute-start | bytes 786440 | tf_op jit(solution)/shard_map/ppermute | solution.py:326
  164.8 20.1 %collective-permute-start.5 = (bf16[256,512]{1,0:T(8,128)(2,1)S(1)}, bf16[256,512]{1,0:T(8,128)(2,1)S(1)}, u32[]{:S(2)}, u32[]{:S(2)}) collective-permute-start(bf16[256,512]{1,0:T(8,128)(2,1)S(1)} %get-tuple-element.58), channel_id=1, source_target_pairs={{2,1},{6,5},{10,9},{14,13},{18,17},{22,21},{26,25},{30,29}} | collective-permute-start | bytes 786440 | tf_op jit(solution)/shard_map/ppermute | solution.py:326
